TPU v7x, 32 devices: a whole 2x2x4 slice. The times are simulated.
32 devices in a mesh: fsdp: 2 (over y), ctx: 8 (over z, x), tp: 2 (over core).
Axes of the slice: x: 2, y: 2, z: 4, core: 2. Of those that a mesh axis runs over, the one named last changes fastest.
Arguments:
- hidden_in: bfloat16 [4096, 2048], P(('fsdp', 'ctx'), 'tp'), may hold values from -6 to 6
- cotangent: bfloat16 [4096, 2048], P(('fsdp', 'ctx'), 'tp'), may hold values from -6 to 6
- positions: int32 [2, 2048], P('fsdp'), may hold values from 0 to 2047, each once within a row
- seq_lengths: int32 [2, 3], P('fsdp'), may hold values from 1 to 1024, 2048 in all within a row
- expert_ids: int32 [4096, 8], P(('fsdp', 'ctx')), may hold values from 0 to 15, all different within a row; in each aligned block of 256 rows (0 to 255, 256 to 511, ...) at most 160 rows name the same one
- attn_norm: bfloat16 [2048], P('tp'), may hold values from 0.099609375 to 1.8984375
- ffn_norm: bfloat16 [2048], P('tp'), may hold values from 0.099609375 to 1.8984375
- query_norm: bfloat16 [128], replicated, may hold values from 0.099609375 to 1.8984375
- key_norm: bfloat16 [128], replicated, may hold values from 0.099609375 to 1.8984375
- w_query: bfloat16 [2048, 2048], P('fsdp', 'tp'), may hold values from -0.125 to 0.125
- w_key: bfloat16 [2048, 2048], P('fsdp', 'tp'), may hold values from -0.125 to 0.125
- w_value: bfloat16 [2048, 2048], P('fsdp', 'tp'), may hold values from -0.125 to 0.125
- w_out: bfloat16 [2048, 2048], P('tp', 'fsdp'), may hold values from -2 to 2
- w_router: bfloat16 [16, 2048], P(None, 'fsdp'), may hold values from -0.0625 to 0.0625
- w_gate: bfloat16 [16, 2048, 1024], P(None, 'fsdp', 'tp'), may hold values from -0.125 to 0.125
- w_up: bfloat16 [16, 2048, 1024], P(None, 'fsdp', 'tp'), may hold values from -0.125 to 0.125
- w_down: bfloat16 [16, 2048, 1024], P(None, 'fsdp', 'tp'), may hold values from -2 to 2
Outputs:
- hidden_out: bfloat16 [4096, 2048], P(('fsdp', 'ctx'), 'tp')
- grad_hidden: float32 [4096, 2048], P(('fsdp', 'ctx'), 'tp')
- grad_attn_norm: float32 [2048], replicated
- grad_ffn_norm: float32 [2048], replicated
- grad_query_norm: float32 [128], replicated
- grad_key_norm: float32 [128], replicated
- grad_query: float32 [2048, 2048], P(('fsdp', 'ctx'), 'tp')
- grad_key: float32 [2048, 2048], P(('fsdp', 'ctx'), 'tp')
- grad_value: float32 [2048, 2048], P(('fsdp', 'ctx'), 'tp')
- grad_out: float32 [2048, 2048], P('tp', ('fsdp', 'ctx'))
- grad_router: float32 [16, 2048], P(None, ('fsdp', 'ctx'))
- grad_gate: float32 [16, 2048, 1024], P(None, ('fsdp', 'ctx'), 'tp')
- grad_up: float32 [16, 2048, 1024], P(None, ('fsdp', 'ctx'), 'tp')
- grad_down: float32 [16, 2048, 1024], P(None, ('fsdp', 'ctx'), 'tp')
- stream_rms: float32 [3], replicated
Inputs may be any that keep to these rules, and one draw needn't show every extreme that they name: Each row of positions names every position of its pack once. `seq_lengths`: each row sums to 2048; the longest sequence of every pack has 1024 tokens. `expert_ids`: a token's 8 experts are different, and every expert is chosen by some token; within the rows of one device (aligned blocks of 256 rows) no expert is chosen more than 160 times, and some expert is chosen exactly 160 times in some block.
All inputs are finite; a program needn't handle non-finite values.
Results may differ from a plain program's by a relative error of at most 0.029.
Values may be sent and summed in bfloat16 or wider, within the bound.
A program may use at most 448 MiB of HBM per device.

v0:
```python
import jax
import jax.numpy as jnp
from jax import lax
from jax.sharding import PartitionSpec as P

CAP = 160


norm_eps = 1e-06
rope_base = 10000.0


def locate(pack_spots, lengths_row):
    seq_ends = jnp.cumsum(lengths_row)
    starts = seq_ends - lengths_row
    segment = jnp.sum((pack_spots[:, None] >= seq_ends[None, :]).astype(jnp.int32), axis=1)
    slot_ids = jnp.arange(lengths_row.shape[0], dtype=jnp.int32)
    seq_begin = jnp.sum(
        jnp.where(segment[:, None] == slot_ids[None, :], starts[None, :], 0), axis=1
    )
    return (segment, pack_spots - seq_begin)


def rope_tables(pack_spots, head_dim):
    half_dim = head_dim // 2
    inv_freq = rope_base ** (-(jnp.arange(half_dim, dtype=jnp.float32) * 2.0 / head_dim))
    angle_grid = pack_spots.astype(jnp.float32)[:, None] * inv_freq[None, :]
    cosine = jnp.concatenate([jnp.cos(angle_grid), jnp.cos(angle_grid)], axis=1)
    sine_table = jnp.concatenate([jnp.sin(angle_grid), jnp.sin(angle_grid)], axis=1)
    return (cosine[:, None, :], sine_table[:, None, :])


def rotate(tensor, cosine, sine_table):
    half_dim = tensor.shape[-1] // 2
    turned = jnp.concatenate([-tensor[..., half_dim:], tensor[..., :half_dim]], axis=-1)
    return tensor * cosine + turned * sine_table


def unrotate(grad_rot, cosine, sine_table):
    half_dim = grad_rot.shape[-1] // 2
    shifted = grad_rot * sine_table
    turned = jnp.concatenate([shifted[..., half_dim:], -shifted[..., :half_dim]], axis=-1)
    return grad_rot * cosine + turned


def on_device(
    hidden_in,
    cotangent,
    positions,
    seq_lengths,
    expert_ids,
    attn_norm,
    ffn_norm,
    query_norm,
    key_norm,
    w_query,
    w_key,
    w_value,
    w_out,
    w_router,
    w_gate,
    w_up,
    w_down,
):
    tok_rows = hidden_in.shape[0]
    col_count = hidden_in.shape[1]
    width_all = col_count * lax.axis_size("tp")
    head_dim = query_norm.shape[0]
    local_heads = w_query.shape[1] // head_dim
    expert_count = w_gate.shape[0]
    top_count = expert_ids.shape[1]
    capacity = CAP
    tp_place = lax.axis_index("tp")
    score_scale = head_dim ** (-0.5)

    def row_total(tensor):
        return lax.psum(tensor, "tp")

    def tp_rows(tensor):
        return lax.all_gather(tensor, "tp", axis=1, tiled=True)

    def tp_share(tensor):
        return lax.psum_scatter(
            tensor.astype(jnp.bfloat16), "tp", scatter_dimension=1, tiled=True
        ).astype(jnp.float32)

    def heads_of(tensor):
        return tensor.reshape(tok_rows, local_heads, head_dim)

    order_row = positions[0]
    pack_size = order_row.shape[0]
    my_spots = lax.dynamic_slice_in_dim(order_row, lax.axis_index("ctx") * tok_rows, tok_rows)
    my_segment, my_place = locate(my_spots, seq_lengths[0])
    pack_segment = locate(order_row, seq_lengths[0])[0]
    cosine, sine_table = rope_tables(my_place, head_dim)
    same_seq = (my_segment[:, None] == pack_segment[None, :])[None]
    expert_range = jnp.arange(expert_count, dtype=jnp.int32)
    pair_expert = expert_ids.reshape(-1)
    pair_token = jnp.arange(tok_rows * top_count, dtype=jnp.int32) // top_count
    sort_order = jnp.argsort(pair_expert, stable=True)
    sorted_expert = pair_expert[sort_order]
    sorted_token = pair_token[sort_order]
    expert_load = jnp.sum((pair_expert[:, None] == expert_range[None, :]).astype(jnp.int32), axis=0)
    load_start = jnp.cumsum(expert_load) - expert_load
    start_of_pair = jnp.sum(
        jnp.where(sorted_expert[:, None] == expert_range[None, :], load_start[None, :], 0), axis=1
    )
    pair_rank = jnp.arange(tok_rows * top_count, dtype=jnp.int32) - start_of_pair
    slot_index = sorted_expert * capacity + pair_rank
    slot_token_flat = (
        jnp.zeros((expert_count * capacity,), jnp.int32).at[slot_index].set(sorted_token)
    )
    slot_valid = (
        jnp.zeros((expert_count * capacity,), jnp.float32)
        .at[slot_index]
        .set(1.0)
        .reshape(expert_count, capacity)
    )
    slot_token = slot_token_flat.reshape(expert_count, capacity)
    resid_in = hidden_in.astype(jnp.float32)
    gain_first = attn_norm.astype(jnp.float32)
    inv_first = lax.rsqrt(row_total(jnp.sum(resid_in * resid_in, axis=1)) / width_all + norm_eps)[
        :, None
    ]
    normed_first = tp_rows((resid_in * inv_first * gain_first).astype(jnp.bfloat16))
    query_full, key_full, value_full, out_full = (
        lax.all_gather(w_query, "fsdp", axis=0, tiled=True),
        lax.all_gather(w_key, "fsdp", axis=0, tiled=True),
        lax.all_gather(w_value, "fsdp", axis=0, tiled=True),
        lax.all_gather(w_out, "fsdp", axis=1, tiled=True),
    )
    query_raw = heads_of(jnp.dot(normed_first, query_full, preferred_element_type=jnp.float32))
    key_raw = heads_of(jnp.dot(normed_first, key_full, preferred_element_type=jnp.float32))
    value_low = jnp.dot(normed_first, value_full, preferred_element_type=jnp.float32).astype(
        jnp.bfloat16
    )
    gain_query = query_norm.astype(jnp.float32)
    gain_key = key_norm.astype(jnp.float32)

    def prepare(raw_proj, gain_vec):
        inverse = lax.rsqrt(jnp.mean(raw_proj * raw_proj, axis=2, keepdims=True) + norm_eps)
        return (
            rotate(raw_proj * inverse * gain_vec, cosine, sine_table).astype(jnp.bfloat16),
            inverse,
        )

    query_low, query_inv = prepare(query_raw, gain_query)
    key_low, key_inv = prepare(key_raw, gain_key)
    key_pack, value_pack = (
        lax.all_gather(key_low.reshape(tok_rows, -1), "ctx", axis=0, tiled=True),
        lax.all_gather(value_low, "ctx", axis=0, tiled=True),
    )

    def scores_of(key_all):
        raw_scores = (
            jnp.einsum(
                "qhd,khd->hqk",
                query_low,
                key_all.reshape(pack_size, local_heads, head_dim),
                preferred_element_type=jnp.float32,
            )
            * score_scale
        )
        return jnp.where(same_seq, raw_scores, -1e30)

    scores = scores_of(key_pack)
    row_peak = jnp.max(scores, axis=2, keepdims=True)
    row_exp = jnp.exp(scores - row_peak)
    row_sum = jnp.sum(row_exp, axis=2, keepdims=True)
    log_total = row_peak + jnp.log(row_sum)
    probs_low = (row_exp / row_sum).astype(jnp.bfloat16)
    attended = jnp.einsum(
        "hqk,khd->qhd",
        probs_low,
        value_pack.reshape(pack_size, local_heads, head_dim),
        preferred_element_type=jnp.float32,
    )
    attended_low = attended.reshape(tok_rows, -1).astype(jnp.bfloat16)
    attn_branch = tp_share(jnp.dot(attended_low, out_full, preferred_element_type=jnp.float32))
    middle = resid_in + attn_branch
    gain_second = ffn_norm.astype(jnp.float32)
    inv_second = lax.rsqrt(row_total(jnp.sum(middle * middle, axis=1)) / width_all + norm_eps)[
        :, None
    ]
    normed_second = tp_rows((middle * inv_second * gain_second).astype(jnp.bfloat16))
    router_full, gate_full, up_full, down_full = (
        lax.all_gather(w_router, "fsdp", axis=1, tiled=True),
        lax.all_gather(w_gate, "fsdp", axis=1, tiled=True),
        lax.all_gather(w_up, "fsdp", axis=1, tiled=True),
        lax.all_gather(w_down, "fsdp", axis=1, tiled=True),
    )
    logits = jnp.einsum("nd,ed->ne", normed_second, router_full, preferred_element_type=jnp.float32)
    logit_peak = jnp.max(logits, axis=1, keepdims=True)
    logit_exp = jnp.exp(logits - logit_peak)
    route_probs = logit_exp / jnp.sum(logit_exp, axis=1, keepdims=True)
    chosen = jnp.sum(
        (expert_ids[:, :, None] == expert_range[None, None, :]).astype(jnp.float32), axis=1
    )
    gate_weights = route_probs * chosen
    slot_gates = (jnp.take_along_axis(gate_weights.T, slot_token, axis=1) * slot_valid)[:, :, None]
    slot_input = normed_second[slot_token_flat].reshape(expert_count, capacity, -1)
    gate_proj = jnp.einsum(
        "ecd,edf->ecf", slot_input, gate_full, preferred_element_type=jnp.float32
    )
    up_proj = jnp.einsum("ecd,edf->ecf", slot_input, up_full, preferred_element_type=jnp.float32)
    gate_sigmoid = jax.nn.sigmoid(gate_proj)
    activity = gate_proj * gate_sigmoid * up_proj
    mixed_low = (slot_gates * activity).astype(jnp.bfloat16)
    slot_out = jnp.einsum("ecf,edf->ecd", mixed_low, down_full, preferred_element_type=jnp.float32)
    expert_part = (
        jnp.zeros((tok_rows, width_all), jnp.float32)
        .at[slot_token_flat]
        .add(slot_out.reshape(expert_count * capacity, -1))
    )
    expert_branch = tp_share(expert_part)
    hidden_out = (middle + expert_branch).astype(jnp.bfloat16)
    grad_in = cotangent.astype(jnp.float32)
    grad_wide = tp_rows(cotangent)
    slot_grad = grad_wide[slot_token_flat].reshape(expert_count, capacity, -1)
    grad_mixed = jnp.einsum(
        "ecd,edf->ecf", slot_grad, down_full, preferred_element_type=jnp.float32
    ).astype(jnp.bfloat16)
    grad_down_full = jnp.einsum(
        "ecf,ecd->edf", mixed_low, slot_grad, preferred_element_type=jnp.float32
    )
    grad_mixed_wide = grad_mixed.astype(jnp.float32)
    slot_gate_grads = jnp.sum(grad_mixed_wide * activity, axis=2) * slot_valid
    flat_pairs = (expert_range[:, None] * tok_rows + slot_token).reshape(-1)
    gates_part = (
        jnp.zeros((expert_count * tok_rows,), jnp.float32)
        .at[flat_pairs]
        .add(slot_gate_grads.reshape(-1))
        .reshape(expert_count, tok_rows)
        .T
    )
    grad_gates = row_total(gates_part)
    grad_activity = grad_mixed_wide * slot_gates
    grad_gate_low = (
        grad_activity * up_proj * gate_sigmoid * (1.0 + gate_proj * (1.0 - gate_sigmoid))
    ).astype(jnp.bfloat16)
    grad_up_low = (grad_activity * gate_proj * gate_sigmoid).astype(jnp.bfloat16)
    grad_probs = grad_gates * chosen
    grad_logits = (
        route_probs * (grad_probs - jnp.sum(route_probs * grad_probs, axis=1, keepdims=True))
    ).astype(jnp.bfloat16)
    grad_gate_full = jnp.einsum(
        "ecd,ecf->edf", slot_input, grad_gate_low, preferred_element_type=jnp.float32
    )
    grad_up_full = jnp.einsum(
        "ecd,ecf->edf", slot_input, grad_up_low, preferred_element_type=jnp.float32
    )
    grad_router_full = jnp.einsum(
        "ne,nd->ed", grad_logits, normed_second, preferred_element_type=jnp.float32
    )
    slot_back = jnp.einsum(
        "ecf,edf->ecd", grad_gate_low, gate_full, preferred_element_type=jnp.float32
    )
    slot_back = slot_back + jnp.einsum(
        "ecf,edf->ecd", grad_up_low, up_full, preferred_element_type=jnp.float32
    )
    back_part = (
        jnp.zeros((tok_rows, width_all), jnp.float32)
        .at[slot_token_flat]
        .add(slot_back.reshape(expert_count * capacity, -1))
    )
    router_mine = lax.dynamic_slice_in_dim(router_full, tp_place * col_count, col_count, 1)
    grad_second = tp_share(back_part) + jnp.einsum(
        "ne,ed->nd", grad_logits, router_mine, preferred_element_type=jnp.float32
    )
    grad_router, grad_gate, grad_up, grad_down = (
        lax.psum_scatter(
            grad_router_full.astype(jnp.bfloat16), ("fsdp", "ctx"), scatter_dimension=1, tiled=True
        ).astype(jnp.float32),
        lax.psum_scatter(
            grad_gate_full.astype(jnp.bfloat16), ("fsdp", "ctx"), scatter_dimension=1, tiled=True
        ).astype(jnp.float32),
        lax.psum_scatter(
            grad_up_full.astype(jnp.bfloat16), ("fsdp", "ctx"), scatter_dimension=1, tiled=True
        ).astype(jnp.float32),
        lax.psum_scatter(
            grad_down_full.astype(jnp.bfloat16), ("fsdp", "ctx"), scatter_dimension=1, tiled=True
        ).astype(jnp.float32),
    )
    gain_two_grad = jnp.sum(grad_second * middle * inv_second, axis=0)
    second_scaled = grad_second * gain_second
    second_inner = row_total(jnp.sum(second_scaled * middle, axis=1))[:, None]
    grad_middle = (
        grad_in + inv_second * second_scaled - middle * inv_second**3 * second_inner / width_all
    )
    grad_middle_wide = tp_rows(grad_middle.astype(jnp.bfloat16))
    grad_attended = jnp.einsum(
        "nd,hd->nh", grad_middle_wide, out_full, preferred_element_type=jnp.float32
    ).astype(jnp.bfloat16)
    grad_out_full = jnp.einsum(
        "nh,nd->hd", attended_low, grad_middle_wide, preferred_element_type=jnp.float32
    )
    probs_back = jnp.exp(scores_of(key_pack) - log_total)
    grad_att_heads = heads_of(grad_attended)
    key_heads = key_pack.reshape(pack_size, local_heads, head_dim)
    value_heads = value_pack.reshape(pack_size, local_heads, head_dim)
    grad_probs_att = jnp.einsum(
        "qhd,khd->hqk", grad_att_heads, value_heads, preferred_element_type=jnp.float32
    )
    grad_scores = (
        probs_back * (grad_probs_att - jnp.sum(probs_back * grad_probs_att, axis=2, keepdims=True))
    ).astype(jnp.bfloat16)
    grad_query_rot = (
        jnp.einsum("hqk,khd->qhd", grad_scores, key_heads, preferred_element_type=jnp.float32)
        * score_scale
    )
    grad_key_pack = (
        jnp.einsum("hqk,qhd->khd", grad_scores, query_low, preferred_element_type=jnp.float32)
        * score_scale
    )
    grad_value_pack = jnp.einsum(
        "hqk,qhd->khd",
        probs_back.astype(jnp.bfloat16),
        grad_att_heads,
        preferred_element_type=jnp.float32,
    )
    grad_key_rot, grad_value_sum = (
        lax.psum_scatter(
            grad_key_pack.reshape(pack_size, -1).astype(jnp.bfloat16),
            "ctx",
            scatter_dimension=0,
            tiled=True,
        ).astype(jnp.float32),
        lax.psum_scatter(
            grad_value_pack.reshape(pack_size, -1).astype(jnp.bfloat16),
            "ctx",
            scatter_dimension=0,
            tiled=True,
        ).astype(jnp.float32),
    )

    def prepare_back(grad_rot, raw_proj, inverse, gain_vec):
        grad_normed = unrotate(grad_rot, cosine, sine_table)
        weighted = grad_normed * gain_vec
        grad_raw = inverse * weighted - raw_proj * inverse**3 * jnp.mean(
            weighted * raw_proj, axis=2, keepdims=True
        )
        gain_grad = jnp.sum(grad_normed * raw_proj * inverse, axis=(0, 1))
        return (grad_raw.reshape(tok_rows, -1).astype(jnp.bfloat16), gain_grad)

    grad_query_low, query_gain_grad = prepare_back(grad_query_rot, query_raw, query_inv, gain_query)
    grad_key_low, key_gain_grad = prepare_back(heads_of(grad_key_rot), key_raw, key_inv, gain_key)
    grad_value_low = grad_value_sum.astype(jnp.bfloat16)
    grad_query_full = jnp.einsum(
        "nd,nh->dh", normed_first, grad_query_low, preferred_element_type=jnp.float32
    )
    grad_key_full = jnp.einsum(
        "nd,nh->dh", normed_first, grad_key_low, preferred_element_type=jnp.float32
    )
    grad_value_full = jnp.einsum(
        "nd,nh->dh", normed_first, grad_value_low, preferred_element_type=jnp.float32
    )
    first_part = jnp.einsum(
        "nh,dh->nd", grad_query_low, query_full, preferred_element_type=jnp.float32
    )
    first_part = first_part + jnp.einsum(
        "nh,dh->nd", grad_key_low, key_full, preferred_element_type=jnp.float32
    )
    first_part = first_part + jnp.einsum(
        "nh,dh->nd", grad_value_low, value_full, preferred_element_type=jnp.float32
    )
    grad_first = tp_share(first_part)
    grad_query, grad_key, grad_value, grad_out = (
        lax.psum_scatter(
            grad_query_full.astype(jnp.bfloat16), ("fsdp", "ctx"), scatter_dimension=0, tiled=True
        ).astype(jnp.float32),
        lax.psum_scatter(
            grad_key_full.astype(jnp.bfloat16), ("fsdp", "ctx"), scatter_dimension=0, tiled=True
        ).astype(jnp.float32),
        lax.psum_scatter(
            grad_value_full.astype(jnp.bfloat16), ("fsdp", "ctx"), scatter_dimension=0, tiled=True
        ).astype(jnp.float32),
        lax.psum_scatter(
            grad_out_full.astype(jnp.bfloat16), ("fsdp", "ctx"), scatter_dimension=1, tiled=True
        ).astype(jnp.float32),
    )
    gain_one_grad = jnp.sum(grad_first * resid_in * inv_first, axis=0)
    first_scaled = grad_first * gain_first
    first_inner = row_total(jnp.sum(first_scaled * resid_in, axis=1))[:, None]
    grad_hidden = (
        grad_middle + inv_first * first_scaled - resid_in * inv_first**3 * first_inner / width_all
    )
    gains_part = lax.dynamic_update_slice(
        jnp.zeros((2, width_all), jnp.float32),
        jnp.stack([gain_one_grad, gain_two_grad]),
        (0, tp_place * col_count),
    )
    stream_part = jnp.stack(
        [
            jnp.sum(middle * middle),
            jnp.sum(attn_branch * attn_branch),
            jnp.sum(expert_branch * expert_branch),
        ]
    )
    stream_sums, gains_sum, query_gain_sum, key_gain_sum = lax.psum(
        (stream_part, gains_part, query_gain_grad, key_gain_grad), ("fsdp", "ctx", "tp")
    )
    token_count = tok_rows * lax.axis_size("fsdp") * lax.axis_size("ctx")
    stream_rms = jnp.sqrt(stream_sums / (token_count * width_all))
    return (
        hidden_out,
        grad_hidden,
        gains_sum[0],
        gains_sum[1],
        query_gain_sum,
        key_gain_sum,
        grad_query,
        grad_key,
        grad_value,
        grad_out,
        grad_router,
        grad_gate,
        grad_up,
        grad_down,
        stream_rms,
    )


def solution(mesh):
    return jax.shard_map(
        on_device,
        mesh=mesh,
        in_specs=(
            P(("fsdp", "ctx"), "tp"),
            P(("fsdp", "ctx"), "tp"),
            P("fsdp", None),
            P("fsdp", None),
            P(("fsdp", "ctx"), None),
            P("tp"),
            P("tp"),
            P(),
            P(),
            P("fsdp", "tp"),
            P("fsdp", "tp"),
            P("fsdp", "tp"),
            P("tp", "fsdp"),
            P(None, "fsdp"),
            P(None, "fsdp", "tp"),
            P(None, "fsdp", "tp"),
            P(None, "fsdp", "tp"),
        ),
        out_specs=(
            P(("fsdp", "ctx"), "tp"),
            P(("fsdp", "ctx"), "tp"),
            P(),
            P(),
            P(),
            P(),
            P(("fsdp", "ctx"), "tp"),
            P(("fsdp", "ctx"), "tp"),
            P(("fsdp", "ctx"), "tp"),
            P("tp", ("fsdp", "ctx")),
            P(None, ("fsdp", "ctx")),
            P(None, ("fsdp", "ctx"), "tp"),
            P(None, ("fsdp", "ctx"), "tp"),
            P(None, ("fsdp", "ctx"), "tp"),
            P(),
        ),
        check_vma=False,
    )
```

profile of v0, /device:TPU:0, one launch (start us, length us, event | category | flops | bytes accessed | tf_op | source)
XLA Modules:
  0.0 4552.9 jit_solution(10297297219115266703)
XLA Ops:
  26.8 59.5 %all-gather.20.cloned.1.call-done = bf16[2048,1024]{1,0:T(8,128)(2,1)} async-done(((bf16[1024,1024]{1,0:T(8,128)(2,1)}), bf16[2048,1024]{1,0:T(8,128)(2,1)}) %all-gather.20.cloned.1.call-update) | async-done | bytes 4194320 | tf_op jit(solution)/shard_map/all_gather | solution.py:127
  91.0 53.5 %all-gather.22.cloned.1.call-done = bf16[2048,1024]{1,0:T(8,128)(2,1)} async-done(((bf16[1024,1024]{1,0:T(8,128)(2,1)}), bf16[2048,1024]{1,0:T(8,128)(2,1)}) %all-gather.22.cloned.1.call-update) | async-done | bytes 4194320 | tf_op jit(solution)/shard_map/all_gather | solution.py:128
  168.4 34.4 all-gather.16.cloned.1.call-done
  208.5 70.3 %all-gather.24.cloned.1.call-done = bf16[2048,1024]{1,0:T(8,128)(2,1)} async-done(((bf16[256,1024]{1,0:T(8,128)(2,1)}), bf16[2048,1024]{1,0:T(8,128)(2,1)}) %all-gather.24.cloned.1.call-update) | async-done | bytes 4194320 | tf_op jit(solution)/shard_map/all_gather | solution.py:150
  303.7 49.3 %all-gather.18.cloned.1.call-done = bf16[2048,1024]{1,0:T(8,128)(2,1)} async-done(((bf16[256,1024]{1,0:T(8,128)(2,1)}), bf16[2048,1024]{1,0:T(8,128)(2,1)}) %all-gather.18.cloned.1.call-update) | async-done | bytes 4194320 | tf_op jit(solution)/shard_map/all_gather | solution.py:151
  363.1 46.5 %all-gather.26.cloned.1.call-done = bf16[1024,2048]{1,0:T(8,128)(2,1)} async-done(((bf16[1024,1024]{1,0:T(8,128)(2,1)}), bf16[1024,2048]{1,0:T(8,128)(2,1)}) %all-gather.26.cloned.1.call-update) | async-done | bytes 4194320 | tf_op jit(solution)/shard_map/all_gather | solution.py:130
  483.9 22.0 gather_fusion.3
  507.7 20.7 gather_fusion.4
  539.3 299.9 %all-gather.32.cloned.1.call-done = bf16[16,2048,512]{2,1,0:T(8,128)(2,1)} async-done(((bf16[16,1024,512]{2,1,0:T(8,128)(2,1)}), bf16[16,2048,512]{2,1,0:T(8,128)(2,1)}) %all-gather.32.cloned.1.call-update) | async-done | bytes 33554448 | tf_op jit(solution)/shard_map/all_gather | solution.py:189
  839.1 26.0 fusion.75
  865.2 364.0 %all-gather.30.cloned.1.call-done = bf16[16,2048,512]{2,1,0:T(8,128)(2,1)} async-done(((bf16[16,1024,512]{2,1,0:T(8,128)(2,1)}), bf16[16,2048,512]{2,1,0:T(8,128)(2,1)}) %all-gather.30.cloned.1.call-update) | async-done | bytes 33554448 | tf_op jit(solution)/shard_map/all_gather | solution.py:188
  1229.2 25.8 fusion.74
  1255.0 364.4 %all-gather.34.cloned.1.call-done = bf16[16,2048,512]{2,1,0:T(8,128)(2,1)} async-done(((bf16[16,1024,512]{2,1,0:T(8,128)(2,1)}), bf16[16,2048,512]{2,1,0:T(8,128)(2,1)}) %all-gather.34.cloned.1.call-update) | async-done | bytes 33554448 | tf_op jit(solution)/shard_map/all_gather | solution.py:190
  1619.5 24.8 fusion.13
  1644.3 22.5 fusion.76
  1666.8 26.5 convolution_add_fusion
  1693.3 34.9 scatter_custom_fusion.3
  1850.5 49.0 %reduce-scatter.25.cloned.1.call-done = bf16[256,1024]{1,0:T(8,128)(2,1)} async-done(((bf16[2048,1024]{1,0:T(8,128)(2,1)}), bf16[256,1024]{1,0:T(8,128)(2,1)}) %reduce-scatter.25.cloned.1.call-update) | async-done | bytes 524304 | tf_op jit(solution)/shard_map/reduce_scatter | solution.py:322
  1910.8 81.4 %reduce-scatter.27.cloned.1.call-done = bf16[256,1024]{0,1:T(8,128)(2,1)} async-done(((bf16[2048,1024]{0,1:T(8,128)(2,1)}), bf16[256,1024]{0,1:T(8,128)(2,1)}) %reduce-scatter.27.cloned.1.call-update) | async-done | bytes 524304 | tf_op jit(solution)/shard_map/reduce_scatter | solution.py:328
  1997.1 23.3 fusion.48
  2020.4 33.9 scatter_custom_fusion.2
  2065.0 20.5 convolution_convert_fusion.2
  2087.3 20.5 convolution_convert_fusion.1
  2107.9 18.9 convolution_convert_fusion
  2128.6 38.2 reduce-scatter.43.cloned.1.call-done
  2168.7 95.9 %reduce-scatter.31.cloned.1.call-done = bf16[128,1024]{1,0:T(8,128)(2,1)} async-done(((bf16[2048,1024]{1,0:T(8,128)(2,1)}), bf16[128,1024]{1,0:T(8,128)(2,1)}) %reduce-scatter.31.cloned.1.call-update) | async-done | bytes 262160 | tf_op jit(solution)/shard_map/reduce_scatter | solution.py:368
  2291.8 49.0 %all-reduce = (f32[2,2048]{1,0:T(2,128)S(1)}, f32[128]{0:T(128)}, f32[128]{0:T(128)}, f32[3]{0:T(128)S(1)}) all-reduce(f32[2,2048]{1,0:T(2,128)S(1)} %maximum_dynamic-update-slice_fusion, f32[128]{0:T(128)S(1)} %copy-done.69, f32[128]{0:T(128)S(1)} %bitcast_reduce_fusion, ...), channel_id=1, replica_groups=mesh['fsdp'=2,'ctx'=8,'tp'=2] {'fsdp','ctx','tp'}, use_global_device_ids=true, to_apply=%region_42.43 | all-reduce | flops 4355 | bytes 34840 | tf_op jit(solution)/shard_map/psum | solution.py:399
  2342.0 46.3 %reduce-scatter.33.cloned.1.call-done = bf16[128,1024]{1,0:T(8,128)(2,1)} async-done(((bf16[2048,1024]{1,0:T(8,128)(2,1)}), bf16[128,1024]{1,0:T(8,128)(2,1)}) %reduce-scatter.33.cloned.1.call-update) | async-done | bytes 262160 | tf_op jit(solution)/shard_map/reduce_scatter | solution.py:371
  2390.1 96.0 %reduce-scatter.35.cloned.1.call-done = bf16[128,1024]{1,0:T(8,128)(2,1)} async-done(((bf16[2048,1024]{1,0:T(8,128)(2,1)}), bf16[128,1024]{1,0:T(8,128)(2,1)}) %reduce-scatter.35.cloned.1.call-update) | async-done | bytes 262160 | tf_op jit(solution)/shard_map/reduce_scatter | solution.py:374
  2488.0 682.1 %reduce-scatter.37.cloned.1.call-done = bf16[16,128,512]{2,1,0:T(8,128)(2,1)} async-done(((bf16[16,2048,512]{2,1,0:T(8,128)(2,1)}), bf16[16,128,512]{2,1,0:T(8,128)(2,1)}) %reduce-scatter.37.cloned.1.call-update) | async-done | bytes 2097168 | tf_op jit(solution)/shard_map/reduce_scatter | solution.py:274
  3174.2 681.6 %reduce-scatter.39.cloned.1.call-done = bf16[16,128,512]{2,1,0:T(8,128)(2,1)} async-done(((bf16[16,2048,512]{2,1,0:T(8,128)(2,1)}), bf16[16,128,512]{2,1,0:T(8,128)(2,1)}) %reduce-scatter.39.cloned.1.call-update) | async-done | bytes 2097168 | tf_op jit(solution)/shard_map/reduce_scatter | solution.py:277
  3860.0 681.6 %reduce-scatter.41.cloned.1.call-done = bf16[16,128,512]{2,1,0:T(8,128)(2,1)} async-done(((bf16[16,2048,512]{2,1,0:T(8,128)(2,1)}), bf16[16,128,512]{2,1,0:T(8,128)(2,1)}) %reduce-scatter.41.cloned.1.call-update) | async-done | bytes 2097168 | tf_op jit(solution)/shard_map/reduce_scatter | solution.py:280
  (368 shorter events, 373.6 us)
Async XLA Ops:
  7.2 19.5 all-gather.14.cloned.1.call-start
  15.0 71.3 %all-gather.20.cloned.1.call-start = ((), (), s32[]{:S(2)}) async-start(), calls=%async_computation.17 | async-start | bytes 6291456 | tf_op jit(solution)/shard_map/all_gather | solution.py:127
  15.7 128.8 %all-gather.22.cloned.1.call-start = ((), (), s32[]{:S(2)}) async-start(), calls=%async_computation.18 | async-start | bytes 6291456 | tf_op jit(solution)/shard_map/all_gather | solution.py:128
  16.5 186.3 %all-gather.16.cloned.1.call-start = ((), (), s32[]{:S(2)}) async-start(), calls=%async_computation.15 | async-start | bytes 6291456 | tf_op jit(solution)/shard_map/all_gather | solution.py:129
  17.0 261.7 %all-gather.24.cloned.1.call-start = ((), (), s32[]{:S(2)}) async-start(), calls=%async_computation.19 | async-start | bytes 4718592 | tf_op jit(solution)/shard_map/all_gather | solution.py:150
  168.3 184.6 %all-gather.18.cloned.1.call-start = ((), (), s32[]{:S(2)}) async-start(), calls=%async_computation.16 | async-start | bytes 4718592 | tf_op jit(solution)/shard_map/all_gather | solution.py:151
  207.0 202.6 %all-gather.26.cloned.1.call-start = ((), (), s32[]{:S(2)}) async-start(), calls=%async_computation.20 | async-start | bytes 6291456 | tf_op jit(solution)/shard_map/all_gather | solution.py:130
  207.8 214.9 %reduce-scatter.19.cloned.1.call-start = ((), (), s32[]{:S(2)}) async-start(), calls=%async_computation.21 | async-start | bytes 1572864 | tf_op jit(solution)/shard_map/reduce_scatter | solution.py:83
  414.0 69.9 %all-gather.36.cloned.1.call-start = ((), (), s32[]{:S(2)}) async-start(), calls=%async_computation.27 | async-start | bytes 1572864 | tf_op jit(solution)/shard_map/all_gather | solution.py:80
  414.8 91.2 %all-gather.28.cloned.1.call-start = ((), (), s32[]{:S(2)}) async-start(), calls=%async_computation.22 | async-start | bytes 1572864 | tf_op jit(solution)/shard_map/all_gather | solution.py:80
  429.7 409.4 %all-gather.32.cloned.1.call-start = ((), (), s32[]{:S(2)}) async-start(), calls=%async_computation.24 | async-start | bytes 50331648 | tf_op jit(solution)/shard_map/all_gather | solution.py:189
  430.5 798.8 %all-gather.30.cloned.1.call-start = ((), (), s32[]{:S(2)}) async-start(), calls=%async_computation.23 | async-start | bytes 50331648 | tf_op jit(solution)/shard_map/all_gather | solution.py:188
  431.1 1188.4 %all-gather.34.cloned.1.call-start = ((), (), s32[]{:S(2)}) async-start(), calls=%async_computation.25 | async-start | bytes 50331648 | tf_op jit(solution)/shard_map/all_gather | solution.py:190
  431.8 1321.3 %reduce-scatter.23.cloned.1.call-start = ((), (), s32[]{:S(2)}) async-start(), calls=%async_computation.28 | async-start | bytes 1572864 | tf_op jit(solution)/shard_map/reduce_scatter | solution.py:83
  1731.0 39.6 all-gather.38.cloned.1.call-start
  1761.4 138.1 %reduce-scatter.25.cloned.1.call-start = ((), (), s32[]{:S(2)}) async-start(), calls=%async_computation.30 | async-start | bytes 4718592 | tf_op jit(solution)/shard_map/reduce_scatter | solution.py:322
  1810.1 182.1 %reduce-scatter.27.cloned.1.call-start = ((), (), s32[]{:S(2)}) async-start(), calls=%async_computation.31 | async-start | bytes 4718592 | tf_op jit(solution)/shard_map/reduce_scatter | solution.py:328
  1820.9 306.0 %reduce-scatter.45.cloned.1.call-start = ((), (), s32[]{:S(2)}) async-start(), calls=%async_computation.40 | async-start | bytes 557056
  1822.3 344.5 %reduce-scatter.43.cloned.1.call-start = ((), (), s32[]{:S(2)}) async-start(), calls=%async_computation.39 | async-start | bytes 4456448
  1832.5 432.1 %reduce-scatter.31.cloned.1.call-start = ((), (), s32[]{:S(2)}) async-start(), calls=%async_computation.33 | async-start | bytes 4456448 | tf_op jit(solution)/shard_map/reduce_scatter | solution.py:368
  1845.3 428.6 %reduce-scatter.29.cloned.1.call-start = ((), (), s32[]{:S(2)}) async-start(), calls=%async_computation.32 | async-start | bytes 1572864 | tf_op jit(solution)/shard_map/reduce_scatter | solution.py:83
  1996.9 289.1 %reduce-scatter.21.cloned.1.call-start = ((), (), s32[]{:S(2)}) async-start(), calls=%async_computation.26 | async-start | bytes 1572864 | tf_op jit(solution)/shard_map/reduce_scatter | solution.py:83
  2055.4 332.9 %reduce-scatter.33.cloned.1.call-start = ((), (), s32[]{:S(2)}) async-start(), calls=%async_computation.34 | async-start | bytes 4456448 | tf_op jit(solution)/shard_map/reduce_scatter | solution.py:371
  2059.9 426.3 %reduce-scatter.35.cloned.1.call-start = ((), (), s32[]{:S(2)}) async-start(), calls=%async_computation.35 | async-start | bytes 4456448 | tf_op jit(solution)/shard_map/reduce_scatter | solution.py:374
  2063.3 1106.8 %reduce-scatter.37.cloned.1.call-start = ((), (), s32[]{:S(2)}) async-start(), calls=%async_computation.36 | async-start | bytes 35651584 | tf_op jit(solution)/shard_map/reduce_scatter | solution.py:274
  2085.6 1770.2 %reduce-scatter.39.cloned.1.call-start = ((), (), s32[]{:S(2)}) async-start(), calls=%async_computation.37 | async-start | bytes 35651584 | tf_op jit(solution)/shard_map/reduce_scatter | solution.py:277
  2107.8 2433.8 %reduce-scatter.41.cloned.1.call-start = ((), (), s32[]{:S(2)}) async-start(), calls=%async_computation.38 | async-start | bytes 35651584 | tf_op jit(solution)/shard_map/reduce_scatter | solution.py:280
  2126.8 159.1 %copy-start.18 = (bf16[256,1024]{1,0:T(8,128)(2,1)S(1)}, bf16[256,1024]{1,0:T(8,128)(2,1)}, u32[]{:S(2)}) copy-start(bf16[256,1024]{1,0:T(8,128)(2,1)} %reduce-scatter.19.cloned.1.call-done) | copy-start | bytes 1572868
  2126.8 159.1 %copy-start.21 = (bf16[256,1024]{1,0:T(8,128)(2,1)S(1)}, bf16[256,1024]{1,0:T(8,128)(2,1)}, u32[]{:S(2)}) copy-start(bf16[256,1024]{1,0:T(8,128)(2,1)} %param.18) | copy-start | bytes 1572868
  2126.8 159.1 %copy-start.23 = (f32[256,1024]{1,0:T(8,128)S(1)}, f32[256,1024]{1,0:T(8,128)}, u32[]{:S(2)}) copy-start(f32[256,1024]{1,0:T(8,128)} %get-tuple-element.75) | copy-start | bytes 3145732
  2126.9 164.9 %copy-start.68 = (f32[1024]{0:T(1024)S(1)}, f32[1024]{0:T(1024)}, u32[]{:S(2)}) copy-start(f32[1024]{0:T(1024)} %get-tuple-element.19) | copy-start | bytes 12292
  2126.9 164.9 %copy-start.69 = (f32[128]{0:T(128)S(1)}, f32[128]{0:T(128)}, u32[]{:S(2)}) copy-start(f32[128]{0:T(128)} %get-tuple-element.17) | copy-start | bytes 1540
  (71 other events, 3364.5 us)
Sparse Core Ops, SparseCore 0:
  15.1 11.6 all-gather.13
  28.3 57.9 all-gather.19
  87.8 56.7 all-gather.21
  146.0 56.7 all-gather.15
  205.3 73.3 all-gather.23
  281.3 71.6 all-gather.17
  354.5 55.0 all-gather.25
  414.1 8.5 reduce-scatter.18
  424.3 10.2 all-gather.35
  436.6 10.3 all-gather.27
  448.7 390.4 all-gather.31
  840.6 388.5 all-gather.29
  1230.9 388.5 all-gather.33
  1731.1 8.5 reduce-scatter.22
  1761.5 9.0 all-gather.37
  1810.2 89.2 reduce-scatter.24
  1903.9 88.2 reduce-scatter.26
  1994.9 76.2 reduce-scatter.44
  2073.6 93.1 reduce-scatter.42
  2169.6 94.9 reduce-scatter.30
  2267.5 6.3 reduce-scatter.28
  2276.2 9.6 reduce-scatter.20
  2288.9 99.3 reduce-scatter.32
  2391.2 94.9 reduce-scatter.34
  2488.6 681.3 reduce-scatter.36
  3172.4 683.4 reduce-scatter.38
  3858.1 683.4 reduce-scatter.40
where the time goes:
time: 4560 us; the launch traced here: 4550 us
  waiting for transfers between devices  3840 us (84%)
  matrix products  315 us (7%)
  other arithmetic  176 us (4%)
  local copies, waits for them, and re-layouts  138 us (3%)
  blocking collectives  67.9 us (1%)
    reduce_scatter x1, waiting for transfers between devices, on_device(): lax.psum_scatter(grad_gate_full.astype(jnp.bfloat16), ('fsdp', 'ctx'), sc...  682 us
    reduce_scatter x1, waiting for transfers between devices, on_device(): lax.psum_scatter(grad_up_full.astype(jnp.bfloat16), ('fsdp', 'ctx'), scat...  682 us
    reduce_scatter x1, waiting for transfers between devices, on_device(): lax.psum_scatter(grad_down_full.astype(jnp.bfloat16), ('fsdp', 'ctx'), sc...  682 us
    all_gather x1, waiting for transfers between devices, on_device(): lax.all_gather(w_down, 'fsdp', axis=1, tiled=True)  364 us
    all_gather x1, waiting for transfers between devices, on_device(): lax.all_gather(w_gate, 'fsdp', axis=1, tiled=True)  364 us
    all_gather x1, waiting for transfers between devices, on_device(): lax.all_gather(w_up, 'fsdp', axis=1, tiled=True)  300 us
    reduce_scatter x1, waiting for transfers between devices, on_device(): lax.psum_scatter(grad_value_full.astype(jnp.bfloat16), ('fsdp', 'ctx'), s...  96 us
    reduce_scatter x1, waiting for transfers between devices, on_device(): lax.psum_scatter(grad_query_full.astype(jnp.bfloat16), ('fsdp', 'ctx'), s...  95.9 us
  transfers between devices with their start and end apart: 27, of which 23 were waited for; matrix products, arithmetic and copies ran while one was open for 10% of the time, Pallas kernels for 0%

commit v1 on v0

v1 whole, which is shorter than its diff:
```python
import jax
import numpy as np
import jax.numpy as jnp
from jax import lax
from jax.sharding import PartitionSpec as P

norm_eps = 1e-06
rope_base = 10000.0


def locate(pack_spots, lengths_row):
    seq_ends = jnp.cumsum(lengths_row)
    starts = seq_ends - lengths_row
    segment = jnp.sum((pack_spots[:, None] >= seq_ends[None, :]).astype(jnp.int32), axis=1)
    slot_ids = jnp.arange(lengths_row.shape[0], dtype=jnp.int32)
    seq_begin = jnp.sum(
        jnp.where(segment[:, None] == slot_ids[None, :], starts[None, :], 0), axis=1
    )
    return (segment, pack_spots - seq_begin)


def rope_tables(pack_spots, head_dim):
    half_dim = head_dim // 2
    inv_freq = rope_base ** (-(jnp.arange(half_dim, dtype=jnp.float32) * 2.0 / head_dim))
    angle_grid = pack_spots.astype(jnp.float32)[:, None] * inv_freq[None, :]
    cosine = jnp.concatenate([jnp.cos(angle_grid), jnp.cos(angle_grid)], axis=1)
    sine_table = jnp.concatenate([jnp.sin(angle_grid), jnp.sin(angle_grid)], axis=1)
    return (cosine[:, None, :], sine_table[:, None, :])


def rotate(tensor, cosine, sine_table):
    half_dim = tensor.shape[-1] // 2
    turned = jnp.concatenate([-tensor[..., half_dim:], tensor[..., :half_dim]], axis=-1)
    return tensor * cosine + turned * sine_table


def unrotate(grad_rot, cosine, sine_table):
    half_dim = grad_rot.shape[-1] // 2
    shifted = grad_rot * sine_table
    turned = jnp.concatenate([shifted[..., half_dim:], -shifted[..., :half_dim]], axis=-1)
    return grad_rot * cosine + turned


def on_device(
    hidden_in,
    cotangent,
    positions,
    seq_lengths,
    expert_ids,
    attn_norm,
    ffn_norm,
    query_norm,
    key_norm,
    w_query,
    w_key,
    w_value,
    w_out,
    w_router,
    w_gate,
    w_up,
    w_down,
):
    tok_rows, col_count = hidden_in.shape
    packs_axis, ctx_size, tp_size = (
        lax.axis_size("fsdp"),
        lax.axis_size("ctx"),
        lax.axis_size("tp"),
    )
    ctx_place, tp_place = lax.axis_index("ctx"), lax.axis_index("tp")
    width_all = col_count * tp_size
    pack_rows = tok_rows * ctx_size
    head_dim = query_norm.shape[0]
    local_heads = w_query.shape[1] // head_dim
    expert_count = w_gate.shape[0]
    own_experts = expert_count // ctx_size
    own_heads = max(1, local_heads // ctx_size)
    sharers = max(1, ctx_size // local_heads)
    head_cols = own_heads * head_dim
    score_scale = head_dim ** (-0.5)
    wide = jnp.float32
    slim = jnp.bfloat16

    masks_even = [ctx_size >> (i + 1) for i in range(ctx_size.bit_length() - 1)]
    masks_odd = masks_even[:-2] + masks_even[:-3:-1]

    def offsets(masks):
        return np.array(
            [
                sum(mask for bit, mask in enumerate(masks) if (j >> bit) & 1)
                for j in range(ctx_size)
            ],
            np.int32,
        )

    block_order = ctx_place ^ jnp.where(
        tp_place % 2 == 0, jnp.asarray(offsets(masks_even)), jnp.asarray(offsets(masks_odd))
    )

    def move(tensor, step):
        pairs = []
        for f in range(packs_axis):
            for c in range(ctx_size):
                for t in range(tp_size):
                    to_c, to_t = step(c, t)
                    pairs.append(
                        (
                            (f * ctx_size + c) * tp_size + t,
                            (f * ctx_size + to_c) * tp_size + to_t,
                        )
                    )
        return lax.ppermute(tensor, ("fsdp", "ctx", "tp"), pairs)

    def ctx_step(index):
        return lambda c, t: (c ^ (masks_even, masks_odd)[t % 2][index], t)

    def tp_step(shift):
        return lambda c, t: (c, t ^ shift)

    def reorder(tensor, shift):
        if shift % 2 == 0:
            return tensor
        shape = tensor.shape
        return jnp.swapaxes(tensor.reshape((2, 2, shape[0] // 4) + shape[1:]), 0, 1).reshape(shape)

    def by_place(parts):
        shift = 1
        while shift < tp_size:
            swap = (tp_place & shift) > 0
            parts = [jnp.where(swap, parts[i ^ shift], parts[i]) for i in range(tp_size)]
            shift *= 2
        return parts

    def gather_pack(tensor):
        held = tensor[None]
        for index in range(len(masks_even)):
            held = jnp.concatenate([held, move(held, ctx_step(index))], axis=0)
        parts = [held]
        for shift in range(1, tp_size):
            parts.append(reorder(move(held, tp_step(shift)), shift))
        return [part.reshape(pack_rows, col_count) for part in by_place(parts)]

    def scatter_pack(tensor):
        def columns(shift):
            return lax.dynamic_slice_in_dim(
                tensor, (tp_place ^ shift) * col_count, col_count, 1
            ).reshape(ctx_size, tok_rows, col_count)

        total = columns(0).astype(wide)
        for shift in range(1, tp_size):
            total = total + reorder(move(columns(shift), tp_step(shift)), shift).astype(wide)
        for index in reversed(range(len(masks_even))):
            half = total.shape[0] // 2
            total = total.astype(slim)
            total = total[:half].astype(wide) + move(total[half:], ctx_step(index)).astype(wide)
        return total[0]

    def row_total(tensor):
        return lax.psum(tensor, "tp")

    def dot(left, right, dims):
        return lax.dot_general(left, right, ((dims[:1], dims[1:]), ((), ())), preferred_element_type=wide)

    head_place = ctx_place if sharers == 1 else ctx_place % local_heads

    def head_slice(weight, axis):
        return lax.dynamic_slice_in_dim(weight, head_place * head_cols, head_cols, axis)

    def expert_slice(weight):
        return lax.dynamic_slice_in_dim(weight, ctx_place * own_experts, own_experts, 0)

    qkv_weight = lax.all_gather(
        jnp.concatenate([head_slice(w, 1) for w in (w_query, w_key, w_value)], axis=1),
        "fsdp",
        axis=0,
        tiled=True,
    )
    out_weight = lax.all_gather(head_slice(w_out, 0), "fsdp", axis=1, tiled=True)
    router_full = lax.all_gather(w_router, "fsdp", axis=1, tiled=True)
    gate_weight, up_weight, down_weight = (
        lax.all_gather(expert_slice(w), "fsdp", axis=1, tiled=True)
        for w in (w_gate, w_up, w_down)
    )
    gain_first_all, gain_second_all = (
        lax.all_gather(g, "tp", axis=0, tiled=True).astype(wide) for g in (attn_norm, ffn_norm)
    )

    def in_order(table):
        return table.reshape((ctx_size, tok_rows) + table.shape[1:])[block_order].reshape(table.shape)

    segment, place = locate(in_order(positions[0]), seq_lengths[0])
    cosine, sine_table = rope_tables(place, head_dim)
    ids_all = in_order(lax.all_gather(expert_ids, "ctx", axis=0, tiled=True))
    expert_range = jnp.arange(expert_count, dtype=jnp.int32)
    chosen = jnp.sum(
        (ids_all[:, :, None] == expert_range[None, None, :]).astype(wide), axis=1
    )

    def query_rows(tensor):
        if sharers == 1:
            return tensor
        shape = tensor.shape
        return tensor.reshape((ctx_size // 2, 2, tok_rows) + shape[1:])[:, 0].reshape(
            (shape[0] // 2,) + shape[1:]
        )

    def all_rows(tensor):
        if sharers == 1:
            return tensor
        shape = tensor.shape
        part = tensor.reshape((ctx_size // 2, 1, tok_rows) + shape[1:])
        return jnp.concatenate([part, jnp.zeros_like(part)], axis=1).reshape(
            (shape[0] * 2,) + shape[1:]
        )

    hidden_all = jnp.concatenate(gather_pack(hidden_in), axis=1).astype(wide)
    inv_all = lax.rsqrt(jnp.mean(hidden_all * hidden_all, axis=1, keepdims=True) + norm_eps)
    normed_first = (hidden_all * inv_all * gain_first_all).astype(slim)
    qkv_raw = dot(normed_first, qkv_weight, (1, 0))

    def heads_of(tensor):
        return tensor.reshape(-1, own_heads, head_dim)

    query_raw = heads_of(query_rows(qkv_raw[:, :head_cols]))
    key_raw = heads_of(qkv_raw[:, head_cols : 2 * head_cols])
    value_low = heads_of(qkv_raw[:, 2 * head_cols :]).astype(slim)
    gain_query = query_norm.astype(wide)
    gain_key = key_norm.astype(wide)
    query_turn = (query_rows(cosine), query_rows(sine_table))
    key_turn = (cosine, sine_table)

    def prepare(raw_proj, gain_vec, turn):
        inverse = lax.rsqrt(jnp.mean(raw_proj * raw_proj, axis=2, keepdims=True) + norm_eps)
        return rotate(raw_proj * inverse * gain_vec, *turn).astype(slim), inverse

    query_low, query_inv = prepare(query_raw, gain_query, query_turn)
    key_low, key_inv = prepare(key_raw, gain_key, key_turn)
    same_seq = (query_rows(segment)[:, None] == segment[None, :])[None]

    def scores_of():
        raw_scores = (
            jnp.einsum("qhd,khd->hqk", query_low, key_low, preferred_element_type=wide)
            * score_scale
        )
        return jnp.where(same_seq, raw_scores, -1e30)

    scores = scores_of()
    row_peak = jnp.max(scores, axis=2, keepdims=True)
    row_exp = jnp.exp(scores - row_peak)
    row_sum = jnp.sum(row_exp, axis=2, keepdims=True)
    log_total = row_peak + jnp.log(row_sum)
    probs_low = (row_exp / row_sum).astype(slim)
    attended_low = all_rows(
        jnp.einsum("hqk,khd->qhd", probs_low, value_low, preferred_element_type=wide)
        .reshape(-1, head_cols)
        .astype(slim)
    )
    attn_branch = scatter_pack(dot(attended_low, out_weight, (1, 0)).astype(slim))

    resid_in = hidden_in.astype(wide)
    middle = resid_in + attn_branch
    gain_second = ffn_norm.astype(wide)
    inv_second = lax.rsqrt(row_total(jnp.sum(middle * middle, axis=1)) / width_all + norm_eps)[
        :, None
    ]
    normed_second = jnp.concatenate(
        gather_pack((middle * inv_second * gain_second).astype(slim)), axis=1
    )
    cotangent_all = jnp.concatenate(gather_pack(cotangent), axis=1)

    logits = dot(normed_second, router_full, (1, 1))
    logit_exp = jnp.exp(logits - jnp.max(logits, axis=1, keepdims=True))
    route_probs = logit_exp / jnp.sum(logit_exp, axis=1, keepdims=True)
    gate_weights = route_probs * chosen
    expert_part = 0.0
    back_part = 0.0
    grad_logits = 0.0
    grad_gate_list, grad_up_list, grad_down_list = [], [], []
    for slot in range(own_experts):
        mine = (expert_range == ctx_place * own_experts + slot).astype(wide)[None, :]
        gates = jnp.sum(gate_weights * mine, axis=1, keepdims=True)
        gate_proj = dot(normed_second, gate_weight[slot], (1, 0))
        up_proj = dot(normed_second, up_weight[slot], (1, 0))
        gate_sigmoid = jax.nn.sigmoid(gate_proj)
        activity = gate_proj * gate_sigmoid * up_proj
        mixed_low = (gates * activity).astype(slim)
        expert_part = expert_part + dot(mixed_low, down_weight[slot], (1, 1))
        grad_mixed = dot(cotangent_all, down_weight[slot], (1, 0)).astype(slim).astype(wide)
        grad_gates = jnp.sum(grad_mixed * activity, axis=1, keepdims=True)
        grad_activity = grad_mixed * gates
        grad_gate_low = (
            grad_activity * up_proj * gate_sigmoid * (1.0 + gate_proj * (1.0 - gate_sigmoid))
        ).astype(slim)
        grad_up_low = (grad_activity * gate_proj * gate_sigmoid).astype(slim)
        grad_logits = grad_logits + gates * grad_gates * (mine - route_probs)
        back_part = back_part + dot(grad_gate_low, gate_weight[slot], (1, 1))
        back_part = back_part + dot(grad_up_low, up_weight[slot], (1, 1))
        grad_gate_list.append(dot(normed_second, grad_gate_low, (0, 0)))
        grad_up_list.append(dot(normed_second, grad_up_low, (0, 0)))
        grad_down_list.append(dot(cotangent_all, mixed_low, (0, 0)))
    grad_logits_low = grad_logits.astype(slim)
    back_part = back_part + dot(grad_logits_low, router_full, (1, 0))
    grad_second = scatter_pack(back_part.astype(slim))
    expert_branch = scatter_pack(expert_part.astype(slim))
    hidden_out = (middle + expert_branch).astype(slim)
    grad_router = row_total(
        lax.psum_scatter(
            dot(grad_logits_low, normed_second, (0, 0)).astype(slim),
            ("fsdp", "ctx"),
            scatter_dimension=1,
            tiled=True,
        ).astype(wide)
    )

    def spread_experts(parts):
        mine = lax.psum_scatter(
            jnp.stack(parts).astype(slim), "fsdp", scatter_dimension=1, tiled=True
        )
        return lax.all_to_all(mine, "ctx", split_axis=1, concat_axis=0, tiled=True).astype(wide)

    grad_gate = spread_experts(grad_gate_list)
    grad_up = spread_experts(grad_up_list)
    grad_down = spread_experts(grad_down_list)

    gain_two_grad = jnp.sum(grad_second * middle * inv_second, axis=0)
    second_scaled = grad_second * gain_second
    second_inner = row_total(jnp.sum(second_scaled * middle, axis=1))[:, None]
    grad_middle = (
        cotangent.astype(wide)
        + inv_second * second_scaled
        - middle * inv_second**3 * second_inner / width_all
    )
    grad_middle_all = jnp.concatenate(gather_pack(grad_middle.astype(slim)), axis=1)

    grad_attended = dot(grad_middle_all, out_weight, (1, 1)).astype(slim)
    grad_out_part = dot(attended_low, grad_middle_all, (0, 0))
    probs_back = jnp.exp(scores_of() - log_total)
    grad_att_heads = heads_of(query_rows(grad_attended))
    grad_probs = jnp.einsum(
        "qhd,khd->hqk", grad_att_heads, value_low, preferred_element_type=wide
    )
    grad_scores = (
        probs_back * (grad_probs - jnp.sum(probs_back * grad_probs, axis=2, keepdims=True))
    ).astype(slim)
    grad_query_rot = (
        jnp.einsum("hqk,khd->qhd", grad_scores, key_low, preferred_element_type=wide) * score_scale
    )
    grad_key_rot = (
        jnp.einsum("hqk,qhd->khd", grad_scores, query_low, preferred_element_type=wide)
        * score_scale
    )
    grad_value_low = jnp.einsum(
        "hqk,qhd->khd", probs_back.astype(slim), grad_att_heads, preferred_element_type=wide
    ).astype(slim)

    def prepare_back(grad_rot, raw_proj, inverse, gain_vec, turn):
        grad_normed = unrotate(grad_rot, *turn)
        weighted = grad_normed * gain_vec
        grad_raw = inverse * weighted - raw_proj * inverse**3 * jnp.mean(
            weighted * raw_proj, axis=2, keepdims=True
        )
        gain_grad = jnp.sum(grad_normed * raw_proj * inverse, axis=(0, 1))
        return grad_raw.reshape(-1, head_cols).astype(slim), gain_grad

    grad_query_low, query_gain_grad = prepare_back(
        grad_query_rot, query_raw, query_inv, gain_query, query_turn
    )
    grad_key_low, key_gain_grad = prepare_back(
        grad_key_rot, key_raw, key_inv, gain_key, key_turn
    )
    grad_qkv_low = jnp.concatenate(
        [all_rows(grad_query_low), grad_key_low, grad_value_low.reshape(-1, head_cols)], axis=1
    )
    grad_first = scatter_pack(dot(grad_qkv_low, qkv_weight, (1, 1)).astype(slim))
    grad_qkv_part = dot(normed_first, grad_qkv_low, (0, 0))

    def over_sharers(tensor):
        if sharers == 1:
            return tensor.astype(wide)
        return jnp.sum(
            tensor.reshape((sharers, local_heads) + tensor.shape[1:]).astype(wide), axis=0
        )

    qkv_mine = lax.psum_scatter(
        grad_qkv_part.astype(slim), "fsdp", scatter_dimension=0, tiled=True
    )
    qkv_rows = qkv_mine.shape[0] // ctx_size
    qkv_mine = over_sharers(
        lax.all_to_all(
            qkv_mine.reshape(ctx_size, qkv_rows, 3 * head_cols), "ctx", split_axis=0, concat_axis=0
        )
    )
    grad_query, grad_key, grad_value = (
        jnp.swapaxes(qkv_mine[:, :, i * head_cols : (i + 1) * head_cols], 0, 1).reshape(qkv_rows, -1)
        for i in range(3)
    )
    out_mine = lax.psum_scatter(
        grad_out_part.astype(slim), "fsdp", scatter_dimension=1, tiled=True
    )
    out_cols = out_mine.shape[1] // ctx_size
    out_mine = jnp.swapaxes(out_mine.reshape(head_cols, ctx_size, out_cols), 0, 1)
    grad_out = over_sharers(
        lax.all_to_all(out_mine, "ctx", split_axis=0, concat_axis=0)
    ).reshape(-1, out_cols)

    gain_first = attn_norm.astype(wide)
    inv_first = lax.dynamic_slice_in_dim(inv_all, 0, tok_rows, 0)
    gain_one_grad = jnp.sum(grad_first * resid_in * inv_first, axis=0)
    first_scaled = grad_first * gain_first
    first_inner = row_total(jnp.sum(first_scaled * resid_in, axis=1))[:, None]
    grad_hidden = (
        grad_middle + inv_first * first_scaled - resid_in * inv_first**3 * first_inner / width_all
    )
    gains_part = lax.dynamic_update_slice(
        jnp.zeros((2, width_all), wide),
        jnp.stack([gain_one_grad, gain_two_grad]),
        (0, tp_place * col_count),
    )
    stream_part = jnp.stack(
        [
            jnp.sum(middle * middle),
            jnp.sum(attn_branch * attn_branch),
            jnp.sum(expert_branch * expert_branch),
        ]
    )
    stream_sums, gains_sum, query_gain_sum, key_gain_sum = lax.psum(
        (stream_part, gains_part, query_gain_grad, key_gain_grad), ("fsdp", "ctx", "tp")
    )
    token_count = tok_rows * packs_axis * ctx_size
    stream_rms = jnp.sqrt(stream_sums / (token_count * width_all))
    return (
        hidden_out,
        grad_hidden,
        gains_sum[0],
        gains_sum[1],
        query_gain_sum,
        key_gain_sum,
        grad_query,
        grad_key,
        grad_value,
        grad_out,
        grad_router,
        grad_gate,
        grad_up,
        grad_down,
        stream_rms,
    )


def solution(mesh):
    return jax.shard_map(
        on_device,
        mesh=mesh,
        in_specs=(
            P(("fsdp", "ctx"), "tp"),
            P(("fsdp", "ctx"), "tp"),
            P("fsdp", None),
            P("fsdp", None),
            P(("fsdp", "ctx"), None),
            P("tp"),
            P("tp"),
            P(),
            P(),
            P("fsdp", "tp"),
            P("fsdp", "tp"),
            P("fsdp", "tp"),
            P("tp", "fsdp"),
            P(None, "fsdp"),
            P(None, "fsdp", "tp"),
            P(None, "fsdp", "tp"),
            P(None, "fsdp", "tp"),
        ),
        out_specs=(
            P(("fsdp", "ctx"), "tp"),
            P(("fsdp", "ctx"), "tp"),
            P(),
            P(),
            P(),
            P(),
            P(("fsdp", "ctx"), "tp"),
            P(("fsdp", "ctx"), "tp"),
            P(("fsdp", "ctx"), "tp"),
            P("tp", ("fsdp", "ctx")),
            P(None, ("fsdp", "ctx")),
            P(None, ("fsdp", "ctx"), "tp"),
            P(None, ("fsdp", "ctx"), "tp"),
            P(None, ("fsdp", "ctx"), "tp"),
            P(),
        ),
        check_vma=False,
    )
```

time: 4560 us -> 1160 us (0.25)
  waiting for transfers between devices: 3840 us -> 437 us
  matrix products: 315 us -> 258 us
  starting transfers between devices: 2.06 us -> 55.1 us
    reduce_scatter x12 -> x5, waiting for transfers between devices: 2440 us -> 22 us  [the longest x1 21.3 us: on_device(): lax.psum_scatter(grad_out_part.astype(slim), 'fsdp', scatter_dimension=1,...]
    all_gather x13 -> x4, waiting for transfers between devices: 1360 us -> 0.06 us  [the longest x3 0.04 us: on_device(): lax.all_gather(expert_slice(w), 'fsdp', axis=1, tiled=True)]
    ppermute x0 -> x32, waiting for transfers between devices: none -> 349 us  [move(): return lax.ppermute(tensor, ('fsdp', 'ctx', 'tp'), pairs)]
    scatter-add x3 -> x0, other arithmetic: 87.1 us -> none  [the longest x1 34.9 us: on_device(): back_part = jnp.zeros((tok_rows, width_all), jnp.float32).at[slot_token_f...]
    gather x7 -> x2, local copies, waits for them, and re-layouts: 77.2 us -> 1.12 us  [in_order(): table.reshape((ctx_size, tok_rows) + table.shape[1:])[block_order]]
    dot_general x29 -> x32, matrix products: 311 us -> 252 us  [the longest x27 223 us: dot(): lax.dot_general(left, right, ((dims[:1], dims[1:]), ((), ())), preferred_...]
    all_gather x1 -> x4, blocking collectives: 5.37 us -> 55.1 us  [the longest x1 30.5 us: on_device(): ids_all = in_order(lax.all_gather(expert_ids, 'ctx', axis=0, tiled=True))]
  transfers between devices with their start and end apart: 27 -> 47, of which waited for: 23 -> 26; matrix products, arithmetic and copies ran while one was open for 10% -> 34% of each run, Pallas kernels for 0% -> 0%
where the time goes in v1:
time: 1160 us; the launch traced here: 1150 us
  waiting for transfers between devices  437 us (38%)
  matrix products  258 us (22%)
  other arithmetic  162 us (14%)
  local copies, waits for them, and re-layouts  119 us (10%)
  blocking collectives  100 us (9%)
  starting transfers between devices  55.1 us (5%)
  between operations  16.8 us (1%)
    ppermute x32, waiting for transfers between devices, move(): return lax.ppermute(tensor, ('fsdp', 'ctx', 'tp'), pairs)  349 us
    dot_general x27, matrix products, dot(): lax.dot_general(left, right, ((dims[:1], dims[1:]), ((), ())), preferred_...  223 us
    psum x1, blocking collectives, on_device(): lax.psum((stream_part, gains_part, query_gain_grad, key_gain_grad), ('fsd...  37.3 us
    convert_element_type x12, other arithmetic, scatter_pack(): total = total.astype(slim)  32.7 us
    all_gather x1, blocking collectives, on_device(): ids_all = in_order(lax.all_gather(expert_ids, 'ctx', axis=0, tiled=True))  30.5 us
    ppermute x32, starting transfers between devices, move(): return lax.ppermute(tensor, ('fsdp', 'ctx', 'tp'), pairs)  28.5 us
    unnamed x11, waiting for transfers between devices  27.4 us
    convert_element_type x4, other arithmetic, scatter_pack(): reorder(move(columns(shift), tp_step(shift)), shift).astype(wide)  24.3 us
  transfers between devices with their start and end apart: 47, of which 26 were waited for; matrix products, arithmetic and copies ran while one was open for 34% of the time, Pallas kernels for 0%

profile of v1, /device:TPU:0, one launch (start us, length us, event | category | flops | bytes accessed | tf_op | source)
XLA Modules:
  0.0 1147.9 jit_solution(7864881943546414467)
XLA Ops:
  11.4 23.4 %collective-permute-done = bf16[1,256,1024]{2,1,0:T(8,128)(2,1)S(1)} collective-permute-done((bf16[1,256,1024]{2,1,0:T(8,128)(2,1)}, bf16[1,256,1024]{2,1,0:T(8,128)(2,1)S(1)}, u32[]{:S(2)}, u32[]{:S(2)}) %collective-permute-start) | collective-permute-done | bytes 524320 | tf_op jit(solution)/shard_map/ppermute | solution.py:111
  36.8 14.0 %collective-permute-done.1 = bf16[2,256,1024]{2,1,0:T(8,128)(2,1)S(1)} collective-permute-done((bf16[2,256,1024]{2,1,0:T(8,128)(2,1)S(1)}, bf16[2,256,1024]{2,1,0:T(8,128)(2,1)S(1)}, u32[]{:S(2)}, u32[]{:S(2)}) %collective-permute-start.1) | collective-permute-done | bytes 1048608 | tf_op jit(solution)/shard_map/ppermute | solution.py:111
  53.7 24.5 %collective-permute-done.2 = bf16[4,256,1024]{2,1,0:T(8,128)(2,1)S(1)} collective-permute-done((bf16[4,256,1024]{2,1,0:T(8,128)(2,1)S(1)}, bf16[4,256,1024]{2,1,0:T(8,128)(2,1)S(1)}, u32[]{:S(2)}, u32[]{:S(2)}) %collective-permute-start.2) | collective-permute-done | bytes 2097184 | tf_op jit(solution)/shard_map/ppermute | solution.py:111
  90.6 14.7 %all_gather.26 = bf16[128,2048]{1,0:T(8,128)(2,1)S(1)} all-gather(bf16[128,1024]{1,0:T(8,128)(2,1)S(1)} %constant_dynamic-slice_fusion.11), channel_id=1, replica_groups=mesh['fsdp'=2,'ctx'=8,'tp'=2] {'fsdp'}, dimensions={1}, use_global_device_ids=true | all-gather | bytes 786432 | tf_op jit(solution)/shard_map/all_gather | solution.py:177
  185.4 24.4 %collective-permute-done.5 = bf16[4,256,1024]{2,1,0:T(8,128)(2,1)S(1)} collective-permute-done((bf16[4,256,1024]{2,1,0:T(8,128)(2,1)S(1)}, bf16[4,256,1024]{2,1,0:T(8,128)(2,1)S(1)}, u32[]{:S(2)}, u32[]{:S(2)}) %collective-permute-start.5) | collective-permute-done | bytes 2097184 | tf_op jit(solution)/shard_map/ppermute | solution.py:111
  215.2 22.8 %collective-permute-done.6 = bf16[2,256,1024]{2,1,0:T(8,128)(2,1)S(1)} collective-permute-done((bf16[2,256,1024]{2,1,0:T(8,128)(2,1)S(1)}, bf16[2,256,1024]{2,1,0:T(8,128)(2,1)S(1)}, u32[]{:S(2)}, u32[]{:S(2)}) %collective-permute-start.6) | collective-permute-done | bytes 1048608 | tf_op jit(solution)/shard_map/ppermute | solution.py:111
  266.1 26.1 %collective-permute-done.8 = bf16[1,256,1024]{2,1,0:T(8,128)(2,1)S(1)} collective-permute-done((bf16[1,256,1024]{2,1,0:T(8,128)(2,1)S(1)}, bf16[1,256,1024]{2,1,0:T(8,128)(2,1)S(1)}, u32[]{:S(2)}, u32[]{:S(2)}) %collective-permute-start.8) | collective-permute-done | bytes 524320 | tf_op jit(solution)/shard_map/ppermute | solution.py:111
  295.8 20.9 %collective-permute-done.9 = bf16[2,256,1024]{2,1,0:T(8,128)(2,1)S(1)} collective-permute-done((bf16[2,256,1024]{2,1,0:T(8,128)(2,1)S(1)}, bf16[2,256,1024]{2,1,0:T(8,128)(2,1)S(1)}, u32[]{:S(2)}, u32[]{:S(2)}) %collective-permute-start.9) | collective-permute-done | bytes 1048608 | tf_op jit(solution)/shard_map/ppermute | solution.py:111
  333.9 16.7 %collective-permute-done.10 = bf16[4,256,1024]{2,1,0:T(8,128)(2,1)} collective-permute-done((bf16[4,256,1024]{2,1,0:T(8,128)(2,1)}, bf16[4,256,1024]{2,1,0:T(8,128)(2,1)}, u32[]{:S(2)}, u32[]{:S(2)}) %collective-permute-start.10) | collective-permute-done | bytes 2097184 | tf_op jit(solution)/shard_map/ppermute | solution.py:111
  359.0 30.5 %all_gather.28 = s32[2048,8]{0,1:T(8,128)S(1)} all-gather(s32[256,8]{0,1:T(8,128)S(1)} %copy-done.89), channel_id=1, replica_groups=mesh['fsdp'=2,'ctx'=8,'tp'=2] {'ctx'}, dimensions={0}, use_global_device_ids=true | all-gather | bytes 73728 | tf_op jit(solution)/shard_map/all_gather | solution.py:192
  418.1 10.7 fusion.50
  428.8 10.7 fusion.52
  439.5 13.2 %fusion.29 = (f32[2048]{0:T(1024)S(1)}, f32[2048,512]{0,1:T(8,128)}, bf16[2048,512]{0,1:T(8,128)(2,1)}, bf16[2048,512]{0,1:T(8,128)(2,1)}) fusion(f32[2048,512]{0,1:T(8,128)} %fusion.52, f32[2048,512]{0,1:T(8,128)} %fusion.50, f32[2048]{0:T(1024)S(1)} %get-tuple-element.29, bf16[2,2048,512]{2,1,0:T(8,128)(2,1)} %all-gather.11.cloned.1.call-done, ...), kind=kOutput, calls=%fused_computation.58 | convolution fusion | flops 4332713984 | bytes 27279360 | tf_op jit(solution)/shard_map/dot_general | solution.py:161
  468.2 12.9 %fusion.30 = (f32[2048]{0:T(1024)S(1)}, f32[2048,512]{0,1:T(8,128)}, bf16[2048,512]{0,1:T(8,128)(2,1)}, bf16[2048,512]{0,1:T(8,128)(2,1)}) fusion(f32[2048,512]{0,1:T(8,128)} %fusion.57, f32[2048,512]{0,1:T(8,128)} %fusion.55, f32[2048]{0:T(1024)S(1)} %get-tuple-element.28, bf16[2,2048,512]{2,1,0:T(8,128)(2,1)} %all-gather.11.cloned.1.call-done, ...), kind=kOutput, calls=%fused_computation.59 | convolution fusion | flops 4332713984 | bytes 27279360 | tf_op jit(solution)/shard_map/dot_general | solution.py:161
  481.2 8.7 fusion.53
  489.9 15.6 %add_convert_fusion.1 = bf16[2048,2048]{1,0:T(8,128)(2,1)} fusion(f32[2048,2048]{1,0:T(8,128)} %fusion.53, bf16[2,2048,512]{2,1,0:T(8,128)(2,1)} %all-gather.11.cloned.1.call-done, f32[2048,512]{0,1:T(8,128)} %get-tuple-element.43, f32[2048]{0:T(1024)S(1)} %get-tuple-element.28), kind=kOutput, calls=%fused_computation.11 | convolution fusion | flops 4305453056 | bytes 31465472 | tf_op jit(solution)/shard_map/dot_general | solution.py:161
  546.8 21.7 %add_convert_fusion = bf16[2048,2048]{1,0:T(8,128)(2,1)S(1)} fusion(f32[2048,2048]{1,0:T(8,128)} %fusion.56, f32[2048,2048]{1,0:T(8,128)} %fusion.54, f32[2048,2048]{1,0:T(8,128)} %fusion.49, f32[2048,2048]{1,0:T(8,128)} %fusion.51, bf16[16,2048]{1,0:T(8,128)(2,1)S(1)} %copy-done.60, f32[2048]{0:T(1024)S(1)} %mul.575, f32[2048]{0:T(1024)S(1)} %mul.571, ...), kind=kOutput, calls=%fused_computation.10 | convolution fusion | flops 155451392 | bytes 75726976 | tf_op jit(solution)/shard_map/dot_general | solution.py:161
  573.5 9.5 fusion.35
  637.0 32.5 %collective-permute-done.21 = bf16[4,256,1024]{2,1,0:T(8,128)(2,1)S(1)} collective-permute-done((bf16[4,256,1024]{2,1,0:T(8,128)(2,1)S(1)}, bf16[4,256,1024]{2,1,0:T(8,128)(2,1)S(1)}, u32[]{:S(2)}, u32[]{:S(2)}) %collective-permute-start.21) | collective-permute-done | bytes 2097184 | tf_op jit(solution)/shard_map/ppermute | solution.py:111
  679.4 9.5 collective-permute-done.22
  695.5 30.3 %collective-permute-done.23 = bf16[1,256,1024]{2,1,0:T(8,128)(2,1)S(1)} collective-permute-done((bf16[1,256,1024]{2,1,0:T(8,128)(2,1)S(1)}, bf16[1,256,1024]{2,1,0:T(8,128)(2,1)S(1)}, u32[]{:S(2)}, u32[]{:S(2)}) %collective-permute-start.23) | collective-permute-done | bytes 524320 | tf_op jit(solution)/shard_map/ppermute | solution.py:111
  736.0 22.7 %collective-permute-done.24 = bf16[1,256,1024]{2,1,0:T(8,128)(2,1)S(1)} collective-permute-done((bf16[1,256,1024]{2,1,0:T(8,128)(2,1)S(1)}, bf16[1,256,1024]{2,1,0:T(8,128)(2,1)S(1)}, u32[]{:S(2)}, u32[]{:S(2)}) %collective-permute-start.24) | collective-permute-done | bytes 524320 | tf_op jit(solution)/shard_map/ppermute | solution.py:111
  758.9 14.8 %collective-permute-done.25 = bf16[2,256,1024]{2,1,0:T(8,128)(2,1)S(1)} collective-permute-done((bf16[2,256,1024]{2,1,0:T(8,128)(2,1)S(1)}, bf16[2,256,1024]{2,1,0:T(8,128)(2,1)S(1)}, u32[]{:S(2)}, u32[]{:S(2)}) %collective-permute-start.25) | collective-permute-done | bytes 1048608 | tf_op jit(solution)/shard_map/ppermute | solution.py:111
  775.0 25.0 %collective-permute-done.26 = bf16[4,256,1024]{2,1,0:T(8,128)(2,1)S(1)} collective-permute-done((bf16[4,256,1024]{2,1,0:T(8,128)(2,1)S(1)}, bf16[4,256,1024]{2,1,0:T(8,128)(2,1)S(1)}, u32[]{:S(2)}, u32[]{:S(2)}) %collective-permute-start.26) | collective-permute-done | bytes 2097184 | tf_op jit(solution)/shard_map/ppermute | solution.py:111
  844.0 8.8 multiply_reduce_fusion
  937.8 14.2 %all-to-all-done.3 = bf16[2,1024,512]{2,0,1:T(2,128)(2,1)S(1)} async-done(((bf16[2,1024,512]{2,0,1:T(2,128)(2,1)}), bf16[2,1024,512]{2,0,1:T(2,128)(2,1)S(1)}, u32[]{:S(2)}, u32[]{:S(2)}) %all-to-all-start.3) | async-done | bytes 2097184 | tf_op jit(solution)/shard_map/all_to_all | solution.py:318
  956.7 9.9 convolution_convert_fusion.10
  966.7 27.2 %reduce-scatter.19.cloned.1.call-done = bf16[128,16]{1,0:T(8,128)(2,1)} async-done(((bf16[2048,16]{1,0:T(8,128)(2,1)}), bf16[128,16]{1,0:T(8,128)(2,1)}) %reduce-scatter.19.cloned.1.call-update) | async-done | bytes 4112
  996.7 21.3 %reduce-scatter.11.cloned.1.call-done = bf16[128,1024]{1,0:T(8,128)(2,1)} async-done(((bf16[128,2048]{1,0:T(8,128)(2,1)}), bf16[128,1024]{1,0:T(8,128)(2,1)}) %reduce-scatter.11.cloned.1.call-update) | async-done | bytes 262160 | tf_op jit(solution)/shard_map/reduce_scatter | solution.py:396
  1035.0 10.5 all-to-all-done.1
  1071.3 13.5 %all-to-all-done = bf16[8,128,384]{2,1,0:T(8,128)(2,1)S(1)} async-done(((bf16[8,128,384]{2,1,0:T(8,128)(2,1)}), bf16[8,128,384]{2,1,0:T(8,128)(2,1)S(1)}, u32[]{:S(2)}, u32[]{:S(2)}) %all-to-all-start) | async-done | bytes 786464 | tf_op jit(solution)/shard_map/all_to_all | solution.py:388
  1096.3 37.3 %all-reduce = (f32[2,2048]{1,0:T(2,128)S(1)}, f32[128]{0:T(128)}, f32[128]{0:T(128)}, f32[3]{0:T(128)S(1)}) all-reduce(f32[2,2048]{1,0:T(2,128)S(1)} %maximum_dynamic-update-slice_fusion, f32[128]{0:T(128)S(1)} %get-tuple-element.20, f32[128]{0:T(128)S(1)} %get-tuple-element.15, ...), channel_id=1, replica_groups=mesh['fsdp'=2,'ctx'=8,'tp'=2] {'fsdp','ctx','tp'}, use_global_device_ids=true, to_apply=%region_26.27 | all-reduce | flops 4355 | bytes 34840 | tf_op jit(solution)/shard_map/psum | solution.py:425
  (517 shorter events, 533.0 us)
Async XLA Ops:
  7.2 112.4 %all-gather.5.cloned.1.call-start = ((), (), s32[]{:S(2)}) async-start(), calls=%async_computation.11 | async-start | bytes 2359296 | tf_op jit(solution)/shard_map/all_gather | solution.py:171
  7.3 27.5 %collective-permute-start = (bf16[1,256,1024]{2,1,0:T(8,128)(2,1)}, bf16[1,256,1024]{2,1,0:T(8,128)(2,1)S(1)}, u32[]{:S(2)}, u32[]{:S(2)}) collective-permute-start(bf16[1,256,1024]{2,1,0:T(8,128)(2,1)} %bitcast.327), channel_id=1, source_target_pairs={{0,8},{1,9},{2,10},{3,11},{4,12},{5,13},{6,14},{7,15},{8,0},{9,1},... | collective-permute-start | bytes 1572872 | tf_op jit(solution)/shard_map/ppermute | solution.py:111
  80.4 26.8 %collective-permute-start.3 = (bf16[8,256,1024]{2,1,0:T(8,128)(2,1)}, bf16[8,256,1024]{2,1,0:T(8,128)(2,1)}, u32[]{:S(2)}, u32[]{:S(2)}) collective-permute-start(bf16[8,256,1024]{2,1,0:T(8,128)(2,1)} %pad_maximum_fusion.6), channel_id=1, source_target_pairs={{0,1},{1,0},{2,3},{3,2},{4,5},{5,4},{6,7},{7,6},{8,9},{9,8},{10,11... | collective-permute-start | bytes 12582920 | tf_op jit(solution)/shard_map/ppermute | solution.py:111
  82.6 335.5 %all-gather.7.cloned.1.call-start = ((), (), s32[]{:S(2)}) async-start(), calls=%async_computation.12 | async-start | bytes 6291456 | tf_op jit(solution)/shard_map/all_gather | solution.py:180
  210.9 27.1 %collective-permute-start.6 = (bf16[2,256,1024]{2,1,0:T(8,128)(2,1)S(1)}, bf16[2,256,1024]{2,1,0:T(8,128)(2,1)S(1)}, u32[]{:S(2)}, u32[]{:S(2)}) collective-permute-start(bf16[2,256,1024]{2,1,0:T(8,128)(2,1)S(1)} %slice.206), channel_id=1, source_target_pairs={{0,4},{1,3},{2,6},{3,1},{4,0},{5,7},{6,2},{7,5},{8,12},{9,11},{10,... | collective-permute-start | bytes 3145736 | tf_op jit(solution)/shard_map/ppermute | solution.py:111
  211.8 38.4 %collective-permute-start.16 = (bf16[1,256,1024]{2,1,0:T(8,128)(2,1)S(1)}, bf16[1,256,1024]{2,1,0:T(8,128)(2,1)}, u32[]{:S(2)}, u32[]{:S(2)}) collective-permute-start(bf16[1,256,1024]{2,1,0:T(8,128)(2,1)S(1)} %bitcast.336), channel_id=1, source_target_pairs={{0,8},{1,9},{2,10},{3,11},{4,12},{5,13},{6,14},{7,15},{8,0},{9,1},... | collective-permute-start | bytes 1572872 | tf_op jit(solution)/shard_map/ppermute | solution.py:111
  242.7 186.1 %all-gather.9.cloned.1.call-start = ((), (), s32[]{:S(2)}) async-start(), calls=%async_computation.13 | async-start | bytes 6291456 | tf_op jit(solution)/shard_map/all_gather | solution.py:180
  252.3 40.1 %collective-permute-start.17 = (bf16[2,256,1024]{2,1,0:T(8,128)(2,1)}, bf16[2,256,1024]{2,1,0:T(8,128)(2,1)}, u32[]{:S(2)}, u32[]{:S(2)}) collective-permute-start(bf16[2,256,1024]{2,1,0:T(8,128)(2,1)} %pad_maximum_fusion.26), channel_id=1, source_target_pairs={{0,4},{1,3},{2,6},{3,1},{4,0},{5,7},{6,2},{7,5},{8,12},{9,11},{10,... | collective-permute-start | bytes 3145736 | tf_op jit(solution)/shard_map/ppermute | solution.py:111
  295.3 32.8 %collective-permute-start.18 = (bf16[4,256,1024]{2,1,0:T(8,128)(2,1)}, bf16[4,256,1024]{2,1,0:T(8,128)(2,1)}, u32[]{:S(2)}, u32[]{:S(2)}) collective-permute-start(bf16[4,256,1024]{2,1,0:T(8,128)(2,1)} %pad_maximum_fusion.19), channel_id=1, source_target_pairs={{0,2},{1,5},{2,0},{3,7},{4,6},{5,1},{6,4},{7,3},{8,10},{9,13},{10,... | collective-permute-start | bytes 6291464 | tf_op jit(solution)/shard_map/ppermute | solution.py:111
  318.4 32.2 %collective-permute-start.10 = (bf16[4,256,1024]{2,1,0:T(8,128)(2,1)}, bf16[4,256,1024]{2,1,0:T(8,128)(2,1)}, u32[]{:S(2)}, u32[]{:S(2)}) collective-permute-start(bf16[4,256,1024]{2,1,0:T(8,128)(2,1)} %pad_maximum_fusion.18), channel_id=1, source_target_pairs={{0,2},{1,5},{2,0},{3,7},{4,6},{5,1},{6,4},{7,3},{8,10},{9,13},{10,... | collective-permute-start | bytes 6291464 | tf_op jit(solution)/shard_map/ppermute | solution.py:111
  321.5 118.0 %all-gather.11.cloned.1.call-start = ((), (), s32[]{:S(2)}) async-start(), calls=%async_computation.14 | async-start | bytes 6291456 | tf_op jit(solution)/shard_map/all_gather | solution.py:180
  332.4 63.1 %collective-permute-start.19 = (bf16[8,256,1024]{2,1,0:T(8,128)(2,1)}, bf16[8,256,1024]{2,1,0:T(8,128)(2,1)}, u32[]{:S(2)}, u32[]{:S(2)}) collective-permute-start(bf16[8,256,1024]{2,1,0:T(8,128)(2,1)} %pad_maximum_fusion.8), channel_id=1, source_target_pairs={{0,1},{1,0},{2,3},{3,2},{4,5},{5,4},{6,7},{7,6},{8,9},{9,8},{10,11... | collective-permute-start | bytes 12582920 | tf_op jit(solution)/shard_map/ppermute | solution.py:111
  354.1 50.4 %collective-permute-start.11 = (bf16[8,256,1024]{2,1,0:T(8,128)(2,1)}, bf16[8,256,1024]{2,1,0:T(8,128)(2,1)}, u32[]{:S(2)}, u32[]{:S(2)}) collective-permute-start(bf16[8,256,1024]{2,1,0:T(8,128)(2,1)} %pad_maximum_fusion.7), channel_id=1, source_target_pairs={{0,1},{1,0},{2,3},{3,2},{4,5},{5,4},{6,7},{7,6},{8,9},{9,8},{10,11... | collective-permute-start | bytes 12582920 | tf_op jit(solution)/shard_map/ppermute | solution.py:111
  358.9 456.0 %reduce-scatter.17.cloned.1.call-start = ((), (), s32[]{:S(2)}) async-start(), calls=%async_computation.19 | async-start | bytes 6291456 | tf_op jit(solution)/shard_map/reduce_scatter | solution.py:315
  513.3 77.9 %collective-permute-start.12 = (bf16[8,256,1024]{2,1,0:T(8,128)(2,1)}, bf16[8,256,1024]{2,1,0:T(8,128)(2,1)}, u32[]{:S(2)}, u32[]{:S(2)}) collective-permute-start(bf16[8,256,1024]{2,1,0:T(8,128)(2,1)} %bitcast.38), channel_id=1, source_target_pairs={{0,1},{1,0},{2,3},{3,2},{4,5},{5,4},{6,7},{7,6},{8,9},{9,8},{10,11... | collective-permute-start | bytes 12582920 | tf_op jit(solution)/shard_map/ppermute | solution.py:111
  573.0 36.7 %collective-permute-start.20 = (bf16[8,256,1024]{2,1,0:T(8,128)(2,1)}, bf16[8,256,1024]{2,1,0:T(8,128)(2,1)}, u32[]{:S(2)}, u32[]{:S(2)}) collective-permute-start(bf16[8,256,1024]{2,1,0:T(8,128)(2,1)} %bitcast.345), channel_id=1, source_target_pairs={{0,1},{1,0},{2,3},{3,2},{4,5},{5,4},{6,7},{7,6},{8,9},{9,8},{10,11... | collective-permute-start | bytes 12582920 | tf_op jit(solution)/shard_map/ppermute | solution.py:111
  590.7 299.1 %reduce-scatter.15.cloned.1.call-start = ((), (), s32[]{:S(2)}) async-start(), calls=%async_computation.18 | async-start | bytes 6291456 | tf_op jit(solution)/shard_map/reduce_scatter | solution.py:315
  628.6 40.8 %collective-permute-start.21 = (bf16[4,256,1024]{2,1,0:T(8,128)(2,1)S(1)}, bf16[4,256,1024]{2,1,0:T(8,128)(2,1)S(1)}, u32[]{:S(2)}, u32[]{:S(2)}) collective-permute-start(bf16[4,256,1024]{2,1,0:T(8,128)(2,1)S(1)} %slice.222), channel_id=1, source_target_pairs={{0,2},{1,5},{2,0},{3,7},{4,6},{5,1},{6,4},{7,3},{8,10},{9,13},{10,... | collective-permute-start | bytes 6291464 | tf_op jit(solution)/shard_map/ppermute | solution.py:111
  636.9 39.9 %collective-permute-start.14 = (bf16[2,256,1024]{2,1,0:T(8,128)(2,1)S(1)}, bf16[2,256,1024]{2,1,0:T(8,128)(2,1)S(1)}, u32[]{:S(2)}, u32[]{:S(2)}) collective-permute-start(bf16[2,256,1024]{2,1,0:T(8,128)(2,1)S(1)} %slice.218), channel_id=1, source_target_pairs={{0,4},{1,3},{2,6},{3,1},{4,0},{5,7},{6,2},{7,5},{8,12},{9,11},{10,... | collective-permute-start | bytes 3145736 | tf_op jit(solution)/shard_map/ppermute | solution.py:111
  678.1 51.4 %collective-permute-start.15 = (bf16[1,256,1024]{2,1,0:T(8,128)(2,1)}, bf16[1,256,1024]{2,1,0:T(8,128)(2,1)}, u32[]{:S(2)}, u32[]{:S(2)}) collective-permute-start(bf16[1,256,1024]{2,1,0:T(8,128)(2,1)} %slice.220), channel_id=1, source_target_pairs={{0,8},{1,9},{2,10},{3,11},{4,12},{5,13},{6,14},{7,15},{8,0},{9,1},... | collective-permute-start | bytes 1572872 | tf_op jit(solution)/shard_map/ppermute | solution.py:111
  689.4 36.3 %collective-permute-start.23 = (bf16[1,256,1024]{2,1,0:T(8,128)(2,1)S(1)}, bf16[1,256,1024]{2,1,0:T(8,128)(2,1)S(1)}, u32[]{:S(2)}, u32[]{:S(2)}) collective-permute-start(bf16[1,256,1024]{2,1,0:T(8,128)(2,1)S(1)} %slice.226), channel_id=1, source_target_pairs={{0,8},{1,9},{2,10},{3,11},{4,12},{5,13},{6,14},{7,15},{8,0},{9,1},... | collective-permute-start | bytes 1572872 | tf_op jit(solution)/shard_map/ppermute | solution.py:111
  736.0 170.3 %reduce-scatter.13.cloned.1.call-start = ((), (), s32[]{:S(2)}) async-start(), calls=%async_computation.17 | async-start | bytes 6291456 | tf_op jit(solution)/shard_map/reduce_scatter | solution.py:315
  820.0 74.9 %all-to-all-start.4 = ((bf16[2,1024,512]{2,0,1:T(2,128)(2,1)}), bf16[2,1024,512]{2,0,1:T(2,128)(2,1)}, u32[]{:S(2)}, u32[]{:S(2)}) async-start(bf16[2,1024,512]{2,0,1:T(2,128)(2,1)} %copy.108), calls=%async_computation.9 | async-start | bytes 4194304 | tf_op jit(solution)/shard_map/all_to_all | solution.py:318
  894.9 57.1 %all-to-all-start.3 = ((bf16[2,1024,512]{2,0,1:T(2,128)(2,1)}), bf16[2,1024,512]{2,0,1:T(2,128)(2,1)S(1)}, u32[]{:S(2)}, u32[]{:S(2)}) async-start(bf16[2,1024,512]{2,0,1:T(2,128)(2,1)} %copy.106), calls=%async_computation.7 | async-start | bytes 4194304 | tf_op jit(solution)/shard_map/all_to_all | solution.py:318
  900.7 93.2 %reduce-scatter.19.cloned.1.call-start = ((), (), s32[]{:S(2)}) async-start(), calls=%async_computation.20 | async-start | bytes 557056
  906.0 111.9 %reduce-scatter.11.cloned.1.call-start = ((), (), s32[]{:S(2)}) async-start(), calls=%async_computation.16 | async-start | bytes 786432 | tf_op jit(solution)/shard_map/reduce_scatter | solution.py:396
  935.8 83.8 %collective-permute-start.29 = (bf16[4,256,1024]{2,1,0:T(8,128)(2,1)}, bf16[4,256,1024]{2,1,0:T(8,128)(2,1)}, u32[]{:S(2)}, u32[]{:S(2)}) collective-permute-start(bf16[4,256,1024]{2,1,0:T(8,128)(2,1)} %slice.232), channel_id=1, source_target_pairs={{0,2},{1,5},{2,0},{3,7},{4,6},{5,1},{6,4},{7,3},{8,10},{9,13},{10,... | collective-permute-start | bytes 6291464 | tf_op jit(solution)/shard_map/ppermute | solution.py:111
  952.0 73.4 %all-to-all-start.2 = ((bf16[2,1024,512]{2,0,1:T(2,128)(2,1)}), bf16[2,1024,512]{2,0,1:T(2,128)(2,1)}, u32[]{:S(2)}, u32[]{:S(2)}) async-start(bf16[2,1024,512]{2,0,1:T(2,128)(2,1)} %copy.104), calls=%async_computation.5 | async-start | bytes 4194304 | tf_op jit(solution)/shard_map/all_to_all | solution.py:318
  956.3 89.9 %reduce-scatter.9.cloned.1.call-start = ((), (), s32[]{:S(2)}) async-start(), calls=%async_computation.15 | async-start | bytes 2359296 | tf_op jit(solution)/shard_map/reduce_scatter | solution.py:383
  1023.9 31.4 %collective-permute-start.30 = (bf16[2,256,1024]{2,1,0:T(8,128)(2,1)}, bf16[2,256,1024]{2,1,0:T(8,128)(2,1)}, u32[]{:S(2)}, u32[]{:S(2)}) collective-permute-start(bf16[2,256,1024]{2,1,0:T(8,128)(2,1)} %slice.234), channel_id=1, source_target_pairs={{0,4},{1,3},{2,6},{3,1},{4,0},{5,7},{6,2},{7,5},{8,12},{9,11},{10,... | collective-permute-start | bytes 3145736 | tf_op jit(solution)/shard_map/ppermute | solution.py:111
  1046.2 38.6 %all-to-all-start = ((bf16[8,128,384]{2,1,0:T(8,128)(2,1)}), bf16[8,128,384]{2,1,0:T(8,128)(2,1)S(1)}, u32[]{:S(2)}, u32[]{:S(2)}) async-start(bf16[8,128,384]{2,1,0:T(8,128)(2,1)} %bitcast.348), calls=%async_computation.1 | async-start | bytes 1572864 | tf_op jit(solution)/shard_map/all_to_all | solution.py:388
  1057.7 37.0 %collective-permute-start.31 = (bf16[1,256,1024]{2,1,0:T(8,128)(2,1)}, bf16[1,256,1024]{2,1,0:T(8,128)(2,1)}, u32[]{:S(2)}, u32[]{:S(2)}) collective-permute-start(bf16[1,256,1024]{2,1,0:T(8,128)(2,1)} %slice.236), channel_id=1, source_target_pairs={{0,8},{1,9},{2,10},{3,11},{4,12},{5,13},{6,14},{7,15},{8,0},{9,1},... | collective-permute-start | bytes 1572872 | tf_op jit(solution)/shard_map/ppermute | solution.py:111
  (145 other events, 2629.4 us)
Sparse Core Ops, SparseCore 0:
  82.7 34.0 all-gather.4
  242.8 57.1 all-gather.6
  321.6 55.4 all-gather.8
  378.5 57.0 all-gather.10
  590.9 52.4 reduce-scatter.16
  736.1 55.3 reduce-scatter.14
  815.0 54.4 reduce-scatter.12
  906.1 87.6 reduce-scatter.18
  996.7 21.1 reduce-scatter.10
  1020.1 26.0 reduce-scatter.8

commit v2 on v1

v2 whole, which is shorter than its diff:
```python
import jax
import jax.numpy as jnp
from jax import lax
from jax.experimental import pallas as pl
from jax.experimental.pallas import tpu as pltpu
from jax.sharding import PartitionSpec as P

norm_eps = 1e-06
rope_base = 10000.0


def locate(pack_spots, lengths_row):
    seq_ends = jnp.cumsum(lengths_row)
    starts = seq_ends - lengths_row
    segment = jnp.sum((pack_spots[:, None] >= seq_ends[None, :]).astype(jnp.int32), axis=1)
    slot_ids = jnp.arange(lengths_row.shape[0], dtype=jnp.int32)
    seq_begin = jnp.sum(
        jnp.where(segment[:, None] == slot_ids[None, :], starts[None, :], 0), axis=1
    )
    return (segment, pack_spots - seq_begin)


def rope_tables(pack_spots, head_dim):
    half_dim = head_dim // 2
    inv_freq = rope_base ** (-(jnp.arange(half_dim, dtype=jnp.float32) * 2.0 / head_dim))
    angle_grid = pack_spots.astype(jnp.float32)[:, None] * inv_freq[None, :]
    cosine, sine = jnp.cos(angle_grid), jnp.sin(angle_grid)
    return jnp.concatenate([cosine, cosine], axis=1), jnp.concatenate([-sine, sine], axis=1)


def unrotate(grad_rot, cosine, sine):
    return grad_rot * cosine + jnp.roll(grad_rot * sine, grad_rot.shape[1] // 2, axis=1)


CHUNKS = 2
MESH_ID = pl.DeviceIdType.MESH
VMEM_LIMIT = 64 * 1000 * 1000


class Pack:
    def __init__(self, ctx_size, tp_size, rows, cols):
        self.line = ctx_size // 2
        self.tp_size, self.rows, self.cols = tp_size, rows, cols
        self.chunk = rows // CHUNKS
        self.steps = self.line * CHUNKS
        place = lax.axis_index("ctx")
        self.a, self.b = place // 2, place % 2
        self.t = lax.axis_index("tp")
        self.has_up, self.has_down = self.a < self.line - 1, self.a > 0

    def up(self):
        return {"ctx": (self.a + 1) * 2 + self.b}

    def down(self):
        return {"ctx": (self.a - 1) * 2 + self.b}

    def pair(self):
        return {"ctx": self.a * 2 + (1 - self.b)}

    def sibling(self, shift):
        return {"tp": self.t ^ shift}

    def meet(self):
        barrier = pltpu.get_barrier_semaphore()

        def greet(device):
            pl.semaphore_signal(barrier, inc=1, device_id=device, device_id_type=MESH_ID)

        @pl.when(self.has_up)
        def _():
            greet(self.up())

        @pl.when(self.has_down)
        def _():
            greet(self.down())

        greet(self.pair())
        for shift in range(1, self.tp_size):
            greet(self.sibling(shift))
        pl.semaphore_wait(
            barrier,
            self.tp_size + jnp.where(self.has_up, 1, 0) + jnp.where(self.has_down, 1, 0),
        )

    def row0(self, block, k):
        return pl.multiple_of(block * self.rows + k * self.chunk, self.chunk)

    def region(self, ref, block, k, part):
        return ref.at[
            pl.ds(self.row0(block, k), self.chunk),
            pl.ds(pl.multiple_of(part * self.cols, self.cols), self.cols),
        ]


def remote(src, dst, send_sem, recv_sem, device):
    return pltpu.make_async_remote_copy(
        src_ref=src,
        dst_ref=dst,
        send_sem=send_sem,
        recv_sem=recv_sem,
        device_id=device,
        device_id_type=MESH_ID,
    )


def loop(count, body):
    lax.fori_loop(0, count, lambda i, carry: (body(i), carry)[1], 0)


def gather_scratch(ctx_size, tp_size, rows, cols, dtype):
    line, dma = ctx_size // 2, pltpu.SemaphoreType.DMA
    return [
        pltpu.VMEM((ctx_size * rows, tp_size * cols), dtype),
        dma((2 * line * CHUNKS,)),
        dma((2 * line * CHUNKS,)),
        dma((4 * line * (tp_size - 1) * CHUNKS,)),
        dma((ctx_size * CHUNKS,)),
        dma(((tp_size - 1) * ctx_size * CHUNKS,)),
        dma,
    ]


def gather_steps(pack, src, scratch, before, compute):
    buf, line_sems, pair_sems, tp_sems, own_sems, sib_sems, local_sem = scratch
    line, t, a, b = pack.line, pack.t, pack.a, pack.b
    ctx_size = 2 * line

    def part(block, k):
        return pack.region(buf, block, k, t)

    def line_copy(piece, block, k, down, dist):
        return remote(
            piece,
            part(block, k),
            line_sems.at[(down * line + dist) * CHUNKS + k],
            own_sems.at[block * CHUNKS + k],
            pack.down() if down else pack.up(),
        )

    def pair_copy(piece, block, k, slot):
        return remote(
            piece,
            part(block, k),
            pair_sems.at[slot * CHUNKS + k],
            own_sems.at[block * CHUNKS + k],
            pack.pair(),
        )

    def tp_copy(piece, block, k, slot, shift):
        return remote(
            piece,
            part(block, k),
            tp_sems.at[(slot * (pack.tp_size - 1) + shift - 1) * CHUNKS + k],
            sib_sems.at[((shift - 1) * ctx_size + block) * CHUNKS + k],
            pack.sibling(shift),
        )

    def send_tp(piece, block, k, slot):
        for shift in range(1, pack.tp_size):
            tp_copy(piece, block, k, slot, shift).start()

    def await_own(block, k):
        piece = part(block, k)
        pair_copy(piece, block, k, 0).wait_recv()

    pack.meet()
    mine = a * 2 + b
    own_copy = pltpu.make_async_copy(
        src,
        buf.at[
            pl.ds(pl.multiple_of(mine * pack.rows, pack.rows), pack.rows),
            pl.ds(pl.multiple_of(t * pack.cols, pack.cols), pack.cols),
        ],
        local_sem,
    )
    own_copy.start()
    for k in range(CHUNKS):
        piece = src.at[pl.ds(k * pack.chunk, pack.chunk), :]

        @pl.when(pack.has_up)
        def _():
            line_copy(piece, mine, k, 0, 0).start()

        @pl.when(pack.has_down)
        def _():
            line_copy(piece, mine, k, 1, 0).start()

        pair_copy(piece, mine, k, 0).start()
    for k in range(CHUNKS):
        send_tp(src.at[pl.ds(k * pack.chunk, pack.chunk), :], mine, k, 0)
    before()
    own_copy.wait()

    def ways(dist):
        below, above = a - dist, a + dist
        return (
            (0, below, below >= 0, jnp.logical_and(below >= 0, pack.has_up)),
            (1, above, above < line, jnp.logical_and(above < line, pack.has_down)),
        )

    def from_line(dist, k):
        for down, node, there, onward in ways(dist):
            block = node * 2 + b

            @pl.when(there)
            def _():
                await_own(block, k)

            @pl.when(onward)
            def _():
                line_copy(part(block, k), block, k, down, dist).start()

            @pl.when(there)
            def _():
                pair_copy(part(block, k), block, k, down * line + dist).start()
                send_tp(part(block, k), block, k, down * line + dist)

    def from_pair(dist, k):
        for down, node, there, _ in ways(dist):
            block = node * 2 + (1 - b)
            if down:
                there = jnp.logical_and(there, dist > 0)

            @pl.when(there)
            def _():
                await_own(block, k)
                send_tp(part(block, k), block, k, (2 + down) * line + dist)

    def work(block, k):
        for shift in range(1, pack.tp_size):
            piece = pack.region(buf, block, k, t ^ shift)
            remote(
                piece,
                piece,
                tp_sems.at[0],
                sib_sems.at[((shift - 1) * ctx_size + block) * CHUNKS + k],
                pack.sibling(shift),
            ).wait_recv()
        compute(pack.row0(block, k), block * CHUNKS + k)

    def step(s):
        dist, k = s // CHUNKS, s % CHUNKS

        @pl.when(dist + 1 < line)
        def _():
            from_line(dist + 1, k)

        @pl.when(s < pack.steps)
        def _():
            from_pair(dist, k)

        def side(i):
            late = s - i
            node, late_k = a ^ (late // CHUNKS), late % CHUNKS

            @pl.when(jnp.logical_and(late >= 0, late < pack.steps))
            def _():
                work(node * 2 + jnp.where(i == 0, b, 1 - b), late_k)

        loop(2, side)

    loop(pack.steps + 1, step)

    def drain(s):
        dist, k = s // CHUNKS, s % CHUNKS
        piece = part(0, 0)
        for down, _, there, onward in ways(dist):

            @pl.when(jnp.logical_and(onward, dist < line - 1))
            def _():
                line_copy(piece, 0, k, down, dist).wait_send()

            if down:
                there = jnp.logical_and(there, dist > 0)

            @pl.when(there)
            def _():
                pair_copy(piece, 0, k, down * line + dist).wait_send()
                for shift in range(1, pack.tp_size):
                    tp_copy(piece, 0, k, down * line + dist, shift).wait_send()
                    tp_copy(piece, 0, k, (2 + down) * line + dist, shift).wait_send()

    loop(pack.steps, drain)


def scatter_scratch(ctx_size, tp_size, rows, cols):
    line, dma = ctx_size // 2, pltpu.SemaphoreType.DMA
    low = jnp.bfloat16
    return [
        pltpu.VMEM((ctx_size * rows, tp_size * cols), low),
        pltpu.VMEM(((tp_size - 1) * ctx_size * rows, cols), low),
        pltpu.VMEM((line * rows, cols), low),
        pltpu.VMEM((2 * line * rows, cols), low),
        dma(((tp_size - 1) * ctx_size * CHUNKS,)),
        dma((line * CHUNKS,)),
        dma((line * CHUNKS,)),
        dma(((tp_size - 1) * ctx_size * CHUNKS,)),
        dma((line * CHUNKS,)),
        dma((2 * line * CHUNKS,)),
    ]


def scatter_steps(pack, scratch, before, compute, finish):
    (full, sib_buf, pair_buf, line_buf, tp_send, pair_send, line_send, tp_recv, pair_recv, line_recv) = scratch
    line, t, a, b = pack.line, pack.t, pack.a, pack.b
    ctx_size = 2 * line
    wide, low = jnp.float32, jnp.bfloat16
    table = [
        sorted(range(line), key=lambda o, node=node: (-abs(o - node), o)) for node in range(line)
    ]

    def owner(i):
        result = jnp.int32(0)
        for node in range(line):
            for place in range(line):
                here = jnp.logical_and(a == node, i == place)
                result = jnp.where(here, table[node][place], result)
        return result

    def tp_copy(block, k, shift):
        return remote(
            pack.region(full, block, k, t ^ shift),
            sib_buf.at[
                pl.ds(pack.row0((shift - 1) * ctx_size + block, k), pack.chunk), :
            ],
            tp_send.at[((shift - 1) * ctx_size + block) * CHUNKS + k],
            tp_recv.at[((shift - 1) * ctx_size + block) * CHUNKS + k],
            pack.sibling(shift),
        )

    def pair_copy(node, k):
        return remote(
            pack.region(full, node * 2 + (1 - b), k, t),
            pair_buf.at[pl.ds(pack.row0(node, k), pack.chunk), :],
            pair_send.at[node * CHUNKS + k],
            pair_recv.at[node * CHUNKS + k],
            pack.pair(),
        )

    def line_copy(node, k, down):
        return remote(
            pack.region(full, node * 2 + b, k, t),
            line_buf.at[pl.ds(pack.row0(down * line + node, k), pack.chunk), :],
            line_send.at[node * CHUNKS + k],
            line_recv.at[(down * line + node) * CHUNKS + k],
            pack.down() if down else pack.up(),
        )

    def own_part(block, k):
        return full[
            pl.ds(pack.row0(block, k), pack.chunk),
            pl.ds(pl.multiple_of(t * pack.cols, pack.cols), pack.cols),
        ].astype(wide)

    def put_part(block, k, value):
        full[
            pl.ds(pack.row0(block, k), pack.chunk),
            pl.ds(pl.multiple_of(t * pack.cols, pack.cols), pack.cols),
        ] = value.astype(low)

    def landed(ref, block, k):
        return ref[pl.ds(pack.row0(block, k), pack.chunk), :].astype(wide)

    def fill(block, k):
        row0 = pack.row0(block, k)
        full[pl.ds(row0, pack.chunk), :] = compute(row0, block * CHUNKS + k)
        for shift in range(1, pack.tp_size):
            tp_copy(block, k, shift).start()

    def join(block, k):
        total = own_part(block, k)
        for shift in range(1, pack.tp_size):
            tp_copy(block, k, shift).wait_recv()
            total = total + landed(sib_buf, (shift - 1) * ctx_size + block, k)
        put_part(block, k, total)

    pack.meet()
    before()

    def step(s):
        @pl.when(s < pack.steps)
        def _():
            node, k = owner(s // CHUNKS), s % CHUNKS

            def side(i):
                fill(node * 2 + jnp.where(i == 0, 1 - b, b), k)

            loop(2, side)

        late = s - 1

        @pl.when(jnp.logical_and(late >= 0, late < pack.steps))
        def _():
            node, k = owner(late // CHUNKS), late % CHUNKS

            def side(i):
                join(node * 2 + jnp.where(i == 0, 1 - b, b), k)

                @pl.when(i == 0)
                def _():
                    pair_copy(node, k).start()

            loop(2, side)

        later = s - 2

        @pl.when(later >= 0)
        def _():
            node, k = owner(later // CHUNKS), later % CHUNKS
            pair_copy(node, k).wait_recv()
            put_part(
                node * 2 + b, k, own_part(node * 2 + b, k) + landed(pair_buf, node, k)
            )
            from_below = jnp.logical_and(pack.has_down, node >= a)
            from_above = jnp.logical_and(pack.has_up, node <= a)
            for down, there in ((0, from_below), (1, from_above)):

                @pl.when(there)
                def _():
                    line_copy(node, k, down).wait_recv()
                    put_part(
                        node * 2 + b,
                        k,
                        own_part(node * 2 + b, k) + landed(line_buf, down * line + node, k),
                    )

            @pl.when(node > a)
            def _():
                line_copy(node, k, 0).start()

            @pl.when(node < a)
            def _():
                line_copy(node, k, 1).start()

            @pl.when(node == a)
            def _():
                finish(k, own_part(node * 2 + b, k))

    loop(pack.steps + 2, step)

    def drain(s):
        node, k = s // CHUNKS, s % CHUNKS
        pair_copy(node, k).wait_send()
        for shift in range(1, pack.tp_size):
            tp_copy(node * 2, k, shift).wait_send()
            tp_copy(node * 2 + 1, k, shift).wait_send()

        @pl.when(node > a)
        def _():
            line_copy(node, k, 0).wait_send()

        @pl.when(node < a)
        def _():
            line_copy(node, k, 1).wait_send()

    loop(pack.steps, drain)


ANY = pl.BlockSpec(memory_space=pl.ANY)


def nn_dot(left, right):
    return lax.dot_general(
        left, right, (((1,), (0,)), ((), ())), preferred_element_type=jnp.float32
    )


def nt_dot(left, right):
    return lax.dot_general(
        left, right, (((1,), (1,)), ((), ())), preferred_element_type=jnp.float32
    )


def pack_gather_call(sizes, tensor, resident, outs, piece, collective_id, keep, flops):
    ctx_size, tp_size = sizes
    rows, cols = tensor.shape
    full = (ctx_size * rows, tp_size * cols)
    count = len(outs)
    pieces = ctx_size * CHUNKS
    dma = pltpu.SemaphoreType.DMA
    base = gather_scratch(ctx_size, tp_size, rows, cols, tensor.dtype)

    def kernel(*refs):
        src, refs = refs[0], refs[1:]
        held_hbm, refs = refs[: len(resident)], refs[len(resident) :]
        out_refs, refs = refs[: count + keep], refs[count + keep :]
        scratch, refs = refs[: len(base)], refs[len(base) :]
        held, refs = refs[: len(resident)], refs[len(resident) :]
        stage, refs = refs[:count], refs[count:]
        held_sem, out_sem = refs
        pack = Pack(ctx_size, tp_size, rows, cols)
        loads = [
            pltpu.make_async_copy(h, v, held_sem.at[i])
            for i, (h, v) in enumerate(zip(held_hbm, held))
        ]

        def before():
            for load in loads:
                load.wait()

        def stores(row0, index):
            window = pl.ds(row0, pack.chunk)
            pairs = list(zip(stage, out_refs))
            if keep:
                pairs.append((scratch[0], out_refs[count]))
            return [
                pltpu.make_async_copy(
                    here.at[window, :], there.at[window, :], out_sem.at[i * pieces + index]
                )
                for i, (here, there) in enumerate(pairs)
            ]

        def compute(row0, index):
            window = pl.ds(row0, pack.chunk)
            for ref, value in zip(stage, piece(scratch[0][window, :], window, held)):
                ref[window, :] = value.astype(ref.dtype)
            for store in stores(row0, index):
                store.start()

        for load in loads:
            load.start()
        gather_steps(pack, src, scratch, before, compute)

        def finish(index):
            for store in stores(pl.multiple_of(index * pack.chunk, pack.chunk), index):
                store.wait()

        loop(pieces, finish)

    shapes = [jax.ShapeDtypeStruct((full[0], width), dtype) for width, dtype in outs]
    if keep:
        shapes.append(jax.ShapeDtypeStruct(full, tensor.dtype))
    return pl.pallas_call(
        kernel,
        out_shape=tuple(shapes),
        in_specs=[ANY] * (1 + len(resident)),
        out_specs=tuple([ANY] * len(shapes)),
        scratch_shapes=base
        + [pltpu.VMEM(r.shape, r.dtype) for r in resident]
        + [pltpu.VMEM((full[0], width), dtype) for width, dtype in outs]
        + [dma((len(resident),)), dma((max(1, len(shapes)) * pieces,))],
        compiler_params=pltpu.CompilerParams(
            collective_id=collective_id, has_side_effects=True, vmem_limit_bytes=VMEM_LIMIT
        ),
        cost_estimate=pl.CostEstimate(
            flops=flops, bytes_accessed=4 * full[0] * full[1] * 2, transcendentals=0
        ),
    )(tensor, *resident)


def pack_scatter_call(sizes, shape, resident, piece, collective_id, flops):
    ctx_size, tp_size = sizes
    rows, cols = shape
    dma = pltpu.SemaphoreType.DMA
    base = scatter_scratch(ctx_size, tp_size, rows, cols)

    def kernel(*refs):
        held_hbm, refs = refs[: len(resident)], refs[len(resident) :]
        out_ref, refs = refs[0], refs[1:]
        scratch, refs = refs[: len(base)], refs[len(base) :]
        held, held_sem = refs[: len(resident)], refs[len(resident)]
        pack = Pack(ctx_size, tp_size, rows, cols)
        loads = [
            pltpu.make_async_copy(h, v, held_sem.at[i])
            for i, (h, v) in enumerate(zip(held_hbm, held))
        ]

        def before():
            for load in loads:
                load.wait()

        def compute(row0, index):
            return piece(pl.ds(row0, pack.chunk), held).astype(jnp.bfloat16)

        def finish(k, total):
            out_ref[pl.ds(pl.multiple_of(k * pack.chunk, pack.chunk), pack.chunk), :] = total

        for load in loads:
            load.start()
        scatter_steps(pack, scratch, before, compute, finish)

    return pl.pallas_call(
        kernel,
        out_shape=jax.ShapeDtypeStruct(shape, jnp.float32),
        in_specs=[ANY] * len(resident),
        out_specs=pl.BlockSpec(memory_space=pltpu.VMEM),
        scratch_shapes=base
        + [pltpu.VMEM(r.shape, r.dtype) for r in resident]
        + [dma((len(resident),))],
        compiler_params=pltpu.CompilerParams(
            collective_id=collective_id, has_side_effects=True, vmem_limit_bytes=VMEM_LIMIT
        ),
        cost_estimate=pl.CostEstimate(
            flops=flops,
            bytes_accessed=4 * ctx_size * rows * tp_size * cols * 2,
            transcendentals=0,
        ),
    )(*resident)


def on_device(
    hidden_in,
    cotangent,
    positions,
    seq_lengths,
    expert_ids,
    attn_norm,
    ffn_norm,
    query_norm,
    key_norm,
    w_query,
    w_key,
    w_value,
    w_out,
    w_router,
    w_gate,
    w_up,
    w_down,
):
    tok_rows, col_count = hidden_in.shape
    ctx_size, tp_size = lax.axis_size("ctx"), lax.axis_size("tp")
    sizes = (ctx_size, tp_size)
    ctx_place, tp_place = lax.axis_index("ctx"), lax.axis_index("tp")
    width_all = col_count * tp_size
    pack_rows = tok_rows * ctx_size
    head_dim = query_norm.shape[0]
    local_heads = w_query.shape[1] // head_dim
    expert_count, hidden_units = w_gate.shape[0], w_gate.shape[2]
    own_experts = expert_count // ctx_size
    sharers = ctx_size // local_heads
    shared_rows = pack_rows // sharers
    score_scale = head_dim ** (-0.5)
    wide = jnp.float32
    slim = jnp.bfloat16
    lanes = 128

    def row_total(tensor):
        return lax.psum(tensor, "tp")

    def dot(left, right, dims):
        return lax.dot_general(
            left, right, ((dims[:1], dims[1:]), ((), ())), preferred_element_type=wide
        )

    head_place = ctx_place % local_heads

    def head_slice(weight, axis):
        return lax.dynamic_slice_in_dim(weight, head_place * head_dim, head_dim, axis)

    def expert_slice(weight):
        return lax.dynamic_slice_in_dim(weight, ctx_place * own_experts, own_experts, 0)

    qkv_weight = lax.all_gather(
        jnp.concatenate([head_slice(w, 1) for w in (w_query, w_key, w_value)], axis=1),
        "fsdp",
        axis=0,
        tiled=True,
    )
    out_weight = lax.all_gather(head_slice(w_out, 0), "fsdp", axis=1, tiled=True)
    router_full = lax.all_gather(w_router, "fsdp", axis=1, tiled=True)
    router_pad = jnp.pad(router_full, ((0, lanes - expert_count), (0, 0)))
    gate_weight, up_weight, down_weight = (
        lax.all_gather(expert_slice(w), "fsdp", axis=1, tiled=True)
        for w in (w_gate, w_up, w_down)
    )
    gain_first_all = lax.all_gather(attn_norm, "tp", axis=0, tiled=True).astype(wide)[None, :]

    segment, place = locate(positions[0], seq_lengths[0])
    cosine, sine = rope_tables(place, head_dim)
    ids_all = lax.all_gather(expert_ids, "ctx", axis=0, tiled=True)
    chosen = jnp.sum(
        (ids_all[:, :, None] == jnp.arange(lanes, dtype=jnp.int32)[None, None, :]).astype(wide),
        axis=1,
    ).astype(slim)

    share = ctx_place // local_heads

    def query_rows(tensor):
        if sharers == 1:
            return tensor
        return lax.dynamic_slice_in_dim(tensor, share * shared_rows, shared_rows, 0)

    def all_rows(tensor):
        if sharers == 1:
            return tensor
        return lax.dynamic_update_slice_in_dim(
            jnp.zeros((pack_rows,) + tensor.shape[1:], tensor.dtype),
            tensor,
            share * shared_rows,
            0,
        )

    def project(rows, window, held):
        weight, gain, cos_table, sin_table, gain_q, gain_k = held
        hidden = rows.astype(wide)
        inverse = lax.rsqrt(jnp.mean(hidden * hidden, axis=1, keepdims=True) + norm_eps)
        normed = (hidden * inverse * gain[...]).astype(slim)
        raw = nn_dot(normed, weight[...])
        cos_rows, sin_rows = cos_table[window, :], sin_table[window, :]

        def prepare(raw_proj, gain_vec):
            inv = lax.rsqrt(jnp.mean(raw_proj * raw_proj, axis=1, keepdims=True) + norm_eps)
            scaled = raw_proj * inv * gain_vec[...]
            return scaled * cos_rows + pltpu.roll(scaled, head_dim // 2, 1) * sin_rows

        query_raw = raw[:, :head_dim]
        key_raw = raw[:, head_dim : 2 * head_dim]
        return (
            normed,
            jnp.broadcast_to(inverse, (rows.shape[0], lanes)),
            query_raw,
            key_raw,
            prepare(query_raw, gain_q),
            prepare(key_raw, gain_k),
            raw[:, 2 * head_dim :],
        )

    gain_query = query_norm.astype(wide)[None, :]
    gain_key = key_norm.astype(wide)[None, :]
    normed_first, inv_all, query_raw, key_raw, query_low, key_low, value_low = pack_gather_call(
        sizes,
        hidden_in,
        (qkv_weight, gain_first_all, cosine, sine, gain_query, gain_key),
        (
            (width_all, slim),
            (lanes, wide),
            (head_dim, wide),
            (head_dim, wide),
            (head_dim, slim),
            (head_dim, slim),
            (head_dim, slim),
        ),
        project,
        1,
        False,
        6 * pack_rows * width_all * head_dim,
    )
    (cotangent_all,) = pack_gather_call(
        sizes, cotangent, (gain_query,), (), lambda rows, window, held: (), 2, True, 0
    )

    query_raw, query_low = query_rows(query_raw), query_rows(query_low)
    query_turn = (query_rows(cosine), query_rows(sine))
    same_seq = query_rows(segment)[:, None] == segment[None, :]

    def scores_of():
        return jnp.where(same_seq, dot(query_low, key_low, (1, 1)) * score_scale, -1e30)

    scores = scores_of()
    row_peak = jnp.max(scores, axis=1, keepdims=True)
    row_exp = jnp.exp(scores - row_peak)
    row_sum = jnp.sum(row_exp, axis=1, keepdims=True)
    log_total = row_peak + jnp.log(row_sum)
    probs_low = (row_exp / row_sum).astype(slim)
    attended_low = all_rows(dot(probs_low, value_low, (1, 0)).astype(slim))
    attn_branch = pack_scatter_call(
        sizes,
        (tok_rows, col_count),
        (attended_low, out_weight),
        lambda window, held: nn_dot(held[0][window, :], held[1][...]),
        3,
        2 * pack_rows * width_all * head_dim,
    )

    resid_in = hidden_in.astype(wide)
    middle = resid_in + attn_branch
    gain_second = ffn_norm.astype(wide)
    inv_second = lax.rsqrt(row_total(jnp.sum(middle * middle, axis=1)) / width_all + norm_eps)[
        :, None
    ]

    def experts(rows, window, held):
        gate_w, up_w, down_w, router_w, chosen_ref, cotangent_ref = held
        lane = lax.broadcasted_iota(jnp.int32, (rows.shape[0], lanes), 1)
        logits = jnp.where(lane < expert_count, nt_dot(rows, router_w[...]), -1e30)
        logit_exp = jnp.exp(logits - jnp.max(logits, axis=1, keepdims=True))
        route_probs = logit_exp / jnp.sum(logit_exp, axis=1, keepdims=True)
        gate_weights = route_probs * chosen_ref[window, :].astype(wide)
        first_expert = lax.axis_index("ctx") * own_experts
        rows_grad = cotangent_ref[window, :]
        grad_logits = jnp.zeros((rows.shape[0], lanes), wide)
        mixed_list, gate_list, up_list = [], [], []
        for slot in range(own_experts):
            mine = (lane == first_expert + slot).astype(wide)
            gates = jnp.sum(gate_weights * mine, axis=1, keepdims=True)
            gate_proj = nn_dot(rows, gate_w[slot])
            up_proj = nn_dot(rows, up_w[slot])
            grad_mixed = nn_dot(rows_grad, down_w[slot]).astype(slim).astype(wide)
            gate_sigmoid = jax.nn.sigmoid(gate_proj)
            silu = gate_proj * gate_sigmoid
            activity = silu * up_proj
            mixed_list.append((gates * activity).astype(slim))
            grad_gates = jnp.sum(grad_mixed * activity, axis=1, keepdims=True)
            grad_activity = grad_mixed * gates
            gate_list.append(
                (
                    grad_activity * up_proj * (gate_sigmoid + silu * (1.0 - gate_sigmoid))
                ).astype(slim)
            )
            up_list.append((grad_activity * silu).astype(slim))
            grad_logits = grad_logits + gates * grad_gates * (mine - route_probs)
        return (
            jnp.concatenate(mixed_list, axis=1),
            jnp.concatenate(gate_list, axis=1),
            jnp.concatenate(up_list, axis=1),
            grad_logits,
        )

    own_units = own_experts * hidden_units
    mixed_low, grad_gate_low, grad_up_low, grad_logits_low, normed_second = pack_gather_call(
        sizes,
        (middle * inv_second * gain_second).astype(slim),
        (gate_weight, up_weight, down_weight, router_pad, chosen, cotangent_all),
        ((own_units, slim), (own_units, slim), (own_units, slim), (lanes, slim)),
        experts,
        4,
        True,
        6 * pack_rows * width_all * own_units,
    )

    def back(window, held):
        gate_grad, up_grad, logit_grad, gate_w, up_w, router_w = held
        total = nn_dot(logit_grad[window, :], router_w[...])
        for slot in range(own_experts):
            units = pl.ds(slot * hidden_units, hidden_units)
            total = total + nt_dot(gate_grad[window, units], gate_w[slot])
            total = total + nt_dot(up_grad[window, units], up_w[slot])
        return total

    grad_second = pack_scatter_call(
        sizes,
        (tok_rows, col_count),
        (grad_gate_low, grad_up_low, grad_logits_low, gate_weight, up_weight, router_pad),
        back,
        5,
        4 * pack_rows * width_all * own_units,
    )

    def units_of(tensor, slot):
        return tensor[:, slot * hidden_units : (slot + 1) * hidden_units]

    def spread_experts(left, right):
        parts = jnp.stack(
            [dot(left, units_of(right, slot), (0, 0)).astype(slim) for slot in range(own_experts)]
        )
        mine = lax.psum_scatter(parts, "fsdp", scatter_dimension=1, tiled=True)
        return lax.all_to_all(mine, "ctx", split_axis=1, concat_axis=0, tiled=True).astype(wide)

    grad_gate = spread_experts(normed_second, grad_gate_low)
    grad_up = spread_experts(normed_second, grad_up_low)
    grad_down = spread_experts(cotangent_all, mixed_low)
    grad_router = row_total(
        lax.psum_scatter(
            dot(grad_logits_low[:, :expert_count], normed_second, (0, 0)).astype(slim),
            ("fsdp", "ctx"),
            scatter_dimension=1,
            tiled=True,
        ).astype(wide)
    )

    gain_two_grad = jnp.sum(grad_second * middle * inv_second, axis=0)
    second_scaled = grad_second * gain_second
    second_inner = row_total(jnp.sum(second_scaled * middle, axis=1))[:, None]
    grad_middle = (
        cotangent.astype(wide)
        + inv_second * second_scaled
        - middle * inv_second**3 * second_inner / width_all
    )

    grad_attended, grad_middle_all = pack_gather_call(
        sizes,
        grad_middle.astype(slim),
        (out_weight,),
        ((head_dim, slim),),
        lambda rows, window, held: (nt_dot(rows, held[0][...]),),
        6,
        True,
        2 * pack_rows * width_all * head_dim,
    )
    grad_out_part = dot(attended_low, grad_middle_all, (0, 0))
    probs_back = jnp.exp(scores_of() - log_total)
    grad_att_rows = query_rows(grad_attended)
    grad_probs = dot(grad_att_rows, value_low, (1, 1))
    grad_scores = (
        probs_back * (grad_probs - jnp.sum(probs_back * grad_probs, axis=1, keepdims=True))
    ).astype(slim)
    grad_query_rot = dot(grad_scores, key_low, (1, 0)) * score_scale
    grad_key_rot = dot(grad_scores, query_low, (0, 0)) * score_scale
    grad_value_low = dot(probs_back.astype(slim), grad_att_rows, (0, 0)).astype(slim)

    expert_branch = pack_scatter_call(
        sizes,
        (tok_rows, col_count),
        (mixed_low, down_weight),
        lambda window, held: sum(
            nt_dot(held[0][window, pl.ds(slot * hidden_units, hidden_units)], held[1][slot])
            for slot in range(own_experts)
        ),
        7,
        2 * pack_rows * width_all * own_units,
    )
    hidden_out = (middle + expert_branch).astype(slim)

    def prepare_back(grad_rot, raw_proj, gain_vec, turn):
        inverse = lax.rsqrt(jnp.mean(raw_proj * raw_proj, axis=1, keepdims=True) + norm_eps)
        grad_normed = unrotate(grad_rot, *turn)
        weighted = grad_normed * gain_vec
        grad_raw = inverse * weighted - raw_proj * inverse**3 * jnp.mean(
            weighted * raw_proj, axis=1, keepdims=True
        )
        gain_grad = jnp.sum(grad_normed * raw_proj * inverse, axis=0)
        return grad_raw.astype(slim), gain_grad

    grad_query_low, query_gain_grad = prepare_back(
        grad_query_rot, query_raw, gain_query, query_turn
    )
    grad_key_low, key_gain_grad = prepare_back(grad_key_rot, key_raw, gain_key, (cosine, sine))
    grad_qkv_low = jnp.concatenate(
        [all_rows(grad_query_low), grad_key_low, grad_value_low], axis=1
    )
    grad_first = pack_scatter_call(
        sizes,
        (tok_rows, col_count),
        (grad_qkv_low, qkv_weight),
        lambda window, held: nt_dot(held[0][window, :], held[1][...]),
        8,
        6 * pack_rows * width_all * head_dim,
    )
    grad_qkv_part = dot(normed_first, grad_qkv_low, (0, 0))

    def over_sharers(tensor):
        if sharers == 1:
            return tensor.astype(wide)
        return jnp.sum(
            tensor.reshape((sharers, local_heads) + tensor.shape[1:]).astype(wide), axis=0
        )

    qkv_mine = lax.psum_scatter(
        grad_qkv_part.astype(slim), "fsdp", scatter_dimension=0, tiled=True
    )
    qkv_rows = qkv_mine.shape[0] // ctx_size
    qkv_mine = over_sharers(
        lax.all_to_all(
            qkv_mine.reshape(ctx_size, qkv_rows, 3 * head_dim), "ctx", split_axis=0, concat_axis=0
        )
    )
    grad_query, grad_key, grad_value = (
        jnp.swapaxes(qkv_mine[:, :, i * head_dim : (i + 1) * head_dim], 0, 1).reshape(qkv_rows, -1)
        for i in range(3)
    )
    out_mine = lax.psum_scatter(
        grad_out_part.astype(slim), "fsdp", scatter_dimension=1, tiled=True
    )
    out_cols = out_mine.shape[1] // ctx_size
    out_mine = jnp.swapaxes(out_mine.reshape(head_dim, ctx_size, out_cols), 0, 1)
    grad_out = over_sharers(
        lax.all_to_all(out_mine, "ctx", split_axis=0, concat_axis=0)
    ).reshape(-1, out_cols)

    gain_first = attn_norm.astype(wide)
    inv_first = lax.dynamic_slice_in_dim(inv_all, ctx_place * tok_rows, tok_rows, 0)[:, :1]
    gain_one_grad = jnp.sum(grad_first * resid_in * inv_first, axis=0)
    first_scaled = grad_first * gain_first
    first_inner = row_total(jnp.sum(first_scaled * resid_in, axis=1))[:, None]
    grad_hidden = (
        grad_middle + inv_first * first_scaled - resid_in * inv_first**3 * first_inner / width_all
    )
    gains_part = lax.dynamic_update_slice(
        jnp.zeros((2, width_all), wide),
        jnp.stack([gain_one_grad, gain_two_grad]),
        (0, tp_place * col_count),
    )
    stream_part = jnp.stack(
        [
            jnp.sum(middle * middle),
            jnp.sum(attn_branch * attn_branch),
            jnp.sum(expert_branch * expert_branch),
        ]
    )
    stream_sums, gains_sum, query_gain_sum, key_gain_sum = lax.psum(
        (stream_part, gains_part, query_gain_grad, key_gain_grad), ("fsdp", "ctx", "tp")
    )
    token_count = tok_rows * lax.axis_size("fsdp") * ctx_size
    stream_rms = jnp.sqrt(stream_sums / (token_count * width_all))
    return (
        hidden_out,
        grad_hidden,
        gains_sum[0],
        gains_sum[1],
        query_gain_sum,
        key_gain_sum,
        grad_query,
        grad_key,
        grad_value,
        grad_out,
        grad_router,
        grad_gate,
        grad_up,
        grad_down,
        stream_rms,
    )


def solution(mesh):
    return jax.shard_map(
        on_device,
        mesh=mesh,
        in_specs=(
            P(("fsdp", "ctx"), "tp"),
            P(("fsdp", "ctx"), "tp"),
            P("fsdp", None),
            P("fsdp", None),
            P(("fsdp", "ctx"), None),
            P("tp"),
            P("tp"),
            P(),
            P(),
            P("fsdp", "tp"),
            P("fsdp", "tp"),
            P("fsdp", "tp"),
            P("tp", "fsdp"),
            P(None, "fsdp"),
            P(None, "fsdp", "tp"),
            P(None, "fsdp", "tp"),
            P(None, "fsdp", "tp"),
        ),
        out_specs=(
            P(("fsdp", "ctx"), "tp"),
            P(("fsdp", "ctx"), "tp"),
            P(),
            P(),
            P(),
            P(),
            P(("fsdp", "ctx"), "tp"),
            P(("fsdp", "ctx"), "tp"),
            P(("fsdp", "ctx"), "tp"),
            P("tp", ("fsdp", "ctx")),
            P(None, ("fsdp", "ctx")),
            P(None, ("fsdp", "ctx"), "tp"),
            P(None, ("fsdp", "ctx"), "tp"),
            P(None, ("fsdp", "ctx"), "tp"),
            P(),
        ),
        check_vma=False,
    )
```

time: 1160 us -> 989 us (0.85)
  Pallas kernels: 0 us -> 495 us
  waiting for transfers between devices: 437 us -> 94.9 us
  matrix products: 258 us -> 110 us
  other arithmetic: 162 us -> 87.4 us
  local copies, waits for them, and re-layouts: 119 us -> 47.2 us
  starting transfers between devices: 55.1 us -> 30.4 us
    pallas_call x0 -> x8, Pallas kernels: none -> 495 us  [the longest x4 268 us: pack_scatter_call(): pl.pallas_call(kernel, out_shape=jax.ShapeDtypeStruct(shape, jnp.float32)...]
    ppermute x32 -> x0, waiting for transfers between devices: 349 us -> none  [move(): return lax.ppermute(tensor, ('fsdp', 'ctx', 'tp'), pairs)]
    dot_general x27 -> x15, matrix products: 223 us -> 110 us  [dot(): lax.dot_general(left, right, ((dims[:1], dims[1:]), ((), ())), preferred_...]
    reduce_scatter x3, waiting for transfers between devices: 0.04 us -> 90.9 us  [spread_experts(): mine = lax.psum_scatter(parts, 'fsdp', scatter_dimension=1, tiled=True)]
    convert_element_type x23 -> x4, other arithmetic: 58.3 us -> 3.44 us  [the longest x2 1.96 us: prepare_back(): return (grad_raw.astype(slim), gain_grad)]
    dot_general x6 -> x0, matrix products: 35.1 us -> none  [the longest x1 8.78 us: on_device(): jnp.einsum('qhd,khd->hqk', grad_att_heads, value_low, preferred_element_t...]
    ppermute x32 -> x0, starting transfers between devices: 28.5 us -> none  [move(): return lax.ppermute(tensor, ('fsdp', 'ctx', 'tp'), pairs)]
    unnamed x11, waiting for transfers between devices: 27.4 us -> 0.17 us
  transfers between devices with their start and end apart: 47 -> 15, of which waited for: 26 -> 4; matrix products, arithmetic and copies ran while one was open for 34% -> 21% of each run, Pallas kernels for 0% -> 24%
where the time goes in v2:
time: 989 us; the launch traced here: 988 us
  Pallas kernels  495 us (50%)
  matrix products  110 us (11%)
  blocking collectives  108 us (11%)
  waiting for transfers between devices  94.9 us (10%)
  other arithmetic  87.4 us (9%)
  local copies, waits for them, and re-layouts  47.2 us (5%)
  starting transfers between devices  30.4 us (3%)
  between operations  15.1 us (2%)
    pallas_call x4, Pallas kernels, pack_scatter_call(): pl.pallas_call(kernel, out_shape=jax.ShapeDtypeStruct(shape, jnp.float32)...  268 us
    pallas_call x4, Pallas kernels, pack_gather_call(): pl.pallas_call(kernel, out_shape=tuple(shapes), in_specs=[ANY] * (1 + len...  226 us
    dot_general x15, matrix products, dot(): lax.dot_general(left, right, ((dims[:1], dims[1:]), ((), ())), preferred_...  110 us
    reduce_scatter x3, waiting for transfers between devices, spread_experts(): mine = lax.psum_scatter(parts, 'fsdp', scatter_dimension=1, tiled=True)  90.9 us
    psum x1, blocking collectives, on_device(): lax.psum((stream_part, gains_part, query_gain_grad, key_gain_grad), ('fsd...  47.6 us
    all_gather x1, blocking collectives, on_device(): ids_all = lax.all_gather(expert_ids, 'ctx', axis=0, tiled=True)  32.3 us
  transfers between devices with their start and end apart: 15, of which 4 were waited for; matrix products, arithmetic and copies ran while one was open for 21% of the time, Pallas kernels for 24%

profile of v2, /device:TPU:0, one launch (start us, length us, event | category | flops | bytes accessed | tf_op | source)
XLA Modules:
  0.0 988.1 jit_solution(11135146329276316065)
XLA Ops:
  23.4 32.3 %all_gather.31 = s32[2048,8]{0,1:T(8,128)S(1)} all-gather(s32[256,8]{0,1:T(8,128)S(1)} %copy-done.23), channel_id=1, replica_groups=mesh['fsdp'=2,'ctx'=8,'tp'=2] {'ctx'}, dimensions={0}, use_global_device_ids=true | all-gather | bytes 73728 | tf_op jit(solution)/shard_map/all_gather | solution.py:670
  55.7 5.6 all_gather.30
  62.3 12.7 %all_gather.26.refs_1_ = bf16[128,2048]{1,0:T(8,128)(2,1)} all-gather(bf16[128,1024]{1,0:T(8,128)(2,1)S(1)} %constant_dynamic-slice_fusion.3), channel_id=1, replica_groups=mesh['fsdp'=2,'ctx'=8,'tp'=2] {'fsdp'}, dimensions={1}, use_global_device_ids=true | all-gather | bytes 786432 | tf_op jit(solution)/shard_map/all_gather | solution.py:659
  75.3 12.2 %convert_reduce_fusion.refs_5_ = bf16[2048,128]{1,0:T(8,128)(2,1)} fusion(s32[2048,8]{1,0:T(8,128)S(1)} %copy.68), kind=kLoop, calls=%fused_computation.10 | loop fusion | flops 6029312 | bytes 589824 | tf_op jit(solution)/shard_map/reduce_sum | solution.py:671
  94.3 50.5 %shard_map.282.refs_6_ = bf16[2048,2048]{1,0:T(8,128)(2,1)} custom-call(bf16[256,1024]{1,0:T(8,128)(2,1)} %refs_0_.3, f32[1,128]{1,0:T(1,128)} %get-tuple-element.95.refs_5_.refs_1_), custom_call_target="tpu_custom_call" | custom-call | bytes 33554432 | tf_op jit(solution)/shard_map/pallas_call | solution.py:533
  147.9 54.0 %shard_map.280 = (bf16[2048,2048]{1,0:T(8,128)(2,1)}, f32[2048,128]{1,0:T(8,128)}, f32[2048,128]{1,0:T(8,128)}, f32[2048,128]{1,0:T(8,128)}, bf16[2048,128]{1,0:...) custom-call(bf16[256,1024]{1,0:T(8,128)(2,1)} %refs_0_.2, ...), custom_call_target="tpu_custom_call" | custom-call | flops 3221225472 | bytes 33554432 | tf_op jit(solution)/shard_map/pallas_call | solution.py:533
  202.0 8.2 fusion.39
  210.1 8.1 fusion
  218.3 9.5 fusion.15.refs_0_
  227.7 54.6 %shard_map.281 = f32[256,1024]{1,0:T(8,128)} custom-call(bf16[2048,128]{1,0:T(8,128)(2,1)} %fusion.15.refs_0_, bf16[128,2048]{1,0:T(8,128)(2,1)} %all_gather.26.refs_1_), custom_call_target="tpu_custom_call" | custom-call | flops 1073741824 | bytes 33554432 | tf_op jit(solution)/shard_map/pallas_call | solution.py:582
  289.9 69.0 %shard_map.283 = (bf16[2048,1024]{1,0:T(8,128)(2,1)}, bf16[2048,1024]{1,0:T(8,128)(2,1)}, bf16[2048,1024]{1,0:T(8,128)(2,1)}, bf16[2048,128]{1,0:T(8,128)(2,1)}, bf16[2048,2048]{1,0:T(8,128)(2,1)}) custom-call(bf16[256,1024]{1,0:T(8,128)(2,1)} %multiply_convert_fusion.1.refs_0_, bf16[2,2048,512]{2,1,0:T(8,128)(2,1)} %all-gather.7.cloned.1.call-done.refs_1_.refs_3_, ...), custom_call_target="tpu_custom_call" | custom-call | flops 25769803776 | bytes 33554432 | tf_op jit(solution)/shard_map/pallas_call | solution.py:533
  358.9 75.5 %shard_map.285 = f32[256,1024]{1,0:T(8,128)} custom-call(bf16[2048,1024]{1,0:T(8,128)(2,1)} %get-tuple-element.33.refs_0_, bf16[2048,1024]{1,0:T(8,128)(2,1)} %get-tuple-element.34.refs_1_, bf16[2048,128]{1,0:T(8,128)(2,1)} %get-tuple-element.35.refs_2_, bf16[2,2048,512]{2,1,0:T(8,128)(2,1)} %all-gather.7.cloned.1.call-done.refs_1_.refs_3_, ...), custom_call_target="tpu_custom_call" | custom-call | flops 17179869184 | bytes 33554432 | tf_op jit(solution)/shard_map/pallas_call | solution.py:582
  439.1 61.4 %shard_map.284 = f32[256,1024]{1,0:T(8,128)} custom-call(bf16[2048,1024]{1,0:T(8,128)(2,1)} %get-tuple-element.32.refs_0_, bf16[2,2048,512]{2,1,0:T(8,128)(2,1)} %all-gather.11.cloned.1.call-done.refs_3_.refs_1_), custom_call_target="tpu_custom_call" | custom-call | flops 8589934592 | bytes 33554432 | tf_op jit(solution)/shard_map/pallas_call | solution.py:582
  504.2 52.8 %shard_map.286 = (bf16[2048,128]{1,0:T(8,128)(2,1)}, bf16[2048,2048]{1,0:T(8,128)(2,1)}) custom-call(bf16[256,1024]{1,0:T(8,128)(2,1)} %get-tuple-element.72.refs_0_, bf16[128,2048]{1,0:T(8,128)(2,1)} %all_gather.26.refs_1_), custom_call_target="tpu_custom_call" | custom-call | flops 1073741824 | bytes 33554432 | tf_op jit(solution)/shard_map/pallas_call | solution.py:533
  557.1 8.5 fusion.12
  565.7 11.7 %multiply_reduce_fusion = (f32[2048]{0:T(1024)S(1)}, f32[2048,2048]{0,1:T(8,128)}) fusion(f32[2048,2048]{0,1:T(8,128)} %get-tuple-element.99, f32[2048]{0:T(1024)S(1)} %log_add_fusion, bf16[2048,128]{1,0:T(8,128)(2,1)S(1)} %copy-done.11, bf16[2048,128]{1,0:T(8,128)(2,1)S(1)} %copy-done.18), kind=kOutput, calls=%fused_computation.1 | convolution fusion | flops 1086322688 | bytes 34619392 | tf_op jit(solution)/shard_map/dot_general | solution.py:641
  579.8 12.4 %multiply_convert_fusion = bf16[2048,2048]{0,1:T(8,128)(2,1)S(1)} fusion(f32[2048,2048]{0,1:T(8,128)} %get-tuple-element.101, f32[2048,2048]{0,1:T(8,128)} %get-tuple-element.99, f32[2048]{0:T(1024)S(1)} %get-tuple-element.100, f32[2048]{0:T(1024)S(1)} %log_add_fusion), kind=kLoop, calls=%fused_computation | loop fusion | flops 16777216 | bytes 41959424 | tf_op jit(solution)/shard_map/convert_element_type | solution.py:886
  603.4 5.7 convolution_convert_fusion.6
  609.5 8.7 fusion.11
  618.3 9.0 fusion.10
  629.9 8.8 fusion.7
  638.7 8.5 fusion.6
  649.6 9.8 fusion.9
  661.2 8.1 all-to-all-start.1
  669.3 9.9 fusion.8
  679.2 6.0 all-to-all-start
  689.9 6.7 reduce-scatter.17.cloned.1.call-done
  710.1 43.8 %reduce-scatter.13.cloned.1.call-done = bf16[2,1024,512]{2,1,0:T(8,128)(2,1)} async-done(((bf16[2,2048,512]{2,1,0:T(8,128)(2,1)}), bf16[2,1024,512]{2,1,0:T(8,128)(2,1)}) %reduce-scatter.13.cloned.1.call-update) | async-done | bytes 2097168 | tf_op jit(solution)/shard_map/reduce_scatter | solution.py:846
  759.0 6.0 all-to-all-start.2
  770.8 40.3 %reduce-scatter.15.cloned.1.call-done = bf16[2,1024,512]{2,1,0:T(8,128)(2,1)} async-done(((bf16[2,2048,512]{2,1,0:T(8,128)(2,1)}), bf16[2,1024,512]{2,1,0:T(8,128)(2,1)}) %reduce-scatter.15.cloned.1.call-update) | async-done | bytes 2097168 | tf_op jit(solution)/shard_map/reduce_scatter | solution.py:846
  827.2 76.8 %shard_map.287 = f32[256,1024]{1,0:T(8,128)} custom-call(bf16[2048,384]{1,0:T(8,128)(2,1)} %pad_maximum_fusion.3.refs_0_, bf16[2048,384]{1,0:T(8,128)(2,1)} %all-gather.5.cloned.1.call-done.refs_1_), custom_call_target="tpu_custom_call" | custom-call | flops 3221225472 | bytes 33554432 | tf_op jit(solution)/shard_map/pallas_call | solution.py:582
  905.6 47.6 %all-reduce.1 = (f32[2,2048]{1,0:T(2,128)S(1)}, f32[128]{0:T(128)}, f32[128]{0:T(128)}, f32[3]{0:T(128)S(1)}) all-reduce(f32[2,2048]{1,0:T(2,128)S(1)} %maximum_dynamic-update-slice_fusion, f32[128]{0:T(128)S(1)} %get-tuple-element.45, f32[128]{0:T(128)S(1)} %get-tuple-element.75, ...), channel_id=1, replica_groups=mesh['fsdp'=2,'ctx'=8,'tp'=2] {'fsdp','ctx','tp'}, use_global_device_ids=true, to_apply=%region_19.20 | all-reduce | flops 4355 | bytes 34840 | tf_op jit(solution)/shard_map/psum | solution.py:980
  (190 shorter events, 138.3 us)
Async XLA Ops:
  7.2 140.7 %all-gather.5.cloned.1.call-start = ((), (), s32[]{:S(2)}) async-start(), calls=%async_computation.11 | async-start | bytes 2359296 | tf_op jit(solution)/shard_map/all_gather | solution.py:653
  11.0 278.9 %all-gather.7.cloned.1.call-start = ((), (), s32[]{:S(2)}) async-start(), calls=%async_computation.12 | async-start | bytes 6291456 | tf_op jit(solution)/shard_map/all_gather | solution.py:663
  14.1 275.8 %all-gather.9.cloned.1.call-start = ((), (), s32[]{:S(2)}) async-start(), calls=%async_computation.13 | async-start | bytes 6291456 | tf_op jit(solution)/shard_map/all_gather | solution.py:663
  17.2 38.5 %copy-start.20 = (bf16[16,1024]{1,0:T(8,128)(2,1)S(1)}, bf16[16,1024]{1,0:T(8,128)(2,1)}, u32[]{:S(2)}) copy-start(bf16[16,1024]{1,0:T(8,128)(2,1)} %param.30) | copy-start | bytes 98308
  17.2 272.6 %all-gather.11.cloned.1.call-start = ((), (), s32[]{:S(2)}) async-start(), calls=%async_computation.14 | async-start | bytes 6291456 | tf_op jit(solution)/shard_map/all_gather | solution.py:663
  20.3 67.2 %copy-start.29 = (bf16[128]{0:T(256)(128)(2,1)S(1)}, bf16[128]{0:T(256)(128)(2,1)}, u32[]{:S(2)}) copy-start(bf16[128]{0:T(256)(128)(2,1)} %param.24) | copy-start | bytes 772
  20.3 67.2 %copy-start.30 = (bf16[128]{0:T(256)(128)(2,1)S(1)}, bf16[128]{0:T(256)(128)(2,1)}, u32[]{:S(2)}) copy-start(bf16[128]{0:T(256)(128)(2,1)} %param.25) | copy-start | bytes 772
  20.4 639.1 %reduce-scatter.11.cloned.1.call-start = ((), (), s32[]{:S(2)}) async-start(), calls=%async_computation.16 | async-start | bytes 786432 | tf_op jit(solution)/shard_map/reduce_scatter | solution.py:951
  94.3 50.5 %copy-start.2 = (f32[2048,64]{1,0:T(8,128)}, f32[2048,64]{1,0:T(8,128)S(1)}, u32[]{:S(2)}) copy-start(f32[2048,64]{1,0:T(8,128)S(1)} %get-tuple-element.87) | copy-start | bytes 1572868
  227.7 54.6 %copy-start.8 = (bf16[256,1024]{1,0:T(8,128)(2,1)S(1)}, bf16[256,1024]{1,0:T(8,128)(2,1)}, u32[]{:S(2)}) copy-start(bf16[256,1024]{1,0:T(8,128)(2,1)} %refs_0_.2) | copy-start | bytes 1572868
  227.7 60.8 %copy-start.4 = (f32[2048,128]{1,0:T(8,128)S(1)}, f32[2048,128]{1,0:T(8,128)}, u32[]{:S(2)}) copy-start(f32[2048,128]{1,0:T(8,128)} %get-tuple-element.39) | copy-start | bytes 3145732
  439.1 61.4 %copy-start.10 = (f32[256,1024]{1,0:T(8,128)S(1)}, f32[256,1024]{1,0:T(8,128)}, u32[]{:S(2)}) copy-start(f32[256,1024]{1,0:T(8,128)} %shard_map.285) | copy-start | bytes 3145732
  439.1 61.4 %copy-start.14 = (bf16[256,1024]{1,0:T(8,128)(2,1)S(1)}, bf16[256,1024]{1,0:T(8,128)(2,1)}, u32[]{:S(2)}) copy-start(bf16[256,1024]{1,0:T(8,128)(2,1)} %refs_0_.3) | copy-start | bytes 1572868
  557.1 20.3 %slice-start = ((s8[8388608]{0:T(1024)(128)(4,1)}), s8[4194304]{0:T(1024)(128)(4,1)S(1)}, s32[]{:S(2)}) async-start(s8[8388608]{0:T(1024)(128)(4,1)} %bitcast.99), calls=%async_computation.21 | async-start | bytes 8388608
  565.6 11.7 %slice-start.1 = ((s8[8388608]{0:T(1024)(128)(4,1)}), s8[4194304]{0:T(1024)(128)(4,1)S(1)}, s32[]{:S(2)}) async-start(s8[8388608]{0:T(1024)(128)(4,1)} %bitcast.99), calls=%async_computation.22 | async-start | bytes 8388608
  565.7 11.7 %copy-start.16 = (bf16[2048,128]{1,0:T(8,128)(2,1)S(1)}, bf16[2048,128]{1,0:T(8,128)(2,1)}, u32[]{:S(2)}) copy-start(bf16[2048,128]{1,0:T(8,128)(2,1)} %fusion.15.refs_0_) | copy-start | bytes 1572868
  579.5 99.7 %reduce-scatter.9.cloned.1.call-start = ((), (), s32[]{:S(2)}) async-start(), calls=%async_computation.15 | async-start | bytes 2359296 | tf_op jit(solution)/shard_map/reduce_scatter | solution.py:938
  579.8 12.4 %copy-start.32 = (bf16[2048,128]{1,0:T(8,128)(2,1)S(1)}, bf16[2048,128]{1,0:T(8,128)(2,1)}, u32[]{:S(2)}) copy-start(bf16[2048,128]{1,0:T(8,128)(2,1)} %get-tuple-element.29) | copy-start | bytes 1572868
  609.1 87.5 %reduce-scatter.17.cloned.1.call-start = ((), (), s32[]{:S(2)}) async-start(), calls=%async_computation.19 | async-start | bytes 6291456 | tf_op jit(solution)/shard_map/reduce_scatter | solution.py:846
  609.5 8.7 copy-start.33
  629.7 124.3 %reduce-scatter.13.cloned.1.call-start = ((), (), s32[]{:S(2)}) async-start(), calls=%async_computation.17 | async-start | bytes 6291456 | tf_op jit(solution)/shard_map/reduce_scatter | solution.py:846
  629.9 8.8 copy-start.34
  661.2 18.0 %all-to-all-start.1 = ((bf16[8,128,128]{2,1,0:T(8,128)(2,1)}), bf16[8,128,128]{2,1,0:T(8,128)(2,1)S(1)}, u32[]{:S(2)}, u32[]{:S(2)}) async-start(bf16[8,128,128]{2,1,0:T(8,128)(2,1)} %bitcast_bitcast_fusion), calls=%async_computation.3 | async-start | bytes 524288 | tf_op jit(solution)/shard_map/all_to_all | solution.py:957
  679.2 26.4 %all-to-all-start = ((bf16[8,128,384]{2,1,0:T(8,128)(2,1)}), bf16[8,128,384]{2,1,0:T(8,128)(2,1)S(1)}, u32[]{:S(2)}, u32[]{:S(2)}) async-start(bf16[8,128,384]{2,1,0:T(8,128)(2,1)} %bitcast.106), calls=%async_computation.1 | async-start | bytes 1572864 | tf_op jit(solution)/shard_map/all_to_all | solution.py:943
  685.2 126.0 %reduce-scatter.15.cloned.1.call-start = ((), (), s32[]{:S(2)}) async-start(), calls=%async_computation.18 | async-start | bytes 6291456 | tf_op jit(solution)/shard_map/reduce_scatter | solution.py:846
  706.5 52.5 %all-to-all-start.4 = ((bf16[2,1024,512]{2,0,1:T(2,128)(2,1)}), bf16[2,1024,512]{2,0,1:T(2,128)(2,1)S(1)}, u32[]{:S(2)}, u32[]{:S(2)}) async-start(bf16[2,1024,512]{2,0,1:T(2,128)(2,1)} %copy.80), calls=%async_computation.9 | async-start | bytes 4194304 | tf_op jit(solution)/shard_map/all_to_all | solution.py:847
  710.1 54.9 %copy-start.25 = (bf16[1024]{0:T(1024)(128)(2,1)S(1)}, bf16[1024]{0:T(1024)(128)(2,1)}, u32[]{:S(2)}) copy-start(bf16[1024]{0:T(1024)(128)(2,1)} %param.22) | copy-start | bytes 6148
  759.0 57.2 %all-to-all-start.2 = ((bf16[2,1024,512]{2,0,1:T(2,128)(2,1)}), bf16[2,1024,512]{2,0,1:T(2,128)(2,1)}, u32[]{:S(2)}, u32[]{:S(2)}) async-start(bf16[2,1024,512]{2,0,1:T(2,128)(2,1)} %copy.76), calls=%async_computation.5 | async-start | bytes 4194304 | tf_op jit(solution)/shard_map/all_to_all | solution.py:847
  816.2 158.9 %all-to-all-start.3 = ((bf16[2,1024,512]{2,0,1:T(2,128)(2,1)}), bf16[2,1024,512]{2,0,1:T(2,128)(2,1)}, u32[]{:S(2)}, u32[]{:S(2)}) async-start(bf16[2,1024,512]{2,0,1:T(2,128)(2,1)} %copy.78), calls=%async_computation.7 | async-start | bytes 4194304 | tf_op jit(solution)/shard_map/all_to_all | solution.py:847
  821.7 132.6 %reduce-scatter.19.cloned.1.call-start = ((), (), s32[]{:S(2)}) async-start(), calls=%async_computation.20 | async-start | bytes 557056
  827.2 76.8 %copy-start.9 = (bf16[256,1024]{1,0:T(8,128)(2,1)S(1)}, bf16[256,1024]{1,0:T(8,128)(2,1)}, u32[]{:S(2)}) copy-start(bf16[256,1024]{1,0:T(8,128)(2,1)} %refs_0_.2) | copy-start | bytes 1572868
  827.2 78.4 %copy-start.22 = (f32[1024]{0:T(1024)S(1)}, f32[1024]{0:T(1024)}, u32[]{:S(2)}) copy-start(f32[1024]{0:T(1024)} %get-tuple-element.47) | copy-start | bytes 12292
  (22 other events, 88.4 us)
Sparse Core Ops, SparseCore 0:
  11.1 29.8 all-gather.4
  43.1 62.7 all-gather.6
  108.0 56.7 all-gather.8
  166.8 56.7 all-gather.10
  579.7 18.6 reduce-scatter.10
  609.2 30.1 reduce-scatter.8
  642.3 54.2 reduce-scatter.16
  699.6 54.3 reduce-scatter.12
  756.8 54.2 reduce-scatter.14
  825.3 86.4 reduce-scatter.18

commit v3 on v2

v3 whole, which is shorter than its diff:
```python
import jax
import jax.numpy as jnp
from jax import lax
from jax.experimental import pallas as pl
from jax.experimental.pallas import tpu as pltpu
from jax.sharding import PartitionSpec as P

norm_eps = 1e-06
rope_base = 10000.0


def locate(pack_spots, lengths_row):
    seq_ends = jnp.cumsum(lengths_row)
    starts = seq_ends - lengths_row
    segment = jnp.sum((pack_spots[:, None] >= seq_ends[None, :]).astype(jnp.int32), axis=1)
    slot_ids = jnp.arange(lengths_row.shape[0], dtype=jnp.int32)
    seq_begin = jnp.sum(
        jnp.where(segment[:, None] == slot_ids[None, :], starts[None, :], 0), axis=1
    )
    return (segment, pack_spots - seq_begin)


def rope_tables(pack_spots, head_dim):
    half_dim = head_dim // 2
    inv_freq = rope_base ** (-(jnp.arange(half_dim, dtype=jnp.float32) * 2.0 / head_dim))
    angle_grid = pack_spots.astype(jnp.float32)[:, None] * inv_freq[None, :]
    cosine, sine = jnp.cos(angle_grid), jnp.sin(angle_grid)
    return jnp.concatenate([cosine, cosine], axis=1), jnp.concatenate([-sine, sine], axis=1)


def unrotate(grad_rot, cosine, sine):
    return grad_rot * cosine + jnp.roll(grad_rot * sine, grad_rot.shape[1] // 2, axis=1)


CHUNKS = 2
MESH_ID = pl.DeviceIdType.MESH
VMEM_LIMIT = 64 * 1000 * 1000


class Pack:
    def __init__(self, ctx_size, tp_size, rows, cols, packs=1):
        self.line = ctx_size // 2
        self.packs = packs
        self.tp_size, self.rows, self.cols = tp_size, rows, cols
        self.chunk = rows // CHUNKS
        self.steps = self.line * CHUNKS
        place = lax.axis_index("ctx")
        self.a, self.b = place // 2, place % 2
        self.t = lax.axis_index("tp")
        self.has_up, self.has_down = self.a < self.line - 1, self.a > 0

    def up(self):
        return {"ctx": (self.a + 1) * 2 + self.b}

    def down(self):
        return {"ctx": (self.a - 1) * 2 + self.b}

    def pair(self):
        return {"ctx": self.a * 2 + (1 - self.b)}

    def sibling(self, shift):
        return {"tp": self.t ^ shift}

    def ctx_peer(self, shift):
        return {"ctx": lax.axis_index("ctx") ^ shift}

    def other_pack(self, shift):
        return {"fsdp": lax.axis_index("fsdp") ^ shift}

    def meet(self, everyone):
        barrier = pltpu.get_barrier_semaphore()

        def greet(device):
            pl.semaphore_signal(barrier, inc=1, device_id=device, device_id_type=MESH_ID)

        if everyone:
            near = 2 * self.line - 1
            for shift in range(1, 2 * self.line):
                greet(self.ctx_peer(shift))
        else:
            near = 1 + jnp.where(self.has_up, 1, 0) + jnp.where(self.has_down, 1, 0)

            @pl.when(self.has_up)
            def _():
                greet(self.up())

            @pl.when(self.has_down)
            def _():
                greet(self.down())

            greet(self.pair())
        for shift in range(1, self.tp_size):
            greet(self.sibling(shift))
        for shift in range(1, self.packs):
            greet(self.other_pack(shift))
        pl.semaphore_wait(barrier, near + self.tp_size + self.packs - 2)

    def row0(self, block, k):
        return pl.multiple_of(block * self.rows + k * self.chunk, self.chunk)

    def region(self, ref, block, k, part):
        return ref.at[
            pl.ds(self.row0(block, k), self.chunk),
            pl.ds(pl.multiple_of(part * self.cols, self.cols), self.cols),
        ]


def remote(src, dst, send_sem, recv_sem, device):
    return pltpu.make_async_remote_copy(
        src_ref=src,
        dst_ref=dst,
        send_sem=send_sem,
        recv_sem=recv_sem,
        device_id=device,
        device_id_type=MESH_ID,
    )


def loop(count, body):
    lax.fori_loop(0, count, lambda i, carry: (body(i), carry)[1], 0)


def gather_scratch(ctx_size, tp_size, rows, cols, dtype):
    line, dma = ctx_size // 2, pltpu.SemaphoreType.DMA
    return [
        pltpu.VMEM((ctx_size * rows, tp_size * cols), dtype),
        dma((2 * line * CHUNKS,)),
        dma((2 * line * CHUNKS,)),
        dma((4 * line * (tp_size - 1) * CHUNKS,)),
        dma((ctx_size * CHUNKS,)),
        dma(((tp_size - 1) * ctx_size * CHUNKS,)),
        dma,
    ]


def gather_steps(pack, src, scratch, everyone, lag, begin, before, compute):
    buf, line_sems, pair_sems, tp_sems, own_sems, sib_sems, local_sem = scratch
    line, t, a, b = pack.line, pack.t, pack.a, pack.b
    ctx_size = 2 * line

    def part(block, k):
        return pack.region(buf, block, k, t)

    def line_copy(piece, block, k, down, dist):
        return remote(
            piece,
            part(block, k),
            line_sems.at[(down * line + dist) * CHUNKS + k],
            own_sems.at[block * CHUNKS + k],
            pack.down() if down else pack.up(),
        )

    def pair_copy(piece, block, k, slot):
        return remote(
            piece,
            part(block, k),
            pair_sems.at[slot * CHUNKS + k],
            own_sems.at[block * CHUNKS + k],
            pack.pair(),
        )

    def tp_copy(piece, block, k, slot, shift):
        return remote(
            piece,
            part(block, k),
            tp_sems.at[(slot * (pack.tp_size - 1) + shift - 1) * CHUNKS + k],
            sib_sems.at[((shift - 1) * ctx_size + block) * CHUNKS + k],
            pack.sibling(shift),
        )

    def send_tp(piece, block, k, slot):
        for shift in range(1, pack.tp_size):
            tp_copy(piece, block, k, slot, shift).start()

    def await_own(block, k):
        piece = part(block, k)
        pair_copy(piece, block, k, 0).wait_recv()

    pack.meet(everyone)
    mine = a * 2 + b
    own_copy = pltpu.make_async_copy(
        src,
        buf.at[
            pl.ds(pl.multiple_of(mine * pack.rows, pack.rows), pack.rows),
            pl.ds(pl.multiple_of(t * pack.cols, pack.cols), pack.cols),
        ],
        local_sem,
    )
    own_copy.start()
    for k in range(CHUNKS):
        piece = src.at[pl.ds(k * pack.chunk, pack.chunk), :]

        @pl.when(pack.has_up)
        def _():
            line_copy(piece, mine, k, 0, 0).start()

        @pl.when(pack.has_down)
        def _():
            line_copy(piece, mine, k, 1, 0).start()

        pair_copy(piece, mine, k, 0).start()
    for k in range(CHUNKS):
        send_tp(src.at[pl.ds(k * pack.chunk, pack.chunk), :], mine, k, 0)
    begin()
    own_copy.wait()

    def ways(dist):
        below, above = a - dist, a + dist
        return (
            (0, below, below >= 0, jnp.logical_and(below >= 0, pack.has_up)),
            (1, above, above < line, jnp.logical_and(above < line, pack.has_down)),
        )

    def from_line(dist, k):
        for down, node, there, onward in ways(dist):
            block = node * 2 + b

            @pl.when(there)
            def _():
                await_own(block, k)

            @pl.when(onward)
            def _():
                line_copy(part(block, k), block, k, down, dist).start()

            @pl.when(there)
            def _():
                pair_copy(part(block, k), block, k, down * line + dist).start()
                send_tp(part(block, k), block, k, down * line + dist)

    def from_pair(dist, k):
        for down, node, there, _ in ways(dist):
            block = node * 2 + (1 - b)
            if down:
                there = jnp.logical_and(there, dist > 0)

            @pl.when(there)
            def _():
                await_own(block, k)
                send_tp(part(block, k), block, k, (2 + down) * line + dist)

    def work(block, k, order):
        for shift in range(1, pack.tp_size):
            piece = pack.region(buf, block, k, t ^ shift)
            remote(
                piece,
                piece,
                tp_sems.at[0],
                sib_sems.at[((shift - 1) * ctx_size + block) * CHUNKS + k],
                pack.sibling(shift),
            ).wait_recv()
        compute(pack.row0(block, k), block * CHUNKS + k, order)

    def step(s):
        dist, k = s // CHUNKS, s % CHUNKS

        @pl.when(dist + 1 < line)
        def _():
            from_line(dist + 1, k)

        @pl.when(s < pack.steps)
        def _():
            from_pair(dist, k)

        @pl.when(s == lag)
        def _():
            before()

        turn = s - lag

        def side(i):
            late = turn - i
            node, late_k = a ^ (late // CHUNKS), late % CHUNKS

            @pl.when(jnp.logical_and(late >= 0, late < pack.steps))
            def _():
                order = jnp.where(
                    i == 0,
                    jnp.maximum(2 * turn - 1, 0),
                    jnp.minimum(2 * turn, 2 * pack.steps - 1),
                )
                work(node * 2 + jnp.where(i == 0, b, 1 - b), late_k, order)

        loop(2, side)

    loop(pack.steps + 1 + lag, step)

    def drain(s):
        dist, k = s // CHUNKS, s % CHUNKS
        piece = part(0, 0)
        for down, _, there, onward in ways(dist):

            @pl.when(jnp.logical_and(onward, dist < line - 1))
            def _():
                line_copy(piece, 0, k, down, dist).wait_send()

            if down:
                there = jnp.logical_and(there, dist > 0)

            @pl.when(there)
            def _():
                pair_copy(piece, 0, k, down * line + dist).wait_send()
                for shift in range(1, pack.tp_size):
                    tp_copy(piece, 0, k, down * line + dist, shift).wait_send()
                    tp_copy(piece, 0, k, (2 + down) * line + dist, shift).wait_send()

    loop(pack.steps, drain)


def scatter_scratch(ctx_size, tp_size, rows, cols):
    line, dma = ctx_size // 2, pltpu.SemaphoreType.DMA
    low = jnp.bfloat16
    return [
        pltpu.VMEM((ctx_size * rows, tp_size * cols), low),
        pltpu.VMEM(((tp_size - 1) * ctx_size * rows, cols), low),
        pltpu.VMEM((line * rows, cols), low),
        pltpu.VMEM((2 * line * rows, cols), low),
        dma(((tp_size - 1) * ctx_size * CHUNKS,)),
        dma((line * CHUNKS,)),
        dma((line * CHUNKS,)),
        dma(((tp_size - 1) * ctx_size * CHUNKS,)),
        dma((line * CHUNKS,)),
        dma((2 * line * CHUNKS,)),
    ]


def scatter_steps(pack, scratch, everyone, begin, before, compute, finish):
    (full, sib_buf, pair_buf, line_buf, tp_send, pair_send, line_send, tp_recv, pair_recv, line_recv) = scratch
    line, t, a, b = pack.line, pack.t, pack.a, pack.b
    ctx_size = 2 * line
    wide, low = jnp.float32, jnp.bfloat16
    table = [
        sorted(range(line), key=lambda o, node=node: (-abs(o - node), o)) for node in range(line)
    ]

    def owner(i):
        result = jnp.int32(0)
        for node in range(line):
            for place in range(line):
                here = jnp.logical_and(a == node, i == place)
                result = jnp.where(here, table[node][place], result)
        return result

    def tp_copy(block, k, shift):
        return remote(
            pack.region(full, block, k, t ^ shift),
            sib_buf.at[
                pl.ds(pack.row0((shift - 1) * ctx_size + block, k), pack.chunk), :
            ],
            tp_send.at[((shift - 1) * ctx_size + block) * CHUNKS + k],
            tp_recv.at[((shift - 1) * ctx_size + block) * CHUNKS + k],
            pack.sibling(shift),
        )

    def pair_copy(node, k):
        return remote(
            pack.region(full, node * 2 + (1 - b), k, t),
            pair_buf.at[pl.ds(pack.row0(node, k), pack.chunk), :],
            pair_send.at[node * CHUNKS + k],
            pair_recv.at[node * CHUNKS + k],
            pack.pair(),
        )

    def line_copy(node, k, down):
        return remote(
            pack.region(full, node * 2 + b, k, t),
            line_buf.at[pl.ds(pack.row0(down * line + node, k), pack.chunk), :],
            line_send.at[node * CHUNKS + k],
            line_recv.at[(down * line + node) * CHUNKS + k],
            pack.down() if down else pack.up(),
        )

    def own_part(block, k):
        return full[
            pl.ds(pack.row0(block, k), pack.chunk),
            pl.ds(pl.multiple_of(t * pack.cols, pack.cols), pack.cols),
        ].astype(wide)

    def put_part(block, k, value):
        full[
            pl.ds(pack.row0(block, k), pack.chunk),
            pl.ds(pl.multiple_of(t * pack.cols, pack.cols), pack.cols),
        ] = value.astype(low)

    def landed(ref, block, k):
        return ref[pl.ds(pack.row0(block, k), pack.chunk), :].astype(wide)

    def fill(block, k, order):
        row0 = pack.row0(block, k)
        full[pl.ds(row0, pack.chunk), :] = compute(row0, block * CHUNKS + k, order)
        for shift in range(1, pack.tp_size):
            tp_copy(block, k, shift).start()

    def join(block, k):
        total = own_part(block, k)
        for shift in range(1, pack.tp_size):
            tp_copy(block, k, shift).wait_recv()
            total = total + landed(sib_buf, (shift - 1) * ctx_size + block, k)
        put_part(block, k, total)

    pack.meet(everyone)
    begin()
    before()

    def step(s):
        @pl.when(s < pack.steps)
        def _():
            node, k = owner(s // CHUNKS), s % CHUNKS

            def side(i):
                fill(node * 2 + jnp.where(i == 0, 1 - b, b), k, 2 * s + i)

            loop(2, side)

        late = s - 1

        @pl.when(jnp.logical_and(late >= 0, late < pack.steps))
        def _():
            node, k = owner(late // CHUNKS), late % CHUNKS

            def side(i):
                join(node * 2 + jnp.where(i == 0, 1 - b, b), k)

                @pl.when(i == 0)
                def _():
                    pair_copy(node, k).start()

            loop(2, side)

        later = s - 2

        @pl.when(later >= 0)
        def _():
            node, k = owner(later // CHUNKS), later % CHUNKS
            pair_copy(node, k).wait_recv()
            put_part(
                node * 2 + b, k, own_part(node * 2 + b, k) + landed(pair_buf, node, k)
            )
            from_below = jnp.logical_and(pack.has_down, node >= a)
            from_above = jnp.logical_and(pack.has_up, node <= a)
            for down, there in ((0, from_below), (1, from_above)):

                @pl.when(there)
                def _():
                    line_copy(node, k, down).wait_recv()
                    put_part(
                        node * 2 + b,
                        k,
                        own_part(node * 2 + b, k) + landed(line_buf, down * line + node, k),
                    )

            @pl.when(node > a)
            def _():
                line_copy(node, k, 0).start()

            @pl.when(node < a)
            def _():
                line_copy(node, k, 1).start()

            @pl.when(node == a)
            def _():
                finish(k, own_part(node * 2 + b, k))

    loop(pack.steps + 2, step)

    def drain(s):
        node, k = s // CHUNKS, s % CHUNKS
        pair_copy(node, k).wait_send()
        for shift in range(1, pack.tp_size):
            tp_copy(node * 2, k, shift).wait_send()
            tp_copy(node * 2 + 1, k, shift).wait_send()

        @pl.when(node > a)
        def _():
            line_copy(node, k, 0).wait_send()

        @pl.when(node < a)
        def _():
            line_copy(node, k, 1).wait_send()

    loop(pack.steps, drain)


ANY = pl.BlockSpec(memory_space=pl.ANY)


def nn_dot(left, right):
    return lax.dot_general(
        left, right, (((1,), (0,)), ((), ())), preferred_element_type=jnp.float32
    )


def nt_dot(left, right):
    return lax.dot_general(
        left, right, (((1,), (1,)), ((), ())), preferred_element_type=jnp.float32
    )


def tn_dot(left, right):
    return lax.dot_general(
        left, right, (((0,), (0,)), ((), ())), preferred_element_type=jnp.float32
    )


class Out:
    def __init__(self, width, dtype, flip=False, late=False):
        self.width, self.dtype, self.flip, self.late = width, dtype, flip, late

    def shape(self, rows):
        return (self.width, rows) if self.flip else (rows, self.width)

    def window(self, ref, window):
        return ref.at[:, window] if self.flip else ref.at[window, :]


class Parts:
    def __init__(self, shape, pieces):
        self.shape, self.pieces = shape, pieces


class Swap:
    def __init__(self, axis, shape, pieces, keep):
        self.axis, self.shape, self.pieces, self.keep = axis, shape, pieces, keep


class Ship:
    def __init__(self, axis, array, source, shape):
        self.axis, self.array, self.source, self.shape = axis, array, source, shape


class Make:
    def __init__(self, width, features, tile, send):
        self.width, self.features, self.tile, self.send = width, features, tile, send


class Deal:
    def __init__(self, own, far):
        self.own, self.far = own, far


class Tiles:
    def __init__(self, width, features, tile):
        self.width, self.features, self.tile = width, features, tile


def whole(ref):
    return ref


def pack_call(
    sizes,
    shape,
    piece,
    collective_id,
    flops,
    gathered=None,
    resident=(),
    outs=(),
    totals=(),
    last=None,
    keep=False,
    swaps=(),
    ships=(),
    tiles=None,
    makes=(),
    deals=(),
    lag=1,
):
    packs, ctx_size, tp_size = sizes
    rows, cols = shape
    all_rows, all_cols = ctx_size * rows, tp_size * cols
    pieces = ctx_size * CHUNKS
    dma = pltpu.SemaphoreType.DMA
    gather = gathered is not None
    if gather:
        base = gather_scratch(ctx_size, tp_size, rows, cols, gathered.dtype)
    else:
        base = scatter_scratch(ctx_size, tp_size, rows, cols)
    axis_size = {"fsdp": packs, "ctx": ctx_size, "tp": tp_size}
    inputs = []

    def enlist(array):
        for i, known in enumerate(inputs):
            if known is array:
                return i
        inputs.append(array)
        return len(inputs) - 1

    if gather:
        enlist(gathered)
    resident = list(resident)
    first_deal = len(resident)
    for deal in deals:
        resident += [deal.own, deal.far]
    parts = [
        r if isinstance(r, Parts) else Parts(r.shape, [(r, whole, whole)]) for r in resident
    ]
    part_list = [[(enlist(x), src, dst) for x, src, dst in p.pieces] for p in parts]
    swap_list = [[(enlist(x), src, dst) for x, src, dst in w.pieces] for w in swaps]
    ship_list = [enlist(ship.array) for ship in ships]
    swap_count = sum(len(w.pieces) * axis_size[w.axis] for w in swaps)
    ship_count = sum(axis_size[ship.axis] for ship in ships)
    kept_swaps = [i for i, w in enumerate(swaps) if w.keep]
    n_out = len(outs) + len(totals) + keep + len(kept_swaps) + len(ships)
    tile_rows = 128
    features = all_cols
    own_features = features // (packs * ctx_size)
    splits = tile_rows // own_features
    own_tiles = features // packs // tile_rows
    far_tiles = (packs - 1) * own_tiles
    assert own_tiles + far_tiles == pieces
    stride = pieces // own_tiles

    def kernel(*refs):
        refs = list(refs)

        def take(count):
            taken = refs[:count]
            del refs[:count]
            return taken

        given = take(len(inputs))
        sum_ref = None if gather else take(1)[0]
        out_refs = take(n_out)
        blocks_ref = None if tiles is None else take(1)[0]
        make_outs = [take(2) for _ in makes]
        deal_outs = take(len(deals))
        scratch = take(len(base))
        held = take(len(resident))
        stage = take(len(outs))
        total_refs = take(len(totals))
        swap_bufs = take(len(swaps))
        (held_sem, out_sem, late_sem, swap_local, swap_send, swap_recv, ship_send, ship_recv) = take(8)
        if tiles is not None:
            tile_stage, tile_far, tile_send, far_recv, block_recv = take(5)
        make_stages = take(len(makes))
        make_send, make_recv, deal_send, deal_recv = take(4)
        over_packs = swaps or ships or tiles is not None or any(make.send for make in makes)
        everyone = tiles is not None or deals or any(ship.axis == "ctx" for ship in ships)
        pack = Pack(ctx_size, tp_size, rows, cols, packs if over_packs else 1)
        mine = {axis: lax.axis_index(axis) for axis in axis_size}
        loads = []
        for target_ref, copies in zip(held, part_list):
            for which, source, target in copies:
                loads.append(
                    pltpu.make_async_copy(
                        source(given[which]), target(target_ref), held_sem.at[len(loads)]
                    )
                )
        swap_copies, swap_sends = [], []
        index = 0
        for swap, buf, copies in zip(swaps, swap_bufs, swap_list):
            for which, source, target in copies:
                here = source(given[which])
                there = target(buf, mine[swap.axis])
                swap_copies.append(pltpu.make_async_copy(here, there, swap_local.at[index]))
                for shift in range(1, axis_size[swap.axis]):
                    slot = index + shift
                    device = {swap.axis: mine[swap.axis] ^ shift}
                    theirs = target(buf, mine[swap.axis] ^ shift)
                    swap_sends.append(
                        (
                            remote(here, there, swap_send.at[slot], swap_recv.at[slot], device),
                            remote(theirs, theirs, swap_send.at[slot], swap_recv.at[slot], device),
                        )
                    )
                index += axis_size[swap.axis]
        late = []
        for i, where in enumerate(kept_swaps):
            late.append((swap_bufs[where], out_refs[len(outs) + len(totals) + keep + i]))
        late_copies = [
            pltpu.make_async_copy(here, there, late_sem.at[i])
            for i, (here, there) in enumerate(late)
        ]
        ship_local, ship_copies = [], []
        index = 0
        for ship, which, landing in zip(ships, ship_list, out_refs[n_out - len(ships) :]):
            place = mine[ship.axis]
            if ship.axis == "ctx":
                here = ship.source(given[which], 0)
                ship_local.append(
                    pltpu.make_async_copy(here, landing.at[place], ship_send.at[index])
                )
            for shift in range(1, axis_size[ship.axis]):
                here = ship.source(given[which], shift)
                there = landing.at[place] if ship.axis == "ctx" else landing.at[shift - 1]
                theirs = landing.at[place ^ shift] if ship.axis == "ctx" else there
                device = {ship.axis: place ^ shift}
                sems = ship_send.at[index + shift], ship_recv.at[index + shift]
                ship_copies.append(
                    (remote(here, there, *sems, device), remote(theirs, theirs, *sems, device))
                )
            index += axis_size[ship.axis]

        def begin():
            for copy in swap_copies + ship_local:
                copy.start()
            for send, _ in swap_sends + ship_copies:
                send.start()

        def before():
            for ref in total_refs:
                ref[...] = jnp.zeros_like(ref)
            for load in loads:
                load.wait()
            for copy in swap_copies:
                copy.wait()
            for send, receive in swap_sends:
                receive.wait_recv()
            for copy in late_copies:
                copy.start()

        def stores(row0, index):
            window = pl.ds(row0, pack.chunk)
            copies = []
            for i, out in enumerate(outs):
                if not out.late:
                    copies.append((out.window(stage[i], window), out.window(out_refs[i], window), i))
            if keep:
                i = len(outs)
                copies.append(
                    (scratch[0].at[window, :], out_refs[i + len(totals)].at[window, :], i)
                )
            return [
                pltpu.make_async_copy(here, there, out_sem.at[i * pieces + index])
                for here, there, i in copies
            ]

        def put(window, values):
            early = [i for i, out in enumerate(outs) if not out.late]
            for i, value in zip(early, values):
                out = outs[i]
                if out.flip:
                    stage[i][:, window] = value.astype(out.dtype)
                else:
                    stage[i][window, :] = value.astype(out.dtype)

        ahead = 3

        def is_far(order):
            if far_tiles != own_tiles:
                return order < far_tiles
            middle = jnp.logical_and(order >= ahead, order < pieces - ahead)
            return jnp.where(middle, (order - ahead) % 2 == 1, order < ahead)

        def rank(order):
            if far_tiles != own_tiles:
                return jnp.where(order < far_tiles, order, order - far_tiles)
            middle = (order - ahead) // 2
            return jnp.where(
                order < ahead,
                order,
                jnp.where(
                    order >= pieces - ahead,
                    order - far_tiles,
                    jnp.where(is_far(order), ahead + middle, middle),
                ),
            )

        def tile_copy(order, which, shift):
            return remote(
                tile_stage.at[order],
                tile_far.at[which],
                tile_send.at[order * splits],
                far_recv.at[which],
                {"fsdp": mine["fsdp"] ^ shift},
            )

        def block_copy(order, split, owner):
            return remote(
                tile_stage.at[order, pl.ds(split * own_features, own_features), :],
                blocks_ref.at[mine["ctx"]],
                tile_send.at[order * splits + split],
                block_recv.at[mine["ctx"]],
                {"ctx": owner},
            )

        def block_store(order, split):
            return pltpu.make_async_copy(
                tile_stage.at[order, pl.ds(split * own_features, own_features), :],
                blocks_ref.at[mine["ctx"]],
                tile_send.at[order * splits + split],
            )

        def each_block(order, go_away, stay):
            for split in range(splits):
                owner = ((mine["ctx"] // splits) ^ rank(order)) * splits + split

                @pl.when(owner != mine["ctx"])
                def _():
                    go_away(order, split, owner)

                @pl.when(owner == mine["ctx"])
                def _():
                    stay(order, split)

        def make_tile(order):
            if tiles is None:
                return
            far, which = is_far(order), rank(order)
            shift = jnp.where(far, which // own_tiles + 1, 0)
            place = (mine["ctx"] // splits) ^ (which % own_tiles)
            first = ((mine["fsdp"] ^ shift) * own_tiles + place) * tile_rows
            value = tiles.tile(pl.ds(pl.multiple_of(first, tile_rows), tile_rows), held)

            @pl.when(far)
            def _():
                tile_stage[order] = value.astype(jnp.bfloat16)
                tile_copy(order, which, shift).start()

            @pl.when(jnp.logical_not(far))
            def _():
                total = value
                for other in range(packs - 1):
                    slot = other * own_tiles + which
                    tile_copy(order, slot, 1).wait_recv()
                    total = total + tile_far[slot].astype(jnp.float32)
                tile_stage[order] = total.astype(jnp.bfloat16)
                each_block(
                    order,
                    lambda *where: block_copy(*where).start(),
                    lambda *where: block_store(*where).start(),
                )

        def finish_tiles():
            if tiles is None:
                return

            def sent(order):
                @pl.when(is_far(order))
                def _():
                    tile_copy(order, 0, 1).wait_send()

                @pl.when(jnp.logical_not(is_far(order)))
                def _():
                    each_block(
                        order,
                        lambda *where: block_copy(*where).wait_send(),
                        lambda *where: block_store(*where).wait(),
                    )

            loop(pieces, sent)
            for shift in range(1, ctx_size):
                landed = blocks_ref.at[mine["ctx"] ^ shift]
                remote(
                    landed,
                    landed,
                    tile_send.at[0],
                    block_recv.at[mine["ctx"] ^ shift],
                    {"ctx": mine["ctx"] ^ shift},
                ).wait_recv()

        def make_copies(i, order):
            far = order < far_tiles
            which = jnp.where(far, order, order - far_tiles)
            shift = jnp.where(far, which // own_tiles + 1, 0)
            window = pl.ds(
                pl.multiple_of(which % own_tiles * tile_rows, tile_rows), tile_rows
            )
            here = make_stages[i].at[order]
            sem = make_send.at[i * pieces + order]
            own_out, far_out = make_outs[i]
            slot = jnp.maximum(shift - 1, 0)
            send = remote(
                here,
                far_out.at[slot, window, :],
                sem,
                make_recv.at[i * pieces + order],
                {"fsdp": mine["fsdp"] ^ shift},
            )
            away = pltpu.make_async_copy(here, far_out.at[slot, window, :], sem)
            stay = pltpu.make_async_copy(here, own_out.at[window, :], sem)
            return far, shift, which % own_tiles, send, away, stay

        def make_parts(order):
            for i, make in enumerate(makes):
                far, shift, place, send, away, stay = make_copies(i, order)
                first = ((mine["fsdp"] ^ shift) * own_tiles + place) * tile_rows
                value = make.tile(pl.ds(pl.multiple_of(first, tile_rows), tile_rows), held)
                make_stages[i][order] = value.astype(jnp.bfloat16)

                @pl.when(far)
                def _():
                    (send if make.send else away).start()

                @pl.when(jnp.logical_not(far))
                def _():
                    stay.start()

        def finish_parts():
            def sent(order):
                for i, make in enumerate(makes):
                    far, _, _, send, away, stay = make_copies(i, order)

                    @pl.when(far)
                    def _():
                        if make.send:
                            send.wait_send()
                            send.wait_recv()
                        else:
                            away.wait()

                    @pl.when(jnp.logical_not(far))
                    def _():
                        stay.wait()

            loop(pieces, sent)

        def deal_blocks(i, turn, go_away, stay):
            own_buf, landing = held[first_deal + 2 * i], deal_outs[i]
            for split in range(splits):
                owner = ((mine["ctx"] // splits) ^ turn) * splits + split
                here = own_buf.at[
                    pl.ds(pl.multiple_of(owner * own_features, own_features), own_features), :
                ]
                there = landing.at[mine["ctx"]]
                sem = deal_send.at[(i * own_tiles + turn) * splits + split]

                @pl.when(owner != mine["ctx"])
                def _():
                    go_away(
                        remote(
                            here,
                            there,
                            sem,
                            deal_recv.at[i * ctx_size + mine["ctx"]],
                            {"ctx": owner},
                        )
                    )

                @pl.when(owner == mine["ctx"])
                def _():
                    stay(pltpu.make_async_copy(here, there, sem))

        def deal_out(order):
            if not deals:
                return

            @pl.when(order % stride == 0)
            def _():
                turn = order // stride
                place = (mine["ctx"] // splits) ^ turn
                window = pl.ds(pl.multiple_of(place * tile_rows, tile_rows), tile_rows)
                for i in range(len(deals)):
                    own_buf, far_buf = held[first_deal + 2 * i], held[first_deal + 2 * i + 1]
                    total = own_buf[window, :].astype(jnp.float32)
                    for other in range(packs - 1):
                        total = total + far_buf[other, window, :].astype(jnp.float32)
                    own_buf[window, :] = total.astype(jnp.bfloat16)
                    deal_blocks(i, turn, lambda copy: copy.start(), lambda copy: copy.start())

        def finish_deals():
            if not deals:
                return

            def sent(turn):
                for i in range(len(deals)):
                    deal_blocks(i, turn, lambda copy: copy.wait_send(), lambda copy: copy.wait())

            loop(own_tiles, sent)
            for i in range(len(deals)):
                for shift in range(1, ctx_size):
                    place = mine["ctx"] ^ shift
                    landed = deal_outs[i].at[place]
                    sem = deal_recv.at[i * ctx_size + place]
                    remote(landed, landed, deal_send.at[0], sem, {"ctx": place}).wait_recv()

        for load in loads:
            load.start()
        if gather:

            def compute(row0, index, order):
                window = pl.ds(row0, pack.chunk)
                put(window, piece(scratch[0][window, :], window, held + swap_bufs, total_refs))
                for store in stores(row0, index):
                    store.start()
                deal_out(order)
                make_tile(order)
                make_parts(order)

            gather_steps(pack, given[0], scratch, everyone, lag, begin, before, compute)
        else:

            def compute(row0, index, order):
                window = pl.ds(row0, pack.chunk)
                deal_out(order)
                make_tile(order)
                make_parts(order)
                rows_value, values = piece(window, held + swap_bufs, total_refs)
                put(window, values)
                for store in stores(row0, index):
                    store.start()
                return rows_value.astype(jnp.bfloat16)

            def finish(k, total):
                sum_ref[pl.ds(pl.multiple_of(k * pack.chunk, pack.chunk), pack.chunk), :] = total

            scatter_steps(pack, scratch, everyone, begin, before, compute, finish)
        if last is not None:
            last(held + swap_bufs, stage, total_refs, pack.chunk)
        ends = []
        for i, out in enumerate(outs):
            if out.late:
                ends.append((stage[i], out_refs[i]))
        for i, ref in enumerate(total_refs):
            ends.append((ref, out_refs[len(outs) + i]))
        end_copies = [
            pltpu.make_async_copy(here, there, late_sem.at[len(late) + i])
            for i, (here, there) in enumerate(ends)
        ]
        for copy in end_copies:
            copy.start()

        def drain(index):
            for store in stores(pl.multiple_of(index * pack.chunk, pack.chunk), index):
                store.wait()

        loop(pieces, drain)
        finish_tiles()
        finish_parts()
        finish_deals()
        for copy in late_copies + end_copies + ship_local:
            copy.wait()
        for send, _ in swap_sends:
            send.wait_send()
        for send, receive in ship_copies:
            send.wait_send()
            receive.wait_recv()

    low = jnp.bfloat16
    shapes = [jax.ShapeDtypeStruct(out.shape(all_rows), out.dtype) for out in outs]
    shapes += [jax.ShapeDtypeStruct(dims, dtype) for dims, dtype in totals]
    if keep:
        shapes.append(jax.ShapeDtypeStruct((all_rows, all_cols), gathered.dtype))
    shapes += [jax.ShapeDtypeStruct(swaps[i].shape, low) for i in kept_swaps]
    for ship in ships:
        slots = ctx_size if ship.axis == "ctx" else packs - 1
        shapes.append(jax.ShapeDtypeStruct((slots,) + ship.shape, ship.array.dtype))
    if tiles is not None:
        shapes.append(jax.ShapeDtypeStruct((ctx_size, own_features, tiles.width), low))
    part_features = features // packs
    for make in makes:
        shapes.append(jax.ShapeDtypeStruct((part_features, make.width), low))
        shapes.append(jax.ShapeDtypeStruct((packs - 1, part_features, make.width), low))
    for deal in deals:
        shapes.append(jax.ShapeDtypeStruct((ctx_size, own_features, deal.own.shape[1]), low))
    out_specs = [ANY] * len(shapes)
    if not gather:
        shapes = [jax.ShapeDtypeStruct(shape, jnp.float32)] + shapes
        out_specs = [pl.BlockSpec(memory_space=pltpu.VMEM)] + out_specs
    tile_scratch = []
    if tiles is not None:
        tile_scratch = [
            pltpu.VMEM((pieces, tile_rows, tiles.width), low),
            pltpu.VMEM((far_tiles, tile_rows, tiles.width), low),
            dma((pieces * splits,)),
            dma((far_tiles,)),
            dma((ctx_size,)),
        ]
    return pl.pallas_call(
        kernel,
        out_shape=tuple(shapes),
        in_specs=[ANY] * len(inputs),
        out_specs=tuple(out_specs),
        scratch_shapes=base
        + [pltpu.VMEM(p.shape, p.pieces[0][0].dtype) for p in parts]
        + [pltpu.VMEM(out.shape(all_rows), out.dtype) for out in outs]
        + [pltpu.VMEM(dims, dtype) for dims, dtype in totals]
        + [pltpu.VMEM(swap.shape, low) for swap in swaps]
        + [
            dma((max(1, sum(len(p.pieces) for p in parts)),)),
            dma(((len(outs) + 1) * pieces,)),
            dma((len(kept_swaps) + len(outs) + len(totals) + 1,)),
            dma((max(1, swap_count),)),
            dma((max(1, swap_count),)),
            dma((max(1, swap_count),)),
            dma((max(1, ship_count),)),
            dma((max(1, ship_count),)),
        ]
        + tile_scratch
        + [pltpu.VMEM((pieces, tile_rows, make.width), low) for make in makes]
        + [
            dma((max(1, len(makes)) * pieces,)),
            dma((max(1, len(makes)) * pieces,)),
            dma((max(1, len(deals)) * own_tiles * splits,)),
            dma((max(1, len(deals)) * ctx_size,)),
        ],
        compiler_params=pltpu.CompilerParams(
            collective_id=collective_id, has_side_effects=True, vmem_limit_bytes=VMEM_LIMIT
        ),
        cost_estimate=pl.CostEstimate(
            flops=flops, bytes_accessed=8 * all_rows * all_cols, transcendentals=0
        ),
    )(*inputs)


def small_sums(sizes, tensor, collective_id):
    packs, ctx_size, tp_size = sizes
    dma = pltpu.SemaphoreType.DMA
    count = tensor.shape[0]

    def kernel(src, out_ref, ctx_buf, mid, rest_buf, send_sems, recv_sems):
        f, c, t = (lax.axis_index(axis) for axis in ("fsdp", "ctx", "tp"))
        ctx_peers = [(shift, {"ctx": c ^ shift}) for shift in range(1, ctx_size)]
        rest_peers = [
            (shift * tp_size + turn, {"fsdp": f ^ shift, "tp": t ^ turn})
            for shift in range(packs)
            for turn in range(tp_size)
            if shift or turn
        ]
        barrier = pltpu.get_barrier_semaphore()
        for _, device in ctx_peers + rest_peers:
            pl.semaphore_signal(barrier, inc=1, device_id=device, device_id_type=MESH_ID)
        pl.semaphore_wait(barrier, len(ctx_peers) + len(rest_peers))

        def exchange(source, buf, peers, offset):
            copies = [
                remote(
                    source,
                    buf.at[slot],
                    send_sems.at[offset + slot],
                    recv_sems.at[offset + slot],
                    device,
                )
                for slot, device in peers
            ]
            for copy in copies:
                copy.start()
            for copy in copies:
                copy.wait()

        exchange(src, ctx_buf, ctx_peers, 0)
        total = src[...]
        for slot, _ in ctx_peers:
            total = total + ctx_buf[slot]
        mid[...] = total
        exchange(mid, rest_buf, rest_peers, ctx_size)
        rest_buf[0] = total
        for turn in range(tp_size):
            part = rest_buf[turn]
            for shift in range(1, packs):
                part = part + rest_buf[shift * tp_size + turn]
            out_ref[t ^ turn] = part

    return pl.pallas_call(
        kernel,
        out_shape=jax.ShapeDtypeStruct((tp_size, count, tensor.shape[1]), jnp.float32),
        in_specs=[pl.BlockSpec(memory_space=pltpu.VMEM)],
        out_specs=pl.BlockSpec(memory_space=pltpu.VMEM),
        scratch_shapes=[
            pltpu.VMEM((ctx_size,) + tensor.shape, jnp.float32),
            pltpu.VMEM(tensor.shape, jnp.float32),
            pltpu.VMEM((packs * tp_size,) + tensor.shape, jnp.float32),
            dma((ctx_size + packs * tp_size,)),
            dma((ctx_size + packs * tp_size,)),
        ],
        compiler_params=pltpu.CompilerParams(collective_id=collective_id, has_side_effects=True),
    )(tensor)

def on_device(
    hidden_in,
    cotangent,
    positions,
    seq_lengths,
    expert_ids,
    attn_norm,
    ffn_norm,
    query_norm,
    key_norm,
    w_query,
    w_key,
    w_value,
    w_out,
    w_router,
    w_gate,
    w_up,
    w_down,
):
    tok_rows, col_count = hidden_in.shape
    packs, ctx_size, tp_size = (lax.axis_size(axis) for axis in ("fsdp", "ctx", "tp"))
    sizes = (packs, ctx_size, tp_size)
    own_shape = (tok_rows, col_count)
    ctx_place = lax.axis_index("ctx")
    width_all = col_count * tp_size
    part_width = width_all // packs
    pack_rows = tok_rows * ctx_size
    head_dim = query_norm.shape[0]
    local_heads = w_query.shape[1] // head_dim
    expert_count, hidden_units = w_gate.shape[0], w_gate.shape[2]
    own_experts = expert_count // ctx_size
    own_units = own_experts * hidden_units
    top_count = expert_ids.shape[1]
    sharers = ctx_size // local_heads
    score_scale = head_dim ** (-0.5)
    wide = jnp.float32
    slim = jnp.bfloat16
    lanes = 128

    def row_total(tensor):
        return lax.psum(tensor, "tp")

    def units_of(ref, window, slot):
        return ref[window, pl.ds(slot * hidden_units, hidden_units)]

    def own_queries(window, value):
        if sharers == 1:
            return value
        share = window.start // (pack_rows // sharers)
        return jnp.where(share == lax.axis_index("ctx") // local_heads, value, 0.0)

    def head_window():
        return pl.ds(
            pl.multiple_of(lax.axis_index("ctx") % local_heads * head_dim, head_dim), head_dim
        )

    def part_of(place, size):
        return pl.ds(pl.multiple_of(place * size, size), size)

    half_rows = part_width // 2

    def half_ship(weight, slot, half):
        return Ship(
            "fsdp",
            weight,
            lambda ref, shift: ref.at[
                lax.axis_index("ctx") * own_experts + slot,
                pl.ds(half * half_rows, half_rows),
                :,
            ],
            (half_rows, hidden_units),
        )

    halves = [(slot, half) for slot in range(own_experts) for half in range(2)]
    expert_ships = [half_ship(w, *which) for w in (w_gate, w_up, w_down) for which in halves]
    first_ships = len(expert_ships) // 6
    second_ships = first_ships + (len(expert_ships) - first_ships) // 2

    def expert_weight(weight, far):
        pieces = [
            (
                weight,
                lambda ref: ref.at[pl.ds(lax.axis_index("ctx") * own_experts, own_experts), :, :],
                lambda buf: buf.at[:, part_of(lax.axis_index("fsdp"), part_width), :],
            )
        ]
        for (slot, half), array in zip(halves, far):
            for shift in range(1, packs):
                pieces.append(
                    (
                        array,
                        lambda ref, shift=shift: ref.at[shift - 1],
                        lambda buf, slot=slot, half=half, shift=shift: buf.at[
                            slot,
                            part_of((lax.axis_index("fsdp") ^ shift) * 2 + half, half_rows),
                            :,
                        ],
                    )
                )
        return Parts((own_experts, width_all, hidden_units), pieces)

    segment, place = locate(positions[0], seq_lengths[0])
    cosine, sine = rope_tables(place, head_dim)
    segment_rows = jnp.broadcast_to(segment[:, None], (pack_rows, lanes))
    segment_cols = jnp.broadcast_to(segment[None, :], (8, pack_rows))

    def project(rows, window, held, totals):
        cos_table, sin_table, gain_q, gain_k, weight, _, gain, _ = held
        hidden = rows.astype(wide)
        inverse = lax.rsqrt(jnp.mean(hidden * hidden, axis=1, keepdims=True) + norm_eps)
        normed = (hidden * inverse * gain[...].astype(wide)).astype(slim)
        raw = nn_dot(normed, weight[...])
        cos_rows, sin_rows = cos_table[window, :], sin_table[window, :]

        def prepare(raw_proj, gain_vec):
            inv = lax.rsqrt(jnp.mean(raw_proj * raw_proj, axis=1, keepdims=True) + norm_eps)
            scaled = raw_proj * inv * gain_vec[...]
            return scaled * cos_rows + pltpu.roll(scaled, head_dim // 2, 1) * sin_rows

        query_raw = raw[:, :head_dim]
        key_raw = raw[:, head_dim : 2 * head_dim]
        key_turned = prepare(key_raw, gain_k)
        return (
            normed,
            jnp.broadcast_to(inverse, (rows.shape[0], lanes)),
            query_raw,
            key_raw,
            prepare(query_raw, gain_q),
            key_turned,
            key_turned.T,
            raw[:, 2 * head_dim :],
        )

    gain_query = query_norm.astype(wide)[None, :]
    gain_key = key_norm.astype(wide)[None, :]
    (
        normed_first,
        inv_all,
        query_raw,
        key_raw,
        query_low,
        key_low,
        key_flip,
        value_low,
        qkv_weight,
        out_weight,
        router_full,
        *first_halves,
        ids_all,
    ) = pack_call(
        sizes,
        own_shape,
        project,
        1,
        6 * pack_rows * width_all * head_dim,
        gathered=hidden_in,
        resident=(cosine, sine, gain_query, gain_key),
        outs=(
            Out(width_all, slim),
            Out(lanes, wide),
            Out(head_dim, wide),
            Out(head_dim, wide),
            Out(head_dim, slim),
            Out(head_dim, slim),
            Out(head_dim, slim, flip=True),
            Out(head_dim, slim),
        ),
        swaps=(
            Swap(
                "fsdp",
                (width_all, 3 * head_dim),
                [
                    (
                        w,
                        lambda ref: ref.at[:, head_window()],
                        lambda buf, place, i=i: buf.at[
                            part_of(place, part_width), pl.ds(i * head_dim, head_dim)
                        ],
                    )
                    for i, w in enumerate((w_query, w_key, w_value))
                ],
                True,
            ),
            Swap(
                "fsdp",
                (head_dim, width_all),
                [
                    (
                        w_out,
                        lambda ref: ref.at[head_window(), :],
                        lambda buf, place: buf.at[:, part_of(place, part_width)],
                    )
                ],
                True,
            ),
            Swap(
                "tp",
                (1, width_all),
                [
                    (
                        attn_norm[None, :],
                        whole,
                        lambda buf, place: buf.at[:, part_of(place, col_count)],
                    )
                ],
                False,
            ),
            Swap(
                "fsdp",
                (expert_count, width_all),
                [(w_router, whole, lambda buf, place: buf.at[:, part_of(place, part_width)])],
                True,
            ),
        ),
        ships=expert_ships[:first_ships]
        + [Ship("ctx", expert_ids.T, lambda ref, shift: ref, (top_count, tok_rows))],
        lag=3,
    )
    router_pad = jnp.pad(router_full, ((0, lanes - expert_count), (0, 0)))

    def attend(rows, window, held, totals):
        query, key, value, seg_rows, seg_cols = held
        scores = nt_dot(query[window, :], key[...]) * score_scale
        same_seq = seg_rows[window, :][:, :1] == seg_cols[0:1, :]
        scores = jnp.where(same_seq, scores, -1e30)
        row_peak = jnp.max(scores, axis=1, keepdims=True)
        row_exp = jnp.exp(scores - row_peak)
        row_sum = jnp.sum(row_exp, axis=1, keepdims=True)
        probs_low = (row_exp * (1.0 / row_sum)).astype(slim)
        log_total = jnp.broadcast_to(row_peak + jnp.log(row_sum), (scores.shape[0], lanes))
        return own_queries(window, nn_dot(probs_low, value[...])), log_total.T[:8, :]

    attended_low, log_total, cotangent_all, *second_halves = pack_call(
        sizes,
        own_shape,
        attend,
        2,
        4 * pack_rows * pack_rows * head_dim,
        gathered=cotangent,
        resident=(query_low, key_low, value_low, segment_rows, segment_cols),
        outs=(Out(head_dim, slim), Out(8, wide, flip=True)),
        keep=True,
        ships=expert_ships[first_ships:second_ships],
    )
    attn_branch, *third_halves = pack_call(
        sizes,
        own_shape,
        lambda window, held, totals: (nn_dot(held[0][window, :], held[1][...]), ()),
        3,
        2 * pack_rows * width_all * head_dim,
        resident=(attended_low, out_weight),
        ships=expert_ships[second_ships:],
    )
    far_halves = first_halves + second_halves + third_halves
    gate_weight, up_weight, down_weight = (
        expert_weight(w, far_halves[i * len(halves) : (i + 1) * len(halves)])
        for i, w in enumerate((w_gate, w_up, w_down))
    )

    resid_in = hidden_in.astype(wide)
    middle = resid_in + attn_branch
    gain_second = ffn_norm.astype(wide)
    inv_second = lax.rsqrt(row_total(jnp.sum(middle * middle, axis=1)) / width_all + norm_eps)[
        :, None
    ]

    def experts(rows, window, held, totals):
        gate_w, up_w, down_w, router_w, ids_ref, cotangent_ref = held
        lane = lax.broadcasted_iota(jnp.int32, (rows.shape[0], lanes), 1)
        logits = jnp.where(lane < expert_count, nt_dot(rows, router_w[...]), -1e30)
        logit_exp = jnp.exp(logits - jnp.max(logits, axis=1, keepdims=True))
        route_probs = logit_exp / jnp.sum(logit_exp, axis=1, keepdims=True)
        block = window.start // tok_rows
        within = pl.multiple_of(window.start - block * tok_rows, rows.shape[0])
        ids = ids_ref[block, :, pl.ds(within, rows.shape[0])].T
        chosen = jnp.zeros((rows.shape[0], lanes), wide)
        for pick in range(ids.shape[1]):
            chosen = chosen + (ids[:, pick : pick + 1] == lane).astype(wide)
        gate_weights = route_probs * chosen
        first_expert = lax.axis_index("ctx") * own_experts
        rows_grad = cotangent_ref[window, :]
        grad_logits = jnp.zeros((rows.shape[0], lanes), wide)
        mixed_list, gate_list, up_list = [], [], []
        for slot in range(own_experts):
            mine = (lane == first_expert + slot).astype(wide)
            gates = jnp.sum(gate_weights * mine, axis=1, keepdims=True)
            gate_proj = nn_dot(rows, gate_w[slot])
            up_proj = nn_dot(rows, up_w[slot])
            grad_mixed = nn_dot(rows_grad, down_w[slot]).astype(slim).astype(wide)
            gate_sigmoid = jax.nn.sigmoid(gate_proj)
            silu = gate_proj * gate_sigmoid
            activity = silu * up_proj
            mixed_list.append((gates * activity).astype(slim))
            grad_gates = jnp.sum(grad_mixed * activity, axis=1, keepdims=True)
            grad_activity = grad_mixed * gates
            gate_list.append(
                (
                    grad_activity * up_proj * (gate_sigmoid + silu * (1.0 - gate_sigmoid))
                ).astype(slim)
            )
            up_list.append((grad_activity * silu).astype(slim))
            grad_logits = grad_logits + gates * grad_gates * (mine - route_probs)
        return (
            jnp.concatenate(mixed_list, axis=1),
            jnp.concatenate(gate_list, axis=1),
            jnp.concatenate(up_list, axis=1),
            grad_logits,
        )

    mixed_low, grad_gate_low, grad_up_low, grad_logits_low, normed_second = pack_call(
        sizes,
        own_shape,
        experts,
        4,
        6 * pack_rows * width_all * own_units,
        gathered=(middle * inv_second * gain_second).astype(slim),
        resident=(gate_weight, up_weight, down_weight, router_pad, ids_all, cotangent_all),
        outs=(
            Out(own_units, slim),
            Out(own_units, slim),
            Out(own_units, slim),
            Out(lanes, slim),
        ),
        keep=True,
    )

    def back(window, held, totals):
        gate_grad, up_grad, logit_grad, gate_w, up_w, router_w, _ = held
        total = nn_dot(logit_grad[window, :], router_w[...])
        for slot in range(own_experts):
            total = total + nt_dot(units_of(gate_grad, window, slot), gate_w[slot])
            total = total + nt_dot(units_of(up_grad, window, slot), up_w[slot])
        return total, ()

    def gate_tile(window, held):
        features = held[6][:, window]
        return jnp.concatenate(
            [tn_dot(features, held[0][...]), tn_dot(features, held[2][...])], axis=1
        )

    grad_second, gate_own, gate_far = pack_call(
        sizes,
        own_shape,
        back,
        5,
        6 * pack_rows * width_all * own_units,
        resident=(
            grad_gate_low,
            grad_up_low,
            grad_logits_low,
            gate_weight,
            up_weight,
            router_pad,
            normed_second,
        ),
        makes=(Make(own_units + lanes, width_all, gate_tile, True),),
    )

    def by_expert(blocks):
        count, rows = blocks.shape[:2]
        return (
            jnp.swapaxes(blocks.reshape(count, rows, own_experts, hidden_units), 1, 2)
            .reshape(expert_count, rows, hidden_units)
            .astype(wide)
        )

    def by_head(blocks):
        rows = blocks.shape[1]
        summed = jnp.sum(
            blocks.reshape(sharers, local_heads, rows, head_dim).astype(wide), axis=0
        )
        return jnp.swapaxes(summed, 0, 1).reshape(rows, local_heads * head_dim)

    gain_two_grad = jnp.sum(grad_second * middle * inv_second, axis=0)
    second_scaled = grad_second * gain_second
    second_inner = row_total(jnp.sum(second_scaled * middle, axis=1))[:, None]
    grad_middle = (
        cotangent.astype(wide)
        + inv_second * second_scaled
        - middle * inv_second**3 * second_inner / width_all
    )

    (
        grad_attended,
        grad_middle_all,
        up_own,
        up_far,
        down_own,
        down_away,
        gate_blocks,
    ) = pack_call(
        sizes,
        own_shape,
        lambda rows, window, held, totals: (own_queries(window, nt_dot(rows, held[0][...])),),
        6,
        2 * pack_rows * width_all * (head_dim + own_units),
        gathered=grad_middle.astype(slim),
        resident=(out_weight, normed_second, grad_up_low, cotangent_all, mixed_low),
        outs=(Out(head_dim, slim),),
        keep=True,
        makes=(
            Make(
                own_units,
                width_all,
                lambda window, held: tn_dot(held[1][:, window], held[2][...]),
                True,
            ),
            Make(
                own_units,
                width_all,
                lambda window, held: tn_dot(held[3][:, window], held[4][...]),
                False,
            ),
        ),
        deals=(Deal(gate_own, gate_far),),
    )
    grad_gate = by_expert(gate_blocks[:, :, :own_units])
    grad_router = row_total(
        jnp.sum(gate_blocks[:, :, own_units : own_units + expert_count].astype(wide), axis=0).T
    )


    def attend_back(window, held, totals):
        mixed_ref, down_w, query, key, key_t, value, grad_att = held[:7]
        seg_rows, seg_cols, log_ref = held[7:10]
        grad_query_rot, grad_key_rot, grad_value, _ = totals
        query_chunk, grad_chunk = query[window, :], grad_att[window, :]
        scores = nt_dot(key[...], query_chunk) * score_scale
        same_seq = seg_rows[...] == seg_cols[0:1, window]
        probs = jnp.exp(jnp.where(same_seq, scores, -1e30) - log_ref[0:1, window])
        grad_probs = nt_dot(value[...], grad_chunk)
        inner = jnp.sum(probs * grad_probs, axis=0, keepdims=True)
        grad_scores = (probs * (grad_probs - inner)).astype(slim)
        grad_value[...] += nn_dot(probs.astype(slim), grad_chunk)
        grad_key_rot[...] += nn_dot(grad_scores, query_chunk)
        grad_query_rot[window, :] = nn_dot(key_t[...], grad_scores).T
        total = sum(
            nt_dot(units_of(mixed_ref, window, slot), down_w[slot]) for slot in range(own_experts)
        )
        return total, ()

    def unturn_all(held, stage, totals, chunk):
        raws, cos_table, sin_table, gains = held[10:12], held[12], held[13], held[14:16]
        grad_rots, grad_value, gain_sums = totals[:2], totals[2], totals[3]

        def unturn(i):
            window = pl.ds(pl.multiple_of(i * chunk, chunk), chunk)
            cos_rows, sin_rows = cos_table[window, :], sin_table[window, :]
            for which in range(2):
                grad_rot = grad_rots[which][window, :] * score_scale
                raw = raws[which][window, :]
                inverse = lax.rsqrt(jnp.mean(raw * raw, axis=1, keepdims=True) + norm_eps)
                grad_normed = grad_rot * cos_rows + pltpu.roll(
                    grad_rot * sin_rows, head_dim // 2, 1
                )
                weighted = grad_normed * gains[which][...]
                grad_raw = inverse * weighted - raw * inverse**3 * jnp.mean(
                    weighted * raw, axis=1, keepdims=True
                )
                stage[0][window, pl.ds(which * head_dim, head_dim)] = grad_raw.astype(slim)
                gain_sums[pl.ds(which, 1), :] += jnp.sum(
                    grad_normed * raw * inverse, axis=0, keepdims=True
                )
            stage[0][window, pl.ds(2 * head_dim, head_dim)] = grad_value[window, :].astype(slim)

        loop(pack_rows // chunk, unturn)

    expert_branch, grad_qkv_low, _, _, _, gain_sums, down_far, up_blocks = pack_call(
        sizes,
        own_shape,
        attend_back,
        7,
        2 * pack_rows * width_all * own_units + 10 * pack_rows * pack_rows * head_dim,
        resident=(
            mixed_low,
            down_weight,
            query_low,
            key_low,
            key_flip,
            value_low,
            grad_attended,
            segment_rows,
            segment_cols,
            log_total,
            query_raw,
            key_raw,
            cosine,
            sine,
            gain_query,
            gain_key,
        ),
        outs=(Out(3 * head_dim, slim, late=True),),
        totals=(
            ((pack_rows, head_dim), wide),
            ((pack_rows, head_dim), wide),
            ((pack_rows, head_dim), wide),
            ((8, head_dim), wide),
        ),
        last=unturn_all,
        ships=(
            Ship(
                "fsdp",
                down_away,
                lambda ref, shift: ref.at[shift - 1],
                (part_width, own_units),
            ),
        ),
        deals=(Deal(up_own, up_far),),
    )
    hidden_out = (middle + expert_branch).astype(slim)
    grad_up = by_expert(up_blocks)

    def last_tile(window, held):
        return jnp.concatenate(
            [
                tn_dot(held[2][:, window], held[0][...]),
                tn_dot(held[3][:, window], held[4][...]),
            ],
            axis=1,
        )

    grad_first, last_blocks, down_blocks = pack_call(
        sizes,
        own_shape,
        lambda window, held, totals: (nt_dot(held[0][window, :], held[1][...]), ()),
        8,
        2 * pack_rows * width_all * 7 * head_dim,
        resident=(grad_qkv_low, qkv_weight, normed_first, grad_middle_all, attended_low),
        tiles=Tiles(4 * head_dim, width_all, last_tile),
        deals=(Deal(down_own, down_far),),
    )
    grad_down = by_expert(down_blocks)
    grad_query, grad_key, grad_value, grad_out = (
        by_head(last_blocks[:, :, i * head_dim : (i + 1) * head_dim]) for i in range(4)
    )
    grad_out = grad_out.T

    gain_first = attn_norm.astype(wide)
    inv_first = lax.dynamic_slice_in_dim(inv_all, ctx_place * tok_rows, tok_rows, 0)[:, :1]
    gain_one_grad = jnp.sum(grad_first * resid_in * inv_first, axis=0)
    first_scaled = grad_first * gain_first
    first_inner = row_total(jnp.sum(first_scaled * resid_in, axis=1))[:, None]
    grad_hidden = (
        grad_middle + inv_first * first_scaled - resid_in * inv_first**3 * first_inner / width_all
    )

    stream_part = jnp.stack(
        [
            jnp.sum(middle * middle),
            jnp.sum(attn_branch * attn_branch),
            jnp.sum(expert_branch * expert_branch),
        ]
    )
    gain_rows = col_count // lanes
    sums = small_sums(
        sizes,
        jnp.concatenate(
            [
                gain_one_grad.reshape(gain_rows, lanes),
                gain_two_grad.reshape(gain_rows, lanes),
                gain_sums,
                jnp.pad(stream_part[None, :], ((0, 7), (0, lanes - 3))),
            ],
            axis=0,
        ),
        9,
    )
    tp_sums = jnp.sum(sums[:, 2 * gain_rows :], axis=0)
    token_count = tok_rows * packs * ctx_size
    stream_rms = jnp.sqrt(tp_sums[8, :3] / (token_count * width_all))
    return (
        hidden_out,
        grad_hidden,
        sums[:, :gain_rows].reshape(width_all),
        sums[:, gain_rows : 2 * gain_rows].reshape(width_all),
        tp_sums[0],
        tp_sums[1],
        grad_query,
        grad_key,
        grad_value,
        grad_out,
        grad_router,
        grad_gate,
        grad_up,
        grad_down,
        stream_rms,
    )


def solution(mesh):
    return jax.shard_map(
        on_device,
        mesh=mesh,
        in_specs=(
            P(("fsdp", "ctx"), "tp"),
            P(("fsdp", "ctx"), "tp"),
            P("fsdp", None),
            P("fsdp", None),
            P(("fsdp", "ctx"), None),
            P("tp"),
            P("tp"),
            P(),
            P(),
            P("fsdp", "tp"),
            P("fsdp", "tp"),
            P("fsdp", "tp"),
            P("tp", "fsdp"),
            P(None, "fsdp"),
            P(None, "fsdp", "tp"),
            P(None, "fsdp", "tp"),
            P(None, "fsdp", "tp"),
        ),
        out_specs=(
            P(("fsdp", "ctx"), "tp"),
            P(("fsdp", "ctx"), "tp"),
            P(),
            P(),
            P(),
            P(),
            P(("fsdp", "ctx"), "tp"),
            P(("fsdp", "ctx"), "tp"),
            P(("fsdp", "ctx"), "tp"),
            P("tp", ("fsdp", "ctx")),
            P(None, ("fsdp", "ctx")),
            P(None, ("fsdp", "ctx"), "tp"),
            P(None, ("fsdp", "ctx"), "tp"),
            P(None, ("fsdp", "ctx"), "tp"),
            P(),
        ),
        check_vma=False,
    )
```

time: 989 us -> 766 us (0.77)
  Pallas kernels: 495 us -> 697 us
  matrix products: 110 us -> 0 us
  blocking collectives: 108 us -> 8.91 us
  waiting for transfers between devices: 94.9 us -> 0 us
  other arithmetic: 87.4 us -> 40.8 us
  starting transfers between devices: 30.4 us -> 0 us
  local copies, waits for them, and re-layouts: 47.2 us -> 17.2 us
  between operations: 15.1 us -> 0.91 us
    pallas_call x8 -> x9, Pallas kernels: 495 us -> 697 us  [the longest x8 680 us: pack_call(): pl.pallas_call(kernel, out_shape=tuple(shapes), in_specs=[ANY] * len(inpu...]
    dot_general x15 -> x0, matrix products: 110 us -> none  [dot(): lax.dot_general(left, right, ((dims[:1], dims[1:]), ((), ())), preferred_...]
    reduce_scatter x5 -> x0, waiting for transfers between devices: 90.9 us -> none  [the longest x3 90.9 us: spread_experts(): mine = lax.psum_scatter(parts, 'fsdp', scatter_dimension=1, tiled=True)]
    all_gather x4 -> x0, blocking collectives: 52.6 us -> none  [the longest x1 32.3 us: on_device(): ids_all = lax.all_gather(expert_ids, 'ctx', axis=0, tiled=True)]
    psum x1 -> x0, blocking collectives: 47.6 us -> none  [on_device(): lax.psum((stream_part, gains_part, query_gain_grad, key_gain_grad), ('fsd...]
    all_to_all x5 -> x0, starting transfers between devices: 29.2 us -> none  [the longest x3 15.1 us: spread_experts(): lax.all_to_all(mine, 'ctx', split_axis=1, concat_axis=0, tiled=True)]
    reduce_sum x5 -> x2, other arithmetic: 24.5 us -> 1.74 us  [the longest x1 1.01 us: on_device(): jnp.sum(gate_blocks[:, :, own_units:own_units + expert_count].astype(wide...]
    reduce_scatter x3 -> x0, local copies, waits for them, and re-layouts: 15.2 us -> none  [spread_experts(): mine = lax.psum_scatter(parts, 'fsdp', scatter_dimension=1, tiled=True)]
  transfers between devices with their start and end apart: 15 -> 0, of which waited for: 4 -> 0; matrix products, arithmetic and copies ran while one was open for 21% -> 0% of each run, Pallas kernels for 24% -> 0%
where the time goes in v3:
time: 766 us; the launch traced here: 765 us
  Pallas kernels  697 us (91%)
  other arithmetic  40.8 us (5%)
  local copies, waits for them, and re-layouts  17.2 us (2%)
  blocking collectives  8.91 us (1%)
    pallas_call x8, Pallas kernels, pack_call(): pl.pallas_call(kernel, out_shape=tuple(shapes), in_specs=[ANY] * len(inpu...  680 us
    pallas_call x1, Pallas kernels, small_sums(): pl.pallas_call(kernel, out_shape=jax.ShapeDtypeStruct((tp_size, count, te...  17.1 us

profile of v3, /device:TPU:0, one launch (start us, length us, event | category | flops | bytes accessed | tf_op | source)
XLA Modules:
  0.0 765.0 jit_solution(1069470276322004037)
XLA Ops:
  4.7 1.3 broadcast_in_dim.61.refs_9_
  8.2 1.3 broadcast_in_dim.62.refs_4_.refs_11_
  9.5 3.7 fusion.6
  13.2 1.9 pad_maximum_fusion.3
  15.2 64.6 %shard_map.280 = (bf16[2048,2048]{1,0:T(8,128)(2,1)}, f32[2048,128]{1,0:T(8,128)}, f32[2048,128]{1,0:T(8,128)}, f32[2048,128]{1,0:T(8,128)}, bf16[2048,128]{1,0:...) custom-call(bf16[256,1024]{1,0:T(8,128)(2,1)} %refs_0_.2, ...), custom_call_target="tpu_custom_call" | custom-call | flops 3221225472 | bytes 33554432 | tf_op jit(solution)/shard_map/pallas_call | solution.py:1060
  80.8 1.7 pad.8.refs_16_.refs_13_
  82.5 63.8 %shard_map.281 = (bf16[2048,128]{1,0:T(8,128)(2,1)}, f32[8,2048]{1,0:T(8,128)}, bf16[2048,2048]{1,0:T(8,128)(2,1)}, bf16[1,512,512]{2,1,0:T(8,128)(2,1)}, bf16[1...) custom-call(bf16[256,1024]{1,0:T(8,128)(2,1)} %refs_0_.3, ...), custom_call_target="tpu_custom_call" | custom-call | flops 2147483648 | bytes 33554432 | tf_op jit(solution)/shard_map/pallas_call | solution.py:1060
  146.4 60.9 %shard_map.282 = (f32[256,1024]{1,0:T(8,128)}, bf16[1,512,512]{2,1,0:T(8,128)(2,1)}, bf16[1,512,512]{2,1,0:T(8,128)(2,1)}, bf16[1,512,512]{2,1,0:T(8,128)(2,1)},...) custom-call(bf16[2048,128]{1,0:T(8,128)(2,1)} %get-tuple-element.69.refs_0_.refs_4_, ...), custom_call_target="tpu_custom_call" | custom-call | flops 1073741824 | bytes 33554432 | tf_op jit(solution)/shard_map/pallas_call | solution.py:1060
  207.3 2.2 multiply_reduce_fusion.5
  209.5 2.4 psum.28
  212.9 63.7 %shard_map.283 = (bf16[2048,1024]{1,0:T(8,128)(2,1)}, bf16[2048,1024]{1,0:T(8,128)(2,1)}, bf16[2048,1024]{1,0:T(8,128)(2,1)}, bf16[2048,128]{1,0:T(8,128)(2,1)}, bf16[2048,2048]{1,0:T(8,128)(2,1)}) custom-call(bf16[256,1024]{1,0:T(8,128)(2,1)} %multiply_convert_fusion.refs_0_, bf16[16,1024,512]{2,1,0:T(8,128)(2,1)} %refs_3_.3, ...), custom_call_target="tpu_custom_call" | custom-call | flops 25769803776 | bytes 33554432 | tf_op jit(solution)/shard_map/pallas_call | solution.py:1060
  276.6 89.0 %shard_map.284 = (f32[256,1024]{1,0:T(8,128)}, bf16[1024,1152]{1,0:T(8,128)(2,1)}, bf16[1,1024,1152]{2,1,0:T(8,128)(2,1)}) custom-call(bf16[2048,1024]{1,0:T(8,128)(2,1)} %get-tuple-element.89.refs_0_, bf16[2048,1024]{1,0:T(8,128)(2,1)} %get-tuple-element.90.refs_1_.refs_3_, bf16[2048,128]{1,0:T(8,128)(2,1)} %get-tuple-element.91.refs_2_, ...), custom_call_target="tpu_custom_call" | custom-call | flops 25769803776 | bytes 33554432 | tf_op jit(solution)/shard_map/pallas_call | solution.py:1060
  365.5 2.4 multiply_reduce_fusion.2
  367.9 2.7 psum.29
  370.6 2.6 fusion.11
  373.2 101.7 %shard_map.285 = (bf16[2048,128]{1,0:T(8,128)(2,1)}, bf16[2048,2048]{1,0:T(8,128)(2,1)}, bf16[1024,1024]{1,0:T(8,128)(2,1)}, bf16[1,1024,1024]{2,1,0:T(8,128)(2,...) custom-call(bf16[256,1024]{1,0:T(8,128)(2,1)} %get-tuple-element.171.refs_0_, ...), custom_call_target="tpu_custom_call" | custom-call | flops 9663676416 | bytes 33554432 | tf_op jit(solution)/shard_map/pallas_call | solution.py:1060
  474.9 102.7 %shard_map.286 = (f32[256,1024]{1,0:T(8,128)}, bf16[2048,384]{1,0:T(8,128)(2,1)}, f32[2048,128]{1,0:T(8,128)}, f32[2048,128]{1,0:T(8,128)}, f32[2048,128]{1,0:T(...) custom-call(bf16[2048,1024]{1,0:T(8,128)(2,1)} %get-tuple-element.87.refs_5_.refs_0_, ...), custom_call_target="tpu_custom_call" | custom-call | flops 13958643712 | bytes 33554432 | tf_op jit(solution)/shard_map/pallas_call | solution.py:1060
  577.6 133.6 %shard_map.287 = (f32[256,1024]{1,0:T(8,128)}, bf16[8,128,512]{2,1,0:T(8,128)(2,1)}, bf16[8,128,1024]{2,1,0:T(8,128)(2,1)}) custom-call(bf16[2048,384]{1,0:T(8,128)(2,1)} %get-tuple-element.105.refs_0_, bf16[2048,384]{1,0:T(8,128)(2,1)} %get-tuple-element.106.refs_1_, bf16[2048,2048]{1,0:T(8,128)(2,1)} %get-tuple-element.107.refs_2_, ...), custom_call_target="tpu_custom_call" | custom-call | flops 7516192768 | bytes 33554432 | tf_op jit(solution)/shard_map/pallas_call | solution.py:1060
  711.3 1.6 multiply_reduce_fusion
  712.9 2.0 maximum_bitcast_fusion
  716.0 17.1 %shard_map.288 = f32[2,32,128]{2,1,0:T(8,128)} custom-call(f32[32,128]{1,0:T(8,128)} %select_maximum_fusion.src), custom_call_target="tpu_custom_call" | custom-call | tf_op jit(solution)/shard_map/pallas_call | solution.py:1145
  733.8 1.3 slice_bitcast_fusion
  737.2 1.7 fusion.12
  739.0 3.8 all-reduce.2
  742.8 2.9 fusion.2
  746.4 2.4 convert_bitcast_fusion
  749.7 1.2 copy.49
  752.0 1.2 copy.48
  754.2 1.2 copy.47
  756.5 2.6 convert.16
  759.4 2.6 convert.18
  762.4 2.6 convert.17
  (43 shorter events, 17.6 us)
Async XLA Ops:
  146.3 61.0 %copy-start = (bf16[256,1024]{1,0:T(8,128)(2,1)S(1)}, bf16[256,1024]{1,0:T(8,128)(2,1)}, u32[]{:S(2)}) copy-start(bf16[256,1024]{1,0:T(8,128)(2,1)} %refs_0_.2) | copy-start | bytes 1572868
  365.5 5.1 copy-start.2
  577.6 133.7 %copy-start.5 = (f32[256,1024]{1,0:T(8,128)S(1)}, f32[256,1024]{1,0:T(8,128)}, u32[]{:S(2)}) copy-start(f32[256,1024]{1,0:T(8,128)} %get-tuple-element.103) | copy-start | bytes 3145732
  711.3 3.7 copy-start.1
  711.3 4.1 copy-start.6
  756.5 2.6 copy-start.4
  759.4 2.6 copy-start.3

commit v4 on v3

--- a/solution.py
+++ b/solution.py
@@ -103,6 +103,13 @@
             pl.ds(self.row0(block, k), self.chunk),
             pl.ds(pl.multiple_of(part * self.cols, self.cols), self.cols),
         ]
+
+
+def pick(table, i):
+    result = jnp.int32(table[-1])
+    for at, value in enumerate(table[:-1]):
+        result = jnp.where(i == at, value, result)
+    return result
 
 
 def remote(src, dst, send_sem, recv_sem, device):
@@ -324,7 +331,7 @@
     ]
 
 
-def scatter_steps(pack, scratch, everyone, begin, before, compute, finish):
+def scatter_steps(pack, scratch, everyone, begin, before, compute, jobs, finish):
     (full, sib_buf, pair_buf, line_buf, tp_send, pair_send, line_send, tp_recv, pair_recv, line_recv) = scratch
     line, t, a, b = pack.line, pack.t, pack.a, pack.b
     ctx_size = 2 * line
@@ -385,11 +392,12 @@
     def landed(ref, block, k):
         return ref[pl.ds(pack.row0(block, k), pack.chunk), :].astype(wide)
 
-    def fill(block, k, order):
-        row0 = pack.row0(block, k)
-        full[pl.ds(row0, pack.chunk), :] = compute(row0, block * CHUNKS + k, order)
-        for shift in range(1, pack.tp_size):
-            tp_copy(block, k, shift).start()
+    def fill(block):
+        row0 = pl.multiple_of(block * pack.rows, pack.rows)
+        full[pl.ds(row0, pack.rows), :] = compute(row0)
+        for k in range(CHUNKS):
+            for shift in range(1, pack.tp_size):
+                tp_copy(block, k, shift).start()
 
     def join(block, k):
         total = own_part(block, k)
@@ -408,7 +416,11 @@
             node, k = owner(s // CHUNKS), s % CHUNKS
 
             def side(i):
-                fill(node * 2 + jnp.where(i == 0, 1 - b, b), k, 2 * s + i)
+                @pl.when(k == 0)
+                def _():
+                    fill(node * 2 + jnp.where(i == 0, 1 - b, b))
+
+                jobs(2 * s + i)
 
             loop(2, side)
 
@@ -427,7 +439,7 @@
 
             loop(2, side)
 
-        later = s - 2
+        later = s - 4
 
         @pl.when(later >= 0)
         def _():
@@ -461,7 +473,7 @@
             def _():
                 finish(k, own_part(node * 2 + b, k))
 
-    loop(pack.steps + 2, step)
+    loop(pack.steps + 4, step)
 
     def drain(s):
         node, k = s // CHUNKS, s % CHUNKS
@@ -610,6 +622,7 @@
     far_tiles = (packs - 1) * own_tiles
     assert own_tiles + far_tiles == pieces
     stride = pieces // own_tiles
+    deal_order = (4, 1, 6, 2, 5, 3, 7, 0) if own_tiles == 8 else tuple(range(own_tiles))
 
     def kernel(*refs):
         refs = list(refs)
@@ -784,7 +797,7 @@
 
         def each_block(order, go_away, stay):
             for split in range(splits):
-                owner = ((mine["ctx"] // splits) ^ rank(order)) * splits + split
+                owner = ((mine["ctx"] // splits) ^ pick(deal_order, rank(order))) * splits + split
 
                 @pl.when(owner != mine["ctx"])
                 def _():
@@ -799,7 +812,7 @@
                 return
             far, which = is_far(order), rank(order)
             shift = jnp.where(far, which // own_tiles + 1, 0)
-            place = (mine["ctx"] // splits) ^ (which % own_tiles)
+            place = (mine["ctx"] // splits) ^ pick(deal_order, which % own_tiles)
             first = ((mine["fsdp"] ^ shift) * own_tiles + place) * tile_rows
             value = tiles.tile(pl.ds(pl.multiple_of(first, tile_rows), tile_rows), held)
 
@@ -909,7 +922,7 @@
         def deal_blocks(i, turn, go_away, stay):
             own_buf, landing = held[first_deal + 2 * i], deal_outs[i]
             for split in range(splits):
-                owner = ((mine["ctx"] // splits) ^ turn) * splits + split
+                owner = ((mine["ctx"] // splits) ^ pick(deal_order, turn)) * splits + split
                 here = own_buf.at[
                     pl.ds(pl.multiple_of(owner * own_features, own_features), own_features), :
                 ]
@@ -939,7 +952,7 @@
             @pl.when(order % stride == 0)
             def _():
                 turn = order // stride
-                place = (mine["ctx"] // splits) ^ turn
+                place = (mine["ctx"] // splits) ^ pick(deal_order, turn)
                 window = pl.ds(pl.multiple_of(place * tile_rows, tile_rows), tile_rows)
                 for i in range(len(deals)):
                     own_buf, far_buf = held[first_deal + 2 * i], held[first_deal + 2 * i + 1]
@@ -981,21 +994,21 @@
             gather_steps(pack, given[0], scratch, everyone, lag, begin, before, compute)
         else:
 
-            def compute(row0, index, order):
-                window = pl.ds(row0, pack.chunk)
+            def compute(row0):
+                window = pl.ds(row0, pack.rows)
+                rows_value, values = piece(window, held + swap_bufs, total_refs)
+                put(window, values)
+                return rows_value.astype(jnp.bfloat16)
+
+            def jobs(order):
                 deal_out(order)
                 make_tile(order)
                 make_parts(order)
-                rows_value, values = piece(window, held + swap_bufs, total_refs)
-                put(window, values)
-                for store in stores(row0, index):
-                    store.start()
-                return rows_value.astype(jnp.bfloat16)
 
             def finish(k, total):
                 sum_ref[pl.ds(pl.multiple_of(k * pack.chunk, pack.chunk), pack.chunk), :] = total
 
-            scatter_steps(pack, scratch, everyone, begin, before, compute, finish)
+            scatter_steps(pack, scratch, everyone, begin, before, compute, jobs, finish)
         if last is not None:
             last(held + swap_bufs, stage, total_refs, pack.chunk)
         ends = []
@@ -1378,8 +1391,8 @@
     router_pad = jnp.pad(router_full, ((0, lanes - expert_count), (0, 0)))
 
     def attend(rows, window, held, totals):
-        query, key, value, seg_rows, seg_cols = held
-        scores = nt_dot(query[window, :], key[...]) * score_scale
+        query, key_t, value, seg_rows, seg_cols = held
+        scores = nn_dot(query[window, :], key_t[...]) * score_scale
         same_seq = seg_rows[window, :][:, :1] == seg_cols[0:1, :]
         scores = jnp.where(same_seq, scores, -1e30)
         row_peak = jnp.max(scores, axis=1, keepdims=True)
@@ -1396,7 +1409,7 @@
         2,
         4 * pack_rows * pack_rows * head_dim,
         gathered=cotangent,
-        resident=(query_low, key_low, value_low, segment_rows, segment_cols),
+        resident=(query_low, key_flip, value_low, segment_rows, segment_cols),
         outs=(Out(head_dim, slim), Out(8, wide, flip=True)),
         keep=True,
         ships=expert_ships[first_ships:second_ships],
@@ -1585,7 +1598,8 @@
         grad_query_rot, grad_key_rot, grad_value, _ = totals
         query_chunk, grad_chunk = query[window, :], grad_att[window, :]
         scores = nt_dot(key[...], query_chunk) * score_scale
-        same_seq = seg_rows[...] == seg_cols[0:1, window]
+        key_segments = jnp.concatenate([seg_rows[...]] * (tok_rows // lanes), axis=1)
+        same_seq = key_segments == seg_cols[0:1, window]
         probs = jnp.exp(jnp.where(same_seq, scores, -1e30) - log_ref[0:1, window])
         grad_probs = nt_dot(value[...], grad_chunk)
         inner = jnp.sum(probs * grad_probs, axis=0, keepdims=True)

time: 766 us -> 694 us (0.906)
  Pallas kernels: 697 us -> 625 us
    pallas_call x8, Pallas kernels: 680 us -> 602 us  [pack_call(): pl.pallas_call(kernel, out_shape=tuple(shapes), in_specs=[ANY] * len(inpu...]
where the time goes in v4:
time: 694 us; the launch traced here: 693 us
  Pallas kernels  625 us (90%)
  other arithmetic  40.8 us (6%)
  local copies, waits for them, and re-layouts  17.2 us (2%)
  blocking collectives  8.91 us (1%)
    pallas_call x8, Pallas kernels, pack_call(): pl.pallas_call(kernel, out_shape=tuple(shapes), in_specs=[ANY] * len(inpu...  602 us
    pallas_call x1, Pallas kernels, small_sums(): pl.pallas_call(kernel, out_shape=jax.ShapeDtypeStruct((tp_size, count, te...  23.2 us

profile of v4, /device:TPU:0, one launch (start us, length us, event | category | flops | bytes accessed | tf_op | source)
XLA Modules:
  0.0 692.6 jit_solution(16302853894511063712)
XLA Ops:
  4.7 1.3 broadcast_in_dim.61.refs_9_
  8.2 1.3 broadcast_in_dim.62.refs_4_.refs_11_
  9.5 3.7 fusion.6
  13.2 1.9 pad_maximum_fusion.3
  15.2 64.6 %shard_map.280 = (bf16[2048,2048]{1,0:T(8,128)(2,1)}, f32[2048,128]{1,0:T(8,128)}, f32[2048,128]{1,0:T(8,128)}, f32[2048,128]{1,0:T(8,128)}, bf16[2048,128]{1,0:...) custom-call(bf16[256,1024]{1,0:T(8,128)(2,1)} %refs_0_.2, ...), custom_call_target="tpu_custom_call" | custom-call | flops 3221225472 | bytes 33554432 | tf_op jit(solution)/shard_map/pallas_call | solution.py:1073
  80.8 1.7 pad.8.refs_16_.refs_13_
  82.5 63.8 %shard_map.281 = (bf16[2048,128]{1,0:T(8,128)(2,1)}, f32[8,2048]{1,0:T(8,128)}, bf16[2048,2048]{1,0:T(8,128)(2,1)}, bf16[1,512,512]{2,1,0:T(8,128)(2,1)}, bf16[1...) custom-call(bf16[256,1024]{1,0:T(8,128)(2,1)} %refs_0_.3, ...), custom_call_target="tpu_custom_call" | custom-call | flops 2147483648 | bytes 33554432 | tf_op jit(solution)/shard_map/pallas_call | solution.py:1073
  146.4 60.9 %shard_map.282 = (f32[256,1024]{1,0:T(8,128)}, bf16[1,512,512]{2,1,0:T(8,128)(2,1)}, bf16[1,512,512]{2,1,0:T(8,128)(2,1)}, bf16[1,512,512]{2,1,0:T(8,128)(2,1)},...) custom-call(bf16[2048,128]{1,0:T(8,128)(2,1)} %get-tuple-element.69.refs_0_.refs_4_, ...), custom_call_target="tpu_custom_call" | custom-call | flops 1073741824 | bytes 33554432 | tf_op jit(solution)/shard_map/pallas_call | solution.py:1073
  207.3 2.2 multiply_reduce_fusion.5
  209.5 2.4 psum.28
  212.9 63.7 %shard_map.283 = (bf16[2048,1024]{1,0:T(8,128)(2,1)}, bf16[2048,1024]{1,0:T(8,128)(2,1)}, bf16[2048,1024]{1,0:T(8,128)(2,1)}, bf16[2048,128]{1,0:T(8,128)(2,1)}, bf16[2048,2048]{1,0:T(8,128)(2,1)}) custom-call(bf16[256,1024]{1,0:T(8,128)(2,1)} %multiply_convert_fusion.refs_0_, bf16[16,1024,512]{2,1,0:T(8,128)(2,1)} %refs_3_.3, ...), custom_call_target="tpu_custom_call" | custom-call | flops 25769803776 | bytes 33554432 | tf_op jit(solution)/shard_map/pallas_call | solution.py:1073
  276.6 71.9 %shard_map.284 = (f32[256,1024]{1,0:T(8,128)}, bf16[1024,1152]{1,0:T(8,128)(2,1)}, bf16[1,1024,1152]{2,1,0:T(8,128)(2,1)}) custom-call(bf16[2048,1024]{1,0:T(8,128)(2,1)} %get-tuple-element.89.refs_0_, bf16[2048,1024]{1,0:T(8,128)(2,1)} %get-tuple-element.90.refs_1_.refs_3_, bf16[2048,128]{1,0:T(8,128)(2,1)} %get-tuple-element.91.refs_2_, ...), custom_call_target="tpu_custom_call" | custom-call | flops 25769803776 | bytes 33554432 | tf_op jit(solution)/shard_map/pallas_call | solution.py:1073
  348.5 2.4 multiply_reduce_fusion.2
  350.9 2.7 psum.29
  353.6 2.6 fusion.11
  356.1 88.7 %shard_map.285 = (bf16[2048,128]{1,0:T(8,128)(2,1)}, bf16[2048,2048]{1,0:T(8,128)(2,1)}, bf16[1024,1024]{1,0:T(8,128)(2,1)}, bf16[1,1024,1024]{2,1,0:T(8,128)(2,...) custom-call(bf16[256,1024]{1,0:T(8,128)(2,1)} %get-tuple-element.171.refs_0_, ...), custom_call_target="tpu_custom_call" | custom-call | flops 9663676416 | bytes 33554432 | tf_op jit(solution)/shard_map/pallas_call | solution.py:1073
  444.8 92.1 %shard_map.286 = (f32[256,1024]{1,0:T(8,128)}, bf16[2048,384]{1,0:T(8,128)(2,1)}, f32[2048,128]{1,0:T(8,128)}, f32[2048,128]{1,0:T(8,128)}, f32[2048,128]{1,0:T(...) custom-call(bf16[2048,1024]{1,0:T(8,128)(2,1)} %get-tuple-element.87.refs_5_.refs_0_, ...), custom_call_target="tpu_custom_call" | custom-call | flops 13958643712 | bytes 33554432 | tf_op jit(solution)/shard_map/pallas_call | solution.py:1073
  536.9 95.8 %shard_map.287 = (f32[256,1024]{1,0:T(8,128)}, bf16[8,128,512]{2,1,0:T(8,128)(2,1)}, bf16[8,128,1024]{2,1,0:T(8,128)(2,1)}) custom-call(bf16[2048,384]{1,0:T(8,128)(2,1)} %get-tuple-element.105.refs_0_, bf16[2048,384]{1,0:T(8,128)(2,1)} %get-tuple-element.106.refs_1_, bf16[2048,2048]{1,0:T(8,128)(2,1)} %get-tuple-element.107.refs_2_, ...), custom_call_target="tpu_custom_call" | custom-call | flops 7516192768 | bytes 33554432 | tf_op jit(solution)/shard_map/pallas_call | solution.py:1073
  632.8 1.6 multiply_reduce_fusion
  634.4 2.0 maximum_bitcast_fusion
  637.5 23.2 %shard_map.288 = f32[2,32,128]{2,1,0:T(8,128)} custom-call(f32[32,128]{1,0:T(8,128)} %select_maximum_fusion.src), custom_call_target="tpu_custom_call" | custom-call | tf_op jit(solution)/shard_map/pallas_call | solution.py:1158
  661.5 1.3 slice_bitcast_fusion
  664.8 1.7 fusion.12
  666.7 3.8 all-reduce.2
  670.5 2.9 fusion.2
  674.0 2.4 convert_bitcast_fusion
  677.4 1.2 copy.49
  679.6 1.2 copy.48
  681.9 1.2 copy.47
  684.1 2.6 convert.16
  687.1 2.6 convert.18
  690.0 2.6 convert.17
  (43 shorter events, 17.6 us)
Async XLA Ops:
  146.3 61.0 %copy-start = (bf16[256,1024]{1,0:T(8,128)(2,1)S(1)}, bf16[256,1024]{1,0:T(8,128)(2,1)}, u32[]{:S(2)}) copy-start(bf16[256,1024]{1,0:T(8,128)(2,1)} %refs_0_.2) | copy-start | bytes 1572868
  348.5 5.1 copy-start.2
  536.9 95.9 %copy-start.5 = (f32[256,1024]{1,0:T(8,128)S(1)}, f32[256,1024]{1,0:T(8,128)}, u32[]{:S(2)}) copy-start(f32[256,1024]{1,0:T(8,128)} %get-tuple-element.103) | copy-start | bytes 3145732
  632.8 3.7 copy-start.1
  632.8 4.1 copy-start.6
  684.1 2.6 copy-start.4
  687.1 2.6 copy-start.3

commit v5 on v4

--- a/solution.py
+++ b/solution.py
@@ -261,14 +261,6 @@
     def step(s):
         dist, k = s // CHUNKS, s % CHUNKS
 
-        @pl.when(dist + 1 < line)
-        def _():
-            from_line(dist + 1, k)
-
-        @pl.when(s < pack.steps)
-        def _():
-            from_pair(dist, k)
-
         @pl.when(s == lag)
         def _():
             before()
@@ -276,6 +268,14 @@
         turn = s - lag
 
         def side(i):
+            @pl.when(jnp.logical_and(i == 0, dist + 1 < line))
+            def _():
+                from_line(dist + 1, k)
+
+            @pl.when(jnp.logical_and(i == 1, s < pack.steps))
+            def _():
+                from_pair(dist, k)
+
             late = turn - i
             node, late_k = a ^ (late // CHUNKS), late % CHUNKS
 
@@ -331,7 +331,7 @@
     ]
 
 
-def scatter_steps(pack, scratch, everyone, begin, before, compute, jobs, finish):
+def scatter_steps(pack, scratch, everyone, begin, before, compute, jobs, tail, finish):
     (full, sib_buf, pair_buf, line_buf, tp_send, pair_send, line_send, tp_recv, pair_recv, line_recv) = scratch
     line, t, a, b = pack.line, pack.t, pack.a, pack.b
     ctx_size = 2 * line
@@ -439,6 +439,14 @@
 
             loop(2, side)
 
+        if tail is not None:
+            turn = s - (pack.steps - 1)
+            share = ctx_size * CHUNKS // 4
+
+            @pl.when(jnp.logical_and(turn >= 0, turn < 4))
+            def _():
+                loop(share, lambda i: tail(turn * share + i))
+
         later = s - 4
 
         @pl.when(later >= 0)
@@ -546,8 +554,9 @@
 
 
 class Deal:
-    def __init__(self, own, far):
-        self.own, self.far = own, far
+    def __init__(self, own, far, parts=1):
+        self.own, self.far, self.parts = own, far, parts
+        self.width = own.shape[1] // parts
 
 
 class Tiles:
@@ -919,31 +928,33 @@
 
             loop(pieces, sent)
 
+        deal_first = [sum(d.parts for d in deals[:i]) for i in range(len(deals))]
+
         def deal_blocks(i, turn, go_away, stay):
             own_buf, landing = held[first_deal + 2 * i], deal_outs[i]
+            parts, width = deals[i].parts, deals[i].width
             for split in range(splits):
                 owner = ((mine["ctx"] // splits) ^ pick(deal_order, turn)) * splits + split
-                here = own_buf.at[
-                    pl.ds(pl.multiple_of(owner * own_features, own_features), own_features), :
-                ]
-                there = landing.at[mine["ctx"]]
-                sem = deal_send.at[(i * own_tiles + turn) * splits + split]
+                window = pl.ds(pl.multiple_of(owner * own_features, own_features), own_features)
+                copies = []
+                for part in range(parts):
+                    here = own_buf.at[window, pl.ds(part * width, width)]
+                    there = landing.at[mine["ctx"] * parts + part]
+                    sem = deal_send.at[
+                        (deal_first[i] + part) * own_tiles * splits + turn * splits + split
+                    ]
+                    arrived = deal_recv.at[(deal_first[i] + part) * ctx_size + mine["ctx"]]
+                    copies.append((here, there, sem, arrived))
 
                 @pl.when(owner != mine["ctx"])
                 def _():
-                    go_away(
-                        remote(
-                            here,
-                            there,
-                            sem,
-                            deal_recv.at[i * ctx_size + mine["ctx"]],
-                            {"ctx": owner},
-                        )
-                    )
+                    for copy in copies:
+                        go_away(remote(*copy, {"ctx": owner}))
 
                 @pl.when(owner == mine["ctx"])
                 def _():
-                    stay(pltpu.make_async_copy(here, there, sem))
+                    for here, there, sem, _ in copies:
+                        stay(pltpu.make_async_copy(here, there, sem))
 
         def deal_out(order):
             if not deals:
@@ -974,9 +985,10 @@
             for i in range(len(deals)):
                 for shift in range(1, ctx_size):
                     place = mine["ctx"] ^ shift
-                    landed = deal_outs[i].at[place]
-                    sem = deal_recv.at[i * ctx_size + place]
-                    remote(landed, landed, deal_send.at[0], sem, {"ctx": place}).wait_recv()
+                    for part in range(deals[i].parts):
+                        landed = deal_outs[i].at[place * deals[i].parts + part]
+                        sem = deal_recv.at[(deal_first[i] + part) * ctx_size + place]
+                        remote(landed, landed, deal_send.at[0], sem, {"ctx": place}).wait_recv()
 
         for load in loads:
             load.start()
@@ -1008,9 +1020,18 @@
             def finish(k, total):
                 sum_ref[pl.ds(pl.multiple_of(k * pack.chunk, pack.chunk), pack.chunk), :] = total
 
-            scatter_steps(pack, scratch, everyone, begin, before, compute, jobs, finish)
-        if last is not None:
-            last(held + swap_bufs, stage, total_refs, pack.chunk)
+            def tail(i):
+                last(
+                    pl.ds(pl.multiple_of(i * pack.chunk, pack.chunk), pack.chunk),
+                    held + swap_bufs,
+                    stage,
+                    total_refs,
+                )
+
+            scatter_steps(
+                pack, scratch, everyone, begin, before, compute, jobs,
+                None if last is None else tail, finish,
+            )
         ends = []
         for i, out in enumerate(outs):
             if out.late:
@@ -1056,7 +1077,9 @@
         shapes.append(jax.ShapeDtypeStruct((part_features, make.width), low))
         shapes.append(jax.ShapeDtypeStruct((packs - 1, part_features, make.width), low))
     for deal in deals:
-        shapes.append(jax.ShapeDtypeStruct((ctx_size, own_features, deal.own.shape[1]), low))
+        shapes.append(
+            jax.ShapeDtypeStruct((ctx_size * deal.parts, own_features, deal.width), low)
+        )
     out_specs = [ANY] * len(shapes)
     if not gather:
         shapes = [jax.ShapeDtypeStruct(shape, jnp.float32)] + shapes
@@ -1095,8 +1118,8 @@
         + [
             dma((max(1, len(makes)) * pieces,)),
             dma((max(1, len(makes)) * pieces,)),
-            dma((max(1, len(deals)) * own_tiles * splits,)),
-            dma((max(1, len(deals)) * ctx_size,)),
+            dma((max(1, sum(deal.parts for deal in deals)) * own_tiles * splits,)),
+            dma((max(1, sum(deal.parts for deal in deals)) * ctx_size,)),
         ],
         compiler_params=pltpu.CompilerParams(
             collective_id=collective_id, has_side_effects=True, vmem_limit_bytes=VMEM_LIMIT
@@ -1245,7 +1268,7 @@
 
     halves = [(slot, half) for slot in range(own_experts) for half in range(2)]
     expert_ships = [half_ship(w, *which) for w in (w_gate, w_up, w_down) for which in halves]
-    first_ships = len(expert_ships) // 6
+    first_ships = len(expert_ships) // 4
     second_ships = first_ships + (len(expert_ships) - first_ships) // 2
 
     def expert_weight(weight, far):
@@ -1504,13 +1527,10 @@
             total = total + nt_dot(units_of(up_grad, window, slot), up_w[slot])
         return total, ()
 
-    def gate_tile(window, held):
-        features = held[6][:, window]
-        return jnp.concatenate(
-            [tn_dot(features, held[0][...]), tn_dot(features, held[2][...])], axis=1
-        )
-
-    grad_second, gate_own, gate_far = pack_call(
+    def feature_tile(left, right):
+        return lambda window, held: tn_dot(held[left][:, window], held[right][...])
+
+    grad_second, gate_own, gate_far, router_own, router_far = pack_call(
         sizes,
         own_shape,
         back,
@@ -1525,16 +1545,11 @@
             router_pad,
             normed_second,
         ),
-        makes=(Make(own_units + lanes, width_all, gate_tile, True),),
-    )
-
-    def by_expert(blocks):
-        count, rows = blocks.shape[:2]
-        return (
-            jnp.swapaxes(blocks.reshape(count, rows, own_experts, hidden_units), 1, 2)
-            .reshape(expert_count, rows, hidden_units)
-            .astype(wide)
-        )
+        makes=(
+            Make(own_units, width_all, feature_tile(6, 0), True),
+            Make(lanes, width_all, feature_tile(6, 2), True),
+        ),
+    )
 
     def by_head(blocks):
         rows = blocks.shape[1]
@@ -1552,14 +1567,24 @@
         - middle * inv_second**3 * second_inner / width_all
     )
 
+    half_units = own_units // 2
+
+    def down_tile(half):
+        return lambda window, held: tn_dot(
+            held[3][:, window], held[4][:, pl.ds(half * half_units, half_units)]
+        )
+
     (
         grad_attended,
         grad_middle_all,
         up_own,
         up_far,
-        down_own,
-        down_away,
+        first_own,
+        first_far,
+        second_own,
+        second_away,
         gate_blocks,
+        router_blocks,
     ) = pack_call(
         sizes,
         own_shape,
@@ -1571,26 +1596,16 @@
         outs=(Out(head_dim, slim),),
         keep=True,
         makes=(
-            Make(
-                own_units,
-                width_all,
-                lambda window, held: tn_dot(held[1][:, window], held[2][...]),
-                True,
-            ),
-            Make(
-                own_units,
-                width_all,
-                lambda window, held: tn_dot(held[3][:, window], held[4][...]),
-                False,
-            ),
+            Make(own_units, width_all, feature_tile(1, 2), True),
+            Make(half_units, width_all, down_tile(0), True),
+            Make(half_units, width_all, down_tile(1), False),
         ),
-        deals=(Deal(gate_own, gate_far),),
-    )
-    grad_gate = by_expert(gate_blocks[:, :, :own_units])
+        deals=(Deal(gate_own, gate_far, own_experts), Deal(router_own, router_far)),
+    )
+    grad_gate = gate_blocks.astype(wide)
     grad_router = row_total(
-        jnp.sum(gate_blocks[:, :, own_units : own_units + expert_count].astype(wide), axis=0).T
-    )
-
+        jnp.sum(router_blocks[:, :, :expert_count].astype(wide), axis=0).T
+    )
 
     def attend_back(window, held, totals):
         mixed_ref, down_w, query, key, key_t, value, grad_att = held[:7]
@@ -1612,33 +1627,26 @@
         )
         return total, ()
 
-    def unturn_all(held, stage, totals, chunk):
+    def unturn(window, held, stage, totals):
         raws, cos_table, sin_table, gains = held[10:12], held[12], held[13], held[14:16]
         grad_rots, grad_value, gain_sums = totals[:2], totals[2], totals[3]
-
-        def unturn(i):
-            window = pl.ds(pl.multiple_of(i * chunk, chunk), chunk)
-            cos_rows, sin_rows = cos_table[window, :], sin_table[window, :]
-            for which in range(2):
-                grad_rot = grad_rots[which][window, :] * score_scale
-                raw = raws[which][window, :]
-                inverse = lax.rsqrt(jnp.mean(raw * raw, axis=1, keepdims=True) + norm_eps)
-                grad_normed = grad_rot * cos_rows + pltpu.roll(
-                    grad_rot * sin_rows, head_dim // 2, 1
-                )
-                weighted = grad_normed * gains[which][...]
-                grad_raw = inverse * weighted - raw * inverse**3 * jnp.mean(
-                    weighted * raw, axis=1, keepdims=True
-                )
-                stage[0][window, pl.ds(which * head_dim, head_dim)] = grad_raw.astype(slim)
-                gain_sums[pl.ds(which, 1), :] += jnp.sum(
-                    grad_normed * raw * inverse, axis=0, keepdims=True
-                )
-            stage[0][window, pl.ds(2 * head_dim, head_dim)] = grad_value[window, :].astype(slim)
-
-        loop(pack_rows // chunk, unturn)
-
-    expert_branch, grad_qkv_low, _, _, _, gain_sums, down_far, up_blocks = pack_call(
+        cos_rows, sin_rows = cos_table[window, :], sin_table[window, :]
+        for which in range(2):
+            grad_rot = grad_rots[which][window, :] * score_scale
+            raw = raws[which][window, :]
+            inverse = lax.rsqrt(jnp.mean(raw * raw, axis=1, keepdims=True) + norm_eps)
+            grad_normed = grad_rot * cos_rows + pltpu.roll(grad_rot * sin_rows, head_dim // 2, 1)
+            weighted = grad_normed * gains[which][...]
+            grad_raw = inverse * weighted - raw * inverse**3 * jnp.mean(
+                weighted * raw, axis=1, keepdims=True
+            )
+            stage[0][window, pl.ds(which * head_dim, head_dim)] = grad_raw.astype(slim)
+            gain_sums[pl.ds(which, 1), :] += jnp.sum(
+                grad_normed * raw * inverse, axis=0, keepdims=True
+            )
+        stage[0][window, pl.ds(2 * head_dim, head_dim)] = grad_value[window, :].astype(slim)
+
+    expert_branch, grad_qkv_low, _, _, _, gain_sums, second_far, up_blocks, first_blocks = pack_call(
         sizes,
         own_shape,
         attend_back,
@@ -1669,19 +1677,19 @@
             ((pack_rows, head_dim), wide),
             ((8, head_dim), wide),
         ),
-        last=unturn_all,
+        last=unturn,
         ships=(
             Ship(
                 "fsdp",
-                down_away,
+                second_away,
                 lambda ref, shift: ref.at[shift - 1],
-                (part_width, own_units),
+                (part_width, half_units),
             ),
         ),
-        deals=(Deal(up_own, up_far),),
+        deals=(Deal(up_own, up_far, own_experts), Deal(first_own, first_far, own_experts // 2)),
     )
     hidden_out = (middle + expert_branch).astype(slim)
-    grad_up = by_expert(up_blocks)
+    grad_up = up_blocks.astype(wide)
 
     def last_tile(window, held):
         return jnp.concatenate(
@@ -1692,7 +1700,7 @@
             axis=1,
         )
 
-    grad_first, last_blocks, down_blocks = pack_call(
+    grad_first, last_blocks, second_blocks = pack_call(
         sizes,
         own_shape,
         lambda window, held, totals: (nt_dot(held[0][window, :], held[1][...]), ()),
@@ -1700,9 +1708,14 @@
         2 * pack_rows * width_all * 7 * head_dim,
         resident=(grad_qkv_low, qkv_weight, normed_first, grad_middle_all, attended_low),
         tiles=Tiles(4 * head_dim, width_all, last_tile),
-        deals=(Deal(down_own, down_far),),
-    )
-    grad_down = by_expert(down_blocks)
+        deals=(Deal(second_own, second_far, own_experts // 2),),
+    )
+    by_halves = (ctx_size, own_experts // 2) + first_blocks.shape[1:]
+    grad_down = (
+        jnp.concatenate([first_blocks.reshape(by_halves), second_blocks.reshape(by_halves)], axis=1)
+        .reshape((expert_count,) + first_blocks.shape[1:])
+        .astype(wide)
+    )
     grad_query, grad_key, grad_value, grad_out = (
         by_head(last_blocks[:, :, i * head_dim : (i + 1) * head_dim]) for i in range(4)
     )

time: 694 us -> 681 us (0.981)
  Pallas kernels: 625 us -> 616 us
where the time goes in v5:
time: 681 us; the launch traced here: 680 us
  Pallas kernels  616 us (90%)
  other arithmetic  39.3 us (6%)
  local copies, waits for them, and re-layouts  14.7 us (2%)
  blocking collectives  8.91 us (1%)
    pallas_call x8, Pallas kernels, pack_call(): pl.pallas_call(kernel, out_shape=tuple(shapes), in_specs=[ANY] * len(inpu...  600 us
    pallas_call x1, Pallas kernels, small_sums(): pl.pallas_call(kernel, out_shape=jax.ShapeDtypeStruct((tp_size, count, te...  16.8 us

profile of v5, /device:TPU:0, one launch (start us, length us, event | category | flops | bytes accessed | tf_op | source)
XLA Modules:
  0.0 680.1 jit_solution(12847624706634628185)
XLA Ops:
  2.1 1.2 bitcast_convert_fusion
  4.7 1.3 broadcast_in_dim.61.refs_9_
  8.2 1.3 broadcast_in_dim.62.refs_4_.refs_11_
  9.5 3.7 fusion.6
  13.2 1.9 pad_maximum_fusion
  15.2 68.5 %shard_map.280 = (bf16[2048,2048]{1,0:T(8,128)(2,1)}, f32[2048,128]{1,0:T(8,128)}, f32[2048,128]{1,0:T(8,128)}, f32[2048,128]{1,0:T(8,128)}, bf16[2048,128]{1,0:...) custom-call(bf16[256,1024]{1,0:T(8,128)(2,1)} %refs_0_.2, ...), custom_call_target="tpu_custom_call" | custom-call | flops 3221225472 | bytes 33554432 | tf_op jit(solution)/shard_map/pallas_call | solution.py:1096
  83.6 1.1 dynamic-slice_reduce_fusion
  84.7 1.7 pad.8.refs_16_.refs_13_
  86.4 53.5 %shard_map.281 = (bf16[2048,128]{1,0:T(8,128)(2,1)}, f32[8,2048]{1,0:T(8,128)}, bf16[2048,2048]{1,0:T(8,128)(2,1)}, bf16[1,512,512]{2,1,0:T(8,128)(2,1)}, bf16[1...) custom-call(bf16[256,1024]{1,0:T(8,128)(2,1)} %refs_0_.3, ...), custom_call_target="tpu_custom_call" | custom-call | flops 2147483648 | bytes 33554432 | tf_op jit(solution)/shard_map/pallas_call | solution.py:1096
  139.9 64.8 %shard_map.282 = (f32[256,1024]{1,0:T(8,128)}, bf16[1,512,512]{2,1,0:T(8,128)(2,1)}, bf16[1,512,512]{2,1,0:T(8,128)(2,1)}, bf16[1,512,512]{2,1,0:T(8,128)(2,1)},...) custom-call(bf16[2048,128]{1,0:T(8,128)(2,1)} %get-tuple-element.75.refs_0_.refs_4_, ...), custom_call_target="tpu_custom_call" | custom-call | flops 1073741824 | bytes 33554432 | tf_op jit(solution)/shard_map/pallas_call | solution.py:1096
  204.8 2.2 multiply_reduce_fusion.5
  206.9 2.4 psum.28
  210.3 60.5 %shard_map.283 = (bf16[2048,1024]{1,0:T(8,128)(2,1)}, bf16[2048,1024]{1,0:T(8,128)(2,1)}, bf16[2048,1024]{1,0:T(8,128)(2,1)}, bf16[2048,128]{1,0:T(8,128)(2,1)}, bf16[2048,2048]{1,0:T(8,128)(2,1)}) custom-call(bf16[256,1024]{1,0:T(8,128)(2,1)} %multiply_convert_fusion.refs_0_, bf16[16,1024,512]{2,1,0:T(8,128)(2,1)} %refs_3_.3, ...), custom_call_target="tpu_custom_call" | custom-call | flops 25769803776 | bytes 33554432 | tf_op jit(solution)/shard_map/pallas_call | solution.py:1096
  270.9 74.7 %shard_map.284 = (f32[256,1024]{1,0:T(8,128)}, bf16[1024,1024]{1,0:T(8,128)(2,1)}, bf16[1,1024,1024]{2,1,0:T(8,128)(2,1)}, bf16[1024,128]{1,0:T(8,128)(2,1)}, bf16[1,1024,128]{2,1,0:T(8,128)(2,1)}) custom-call(bf16[2048,1024]{1,0:T(8,128)(2,1)} %get-tuple-element.95.refs_0_, bf16[2048,1024]{1,0:T(8,128)(2,1)} %get-tuple-element.96.refs_1_.refs_3_, ...), custom_call_target="tpu_custom_call" | custom-call | flops 25769803776 | bytes 33554432 | tf_op jit(solution)/shard_map/pallas_call | solution.py:1096
  345.6 2.3 multiply_reduce_fusion.2
  347.9 2.7 psum.29
  350.6 2.5 fusion.11
  353.1 92.1 %shard_map.285 = (bf16[2048,128]{1,0:T(8,128)(2,1)}, bf16[2048,2048]{1,0:T(8,128)(2,1)}, bf16[1024,1024]{1,0:T(8,128)(2,1)}, bf16[1,1024,1024]{2,1,0:T(8,128)(2,...) custom-call(bf16[256,1024]{1,0:T(8,128)(2,1)} %get-tuple-element.183, ...), custom_call_target="tpu_custom_call" | custom-call | flops 9663676416 | bytes 33554432 | tf_op jit(solution)/shard_map/pallas_call | solution.py:1096
  445.2 101.0 %shard_map.286 = (f32[256,1024]{1,0:T(8,128)}, bf16[2048,384]{1,0:T(8,128)(2,1)}, f32[2048,128]{1,0:T(8,128)}, f32[2048,128]{1,0:T(8,128)}, f32[2048,128]{1,0:T(...) custom-call(bf16[2048,1024]{1,0:T(8,128)(2,1)} %get-tuple-element.93, ...), custom_call_target="tpu_custom_call" | custom-call | flops 13958643712 | bytes 33554432 | tf_op jit(solution)/shard_map/pallas_call | solution.py:1096
  546.2 84.4 %shard_map.287 = (f32[256,1024]{1,0:T(8,128)}, bf16[8,128,512]{2,1,0:T(8,128)(2,1)}, bf16[8,128,512]{2,1,0:T(8,128)(2,1)}) custom-call(bf16[2048,384]{1,0:T(8,128)(2,1)} %get-tuple-element.115.refs_0_, bf16[2048,384]{1,0:T(8,128)(2,1)} %get-tuple-element.116.refs_1_, bf16[2048,2048]{1,0:T(8,128)(2,1)} %get-tuple-element.117.refs_2_, ...), custom_call_target="tpu_custom_call" | custom-call | flops 7516192768 | bytes 33554432 | tf_op jit(solution)/shard_map/pallas_call | solution.py:1096
  630.6 2.9 multiply_reduce_fusion
  633.5 2.0 maximum_bitcast_fusion
  635.5 1.6 fusion.5
  637.7 16.8 %shard_map.288 = f32[2,32,128]{2,1,0:T(8,128)} custom-call(f32[32,128]{1,0:T(8,128)} %select_maximum_fusion.src), custom_call_target="tpu_custom_call" | custom-call | tf_op jit(solution)/shard_map/pallas_call | solution.py:1181
  655.2 1.3 slice_bitcast_fusion
  657.6 3.8 all-reduce.2
  661.4 2.6 fusion.2
  664.6 1.4 convert_bitcast_fusion
  670.7 1.5 maximum_convert_fusion
  672.2 2.7 copy.53
  674.9 2.6 convert_element_type.71
  677.5 2.6 convert_element_type.70
  (36 shorter events, 13.7 us)
Async XLA Ops:
  139.9 64.8 %copy-start = (bf16[256,1024]{1,0:T(8,128)(2,1)S(1)}, bf16[256,1024]{1,0:T(8,128)(2,1)}, u32[]{:S(2)}) copy-start(bf16[256,1024]{1,0:T(8,128)(2,1)} %refs_0_.2) | copy-start | bytes 1572868
  630.6 6.5 copy-start.5
  630.6 27.0 %copy-start.4 = (bf16[8,128,128]{2,1,0:T(8,128)(2,1)S(1)}, bf16[8,128,128]{2,1,0:T(8,128)(2,1)}, u32[]{:S(2)}) copy-start(bf16[8,128,128]{2,1,0:T(8,128)(2,1)} %get-tuple-element.124) | copy-start | bytes 786436
  666.1 4.6 copy-start.3
  672.2 2.7 copy-start.2
  674.9 2.6 copy-start.1

commit v6 on v5

--- a/solution.py
+++ b/solution.py
@@ -585,7 +585,8 @@
     tiles=None,
     makes=(),
     deals=(),
-    lag=1,
+    lag=0,
+    needed=None,
 ):
     packs, ctx_size, tp_size = sizes
     rows, cols = shape
@@ -714,6 +715,14 @@
                 )
             index += axis_size[ship.axis]
 
+        prompt = sum(len(copies) for copies in part_list[:needed])
+
+        def await_rest(order):
+            @pl.when(order == 0)
+            def _():
+                for load in loads[prompt:]:
+                    load.wait()
+
         def begin():
             for copy in swap_copies + ship_local:
                 copy.start()
@@ -723,7 +732,7 @@
         def before():
             for ref in total_refs:
                 ref[...] = jnp.zeros_like(ref)
-            for load in loads:
+            for load in loads[:prompt]:
                 load.wait()
             for copy in swap_copies:
                 copy.wait()
@@ -999,6 +1008,7 @@
                 put(window, piece(scratch[0][window, :], window, held + swap_bufs, total_refs))
                 for store in stores(row0, index):
                     store.start()
+                await_rest(order)
                 deal_out(order)
                 make_tile(order)
                 make_parts(order)
@@ -1013,6 +1023,7 @@
                 return rows_value.astype(jnp.bfloat16)
 
             def jobs(order):
+                await_rest(order)
                 deal_out(order)
                 make_tile(order)
                 make_parts(order)
@@ -1409,7 +1420,7 @@
         ),
         ships=expert_ships[:first_ships]
         + [Ship("ctx", expert_ids.T, lambda ref, shift: ref, (top_count, tok_rows))],
-        lag=3,
+        lag=2,
     )
     router_pad = jnp.pad(router_full, ((0, lanes - expert_count), (0, 0)))
 
@@ -1545,6 +1556,7 @@
             router_pad,
             normed_second,
         ),
+        needed=6,
         makes=(
             Make(own_units, width_all, feature_tile(6, 0), True),
             Make(lanes, width_all, feature_tile(6, 2), True),
@@ -1601,6 +1613,7 @@
             Make(half_units, width_all, down_tile(1), False),
         ),
         deals=(Deal(gate_own, gate_far, own_experts), Deal(router_own, router_far)),
+        needed=1,
     )
     grad_gate = gate_blocks.astype(wide)
     grad_router = row_total(
@@ -1709,6 +1722,7 @@
         resident=(grad_qkv_low, qkv_weight, normed_first, grad_middle_all, attended_low),
         tiles=Tiles(4 * head_dim, width_all, last_tile),
         deals=(Deal(second_own, second_far, own_experts // 2),),
+        needed=2,
     )
     by_halves = (ctx_size, own_experts // 2) + first_blocks.shape[1:]
     grad_down = (

time: 681 us -> 672 us (0.987)
  Pallas kernels: 616 us -> 607 us
    pallas_call x8, Pallas kernels: 600 us -> 591 us  [pack_call(): pl.pallas_call(kernel, out_shape=tuple(shapes), in_specs=[ANY] * len(inpu...]
where the time goes in v6:
time: 672 us; the launch traced here: 671 us
  Pallas kernels  607 us (90%)
  other arithmetic  39.3 us (6%)
  local copies, waits for them, and re-layouts  14.7 us (2%)
  blocking collectives  8.91 us (1%)
    pallas_call x8, Pallas kernels, pack_call(): pl.pallas_call(kernel, out_shape=tuple(shapes), in_specs=[ANY] * len(inpu...  591 us
    pallas_call x1, Pallas kernels, small_sums(): pl.pallas_call(kernel, out_shape=jax.ShapeDtypeStruct((tp_size, count, te...  16.5 us

profile of v6, /device:TPU:0, one launch (start us, length us, event | category | flops | bytes accessed | tf_op | source)
XLA Modules:
  0.0 671.2 jit_solution(410897339137145614)
XLA Ops:
  2.1 1.2 bitcast_convert_fusion
  4.7 1.3 broadcast_in_dim.61.refs_9_
  8.2 1.3 broadcast_in_dim.62.refs_4_.refs_11_
  9.5 3.7 fusion.6
  13.2 1.9 pad_maximum_fusion
  15.2 68.5 %shard_map.280 = (bf16[2048,2048]{1,0:T(8,128)(2,1)}, f32[2048,128]{1,0:T(8,128)}, f32[2048,128]{1,0:T(8,128)}, f32[2048,128]{1,0:T(8,128)}, bf16[2048,128]{1,0:...) custom-call(bf16[256,1024]{1,0:T(8,128)(2,1)} %refs_0_.2, ...), custom_call_target="tpu_custom_call" | custom-call | flops 3221225472 | bytes 33554432 | tf_op jit(solution)/shard_map/pallas_call | solution.py:1107
  83.6 1.1 dynamic-slice_reduce_fusion
  84.7 1.7 pad.8.refs_16_.refs_13_
  86.4 51.7 %shard_map.281 = (bf16[2048,128]{1,0:T(8,128)(2,1)}, f32[8,2048]{1,0:T(8,128)}, bf16[2048,2048]{1,0:T(8,128)(2,1)}, bf16[1,512,512]{2,1,0:T(8,128)(2,1)}, bf16[1...) custom-call(bf16[256,1024]{1,0:T(8,128)(2,1)} %refs_0_.3, ...), custom_call_target="tpu_custom_call" | custom-call | flops 2147483648 | bytes 33554432 | tf_op jit(solution)/shard_map/pallas_call | solution.py:1107
  138.1 64.1 %shard_map.282 = (f32[256,1024]{1,0:T(8,128)}, bf16[1,512,512]{2,1,0:T(8,128)(2,1)}, bf16[1,512,512]{2,1,0:T(8,128)(2,1)}, bf16[1,512,512]{2,1,0:T(8,128)(2,1)},...) custom-call(bf16[2048,128]{1,0:T(8,128)(2,1)} %get-tuple-element.75.refs_0_.refs_4_, ...), custom_call_target="tpu_custom_call" | custom-call | flops 1073741824 | bytes 33554432 | tf_op jit(solution)/shard_map/pallas_call | solution.py:1107
  202.3 2.2 multiply_reduce_fusion.5
  204.4 2.4 psum.28
  207.8 57.0 %shard_map.283 = (bf16[2048,1024]{1,0:T(8,128)(2,1)}, bf16[2048,1024]{1,0:T(8,128)(2,1)}, bf16[2048,1024]{1,0:T(8,128)(2,1)}, bf16[2048,128]{1,0:T(8,128)(2,1)}, bf16[2048,2048]{1,0:T(8,128)(2,1)}) custom-call(bf16[256,1024]{1,0:T(8,128)(2,1)} %multiply_convert_fusion.refs_0_, bf16[16,1024,512]{2,1,0:T(8,128)(2,1)} %refs_3_.3, ...), custom_call_target="tpu_custom_call" | custom-call | flops 25769803776 | bytes 33554432 | tf_op jit(solution)/shard_map/pallas_call | solution.py:1107
  264.9 74.2 %shard_map.284 = (f32[256,1024]{1,0:T(8,128)}, bf16[1024,1024]{1,0:T(8,128)(2,1)}, bf16[1,1024,1024]{2,1,0:T(8,128)(2,1)}, bf16[1024,128]{1,0:T(8,128)(2,1)}, bf16[1,1024,128]{2,1,0:T(8,128)(2,1)}) custom-call(bf16[2048,1024]{1,0:T(8,128)(2,1)} %get-tuple-element.95.refs_0_, bf16[2048,1024]{1,0:T(8,128)(2,1)} %get-tuple-element.96.refs_1_.refs_3_, ...), custom_call_target="tpu_custom_call" | custom-call | flops 25769803776 | bytes 33554432 | tf_op jit(solution)/shard_map/pallas_call | solution.py:1107
  339.0 2.3 multiply_reduce_fusion.2
  341.3 2.7 psum.29
  344.0 2.5 fusion.11
  346.5 90.7 %shard_map.285 = (bf16[2048,128]{1,0:T(8,128)(2,1)}, bf16[2048,2048]{1,0:T(8,128)(2,1)}, bf16[1024,1024]{1,0:T(8,128)(2,1)}, bf16[1,1024,1024]{2,1,0:T(8,128)(2,...) custom-call(bf16[256,1024]{1,0:T(8,128)(2,1)} %get-tuple-element.183, ...), custom_call_target="tpu_custom_call" | custom-call | flops 9663676416 | bytes 33554432 | tf_op jit(solution)/shard_map/pallas_call | solution.py:1107
  437.3 101.1 %shard_map.286 = (f32[256,1024]{1,0:T(8,128)}, bf16[2048,384]{1,0:T(8,128)(2,1)}, f32[2048,128]{1,0:T(8,128)}, f32[2048,128]{1,0:T(8,128)}, f32[2048,128]{1,0:T(...) custom-call(bf16[2048,1024]{1,0:T(8,128)(2,1)} %get-tuple-element.93, ...), custom_call_target="tpu_custom_call" | custom-call | flops 13958643712 | bytes 33554432 | tf_op jit(solution)/shard_map/pallas_call | solution.py:1107
  538.4 83.6 %shard_map.287 = (f32[256,1024]{1,0:T(8,128)}, bf16[8,128,512]{2,1,0:T(8,128)(2,1)}, bf16[8,128,512]{2,1,0:T(8,128)(2,1)}) custom-call(bf16[2048,384]{1,0:T(8,128)(2,1)} %get-tuple-element.115.refs_0_, bf16[2048,384]{1,0:T(8,128)(2,1)} %get-tuple-element.116.refs_1_, bf16[2048,2048]{1,0:T(8,128)(2,1)} %get-tuple-element.117.refs_2_, ...), custom_call_target="tpu_custom_call" | custom-call | flops 7516192768 | bytes 33554432 | tf_op jit(solution)/shard_map/pallas_call | solution.py:1107
  622.0 2.9 multiply_reduce_fusion
  624.9 2.0 maximum_bitcast_fusion
  626.9 1.6 fusion.5
  629.1 16.5 %shard_map.288 = f32[2,32,128]{2,1,0:T(8,128)} custom-call(f32[32,128]{1,0:T(8,128)} %select_maximum_fusion.src), custom_call_target="tpu_custom_call" | custom-call | tf_op jit(solution)/shard_map/pallas_call | solution.py:1192
  646.3 1.3 slice_bitcast_fusion
  648.7 3.8 all-reduce.2
  652.5 2.6 fusion.2
  655.7 1.4 convert_bitcast_fusion
  661.8 1.5 maximum_convert_fusion
  663.3 2.7 copy.53
  666.0 2.6 convert_element_type.71
  668.6 2.6 convert_element_type.70
  (36 shorter events, 13.7 us)
Async XLA Ops:
  138.1 64.1 %copy-start = (bf16[256,1024]{1,0:T(8,128)(2,1)S(1)}, bf16[256,1024]{1,0:T(8,128)(2,1)}, u32[]{:S(2)}) copy-start(bf16[256,1024]{1,0:T(8,128)(2,1)} %refs_0_.2) | copy-start | bytes 1572868
  621.9 6.5 copy-start.5
  621.9 26.7 %copy-start.4 = (bf16[8,128,128]{2,1,0:T(8,128)(2,1)S(1)}, bf16[8,128,128]{2,1,0:T(8,128)(2,1)}, u32[]{:S(2)}) copy-start(bf16[8,128,128]{2,1,0:T(8,128)(2,1)} %get-tuple-element.124) | copy-start | bytes 786436
  657.2 4.6 copy-start.3
  663.3 2.7 copy-start.2
  666.0 2.6 copy-start.1

commit v7 on v6

--- a/solution.py
+++ b/solution.py
@@ -25,6 +25,10 @@
     inv_freq = rope_base ** (-(jnp.arange(half_dim, dtype=jnp.float32) * 2.0 / head_dim))
     angle_grid = pack_spots.astype(jnp.float32)[:, None] * inv_freq[None, :]
     cosine, sine = jnp.cos(angle_grid), jnp.sin(angle_grid)
+    return cosine, sine
+
+
+def full_turn(cosine, sine):
     return jnp.concatenate([cosine, cosine], axis=1), jnp.concatenate([-sine, sine], axis=1)
 
 
@@ -1316,7 +1320,7 @@
         inverse = lax.rsqrt(jnp.mean(hidden * hidden, axis=1, keepdims=True) + norm_eps)
         normed = (hidden * inverse * gain[...].astype(wide)).astype(slim)
         raw = nn_dot(normed, weight[...])
-        cos_rows, sin_rows = cos_table[window, :], sin_table[window, :]
+        cos_rows, sin_rows = full_turn(cos_table[window, :], sin_table[window, :])
 
         def prepare(raw_proj, gain_vec):
             inv = lax.rsqrt(jnp.mean(raw_proj * raw_proj, axis=1, keepdims=True) + norm_eps)
@@ -1643,7 +1647,7 @@
     def unturn(window, held, stage, totals):
         raws, cos_table, sin_table, gains = held[10:12], held[12], held[13], held[14:16]
         grad_rots, grad_value, gain_sums = totals[:2], totals[2], totals[3]
-        cos_rows, sin_rows = cos_table[window, :], sin_table[window, :]
+        cos_rows, sin_rows = full_turn(cos_table[window, :], sin_table[window, :])
         for which in range(2):
             grad_rot = grad_rots[which][window, :] * score_scale
             raw = raws[which][window, :]

time: 672 us -> 671 us (level)
  no operation moved by 1% of the time
where the time goes in v7:
time: 671 us
  Pallas kernels  607 us (90%)
  other arithmetic  39.2 us (6%)
  local copies, waits for them, and re-layouts  14.7 us (2%)
  blocking collectives  8.65 us (1%)
    pallas_call x8, Pallas kernels, pack_call(): pl.pallas_call(kernel, out_shape=tuple(shapes), in_specs=[ANY] * len(inpu...  591 us
    pallas_call x1, Pallas kernels, small_sums(): pl.pallas_call(kernel, out_shape=jax.ShapeDtypeStruct((tp_size, count, te...  16.3 us

profile of v7, /device:TPU:0, one launch (start us, length us, event | category | flops | bytes accessed | tf_op | source)
XLA Modules:
  0.0 670.6 jit_solution(673403937644839350)
XLA Ops:
  2.1 1.2 bitcast_convert_fusion
  4.7 1.3 broadcast_in_dim.61.refs_9_
  8.2 1.3 broadcast_in_dim.62.refs_4_.refs_11_
  9.5 5.5 multiply_sine_fusion
  15.0 68.5 %shard_map.280 = (bf16[2048,2048]{1,0:T(8,128)(2,1)}, f32[2048,128]{1,0:T(8,128)}, f32[2048,128]{1,0:T(8,128)}, f32[2048,128]{1,0:T(8,128)}, bf16[2048,128]{1,0:...) custom-call(bf16[256,1024]{1,0:T(8,128)(2,1)} %refs_0_.2, ...), custom_call_target="tpu_custom_call" | custom-call | flops 3221225472 | bytes 33554432 | tf_op jit(solution)/shard_map/pallas_call | solution.py:1111
  83.5 1.1 dynamic-slice_reduce_fusion
  84.5 1.7 pad.8.refs_16_.refs_13_
  86.2 51.8 %shard_map.281 = (bf16[2048,128]{1,0:T(8,128)(2,1)}, f32[8,2048]{1,0:T(8,128)}, bf16[2048,2048]{1,0:T(8,128)(2,1)}, bf16[1,512,512]{2,1,0:T(8,128)(2,1)}, bf16[1...) custom-call(bf16[256,1024]{1,0:T(8,128)(2,1)} %refs_0_.3, ...), custom_call_target="tpu_custom_call" | custom-call | flops 2147483648 | bytes 33554432 | tf_op jit(solution)/shard_map/pallas_call | solution.py:1111
  138.0 64.1 %shard_map.282 = (f32[256,1024]{1,0:T(8,128)}, bf16[1,512,512]{2,1,0:T(8,128)(2,1)}, bf16[1,512,512]{2,1,0:T(8,128)(2,1)}, bf16[1,512,512]{2,1,0:T(8,128)(2,1)},...) custom-call(bf16[2048,128]{1,0:T(8,128)(2,1)} %get-tuple-element.75.refs_0_.refs_4_, ...), custom_call_target="tpu_custom_call" | custom-call | flops 1073741824 | bytes 33554432 | tf_op jit(solution)/shard_map/pallas_call | solution.py:1111
  202.1 2.2 multiply_reduce_fusion.5
  204.3 2.4 psum.28
  207.7 56.8 %shard_map.283 = (bf16[2048,1024]{1,0:T(8,128)(2,1)}, bf16[2048,1024]{1,0:T(8,128)(2,1)}, bf16[2048,1024]{1,0:T(8,128)(2,1)}, bf16[2048,128]{1,0:T(8,128)(2,1)}, bf16[2048,2048]{1,0:T(8,128)(2,1)}) custom-call(bf16[256,1024]{1,0:T(8,128)(2,1)} %multiply_convert_fusion.refs_0_, bf16[16,1024,512]{2,1,0:T(8,128)(2,1)} %refs_3_.3, ...), custom_call_target="tpu_custom_call" | custom-call | flops 25769803776 | bytes 33554432 | tf_op jit(solution)/shard_map/pallas_call | solution.py:1111
  264.5 74.1 %shard_map.284 = (f32[256,1024]{1,0:T(8,128)}, bf16[1024,1024]{1,0:T(8,128)(2,1)}, bf16[1,1024,1024]{2,1,0:T(8,128)(2,1)}, bf16[1024,128]{1,0:T(8,128)(2,1)}, bf16[1,1024,128]{2,1,0:T(8,128)(2,1)}) custom-call(bf16[2048,1024]{1,0:T(8,128)(2,1)} %get-tuple-element.95.refs_0_, bf16[2048,1024]{1,0:T(8,128)(2,1)} %get-tuple-element.96.refs_1_.refs_3_, ...), custom_call_target="tpu_custom_call" | custom-call | flops 25769803776 | bytes 33554432 | tf_op jit(solution)/shard_map/pallas_call | solution.py:1111
  338.7 2.3 multiply_reduce_fusion.2
  341.0 2.4 psum.29
  343.4 2.5 fusion.10
  346.0 90.8 %shard_map.285 = (bf16[2048,128]{1,0:T(8,128)(2,1)}, bf16[2048,2048]{1,0:T(8,128)(2,1)}, bf16[1024,1024]{1,0:T(8,128)(2,1)}, bf16[1,1024,1024]{2,1,0:T(8,128)(2,...) custom-call(bf16[256,1024]{1,0:T(8,128)(2,1)} %get-tuple-element.183, ...), custom_call_target="tpu_custom_call" | custom-call | flops 9663676416 | bytes 33554432 | tf_op jit(solution)/shard_map/pallas_call | solution.py:1111
  436.7 101.0 %shard_map.286 = (f32[256,1024]{1,0:T(8,128)}, bf16[2048,384]{1,0:T(8,128)(2,1)}, f32[2048,128]{1,0:T(8,128)}, f32[2048,128]{1,0:T(8,128)}, f32[2048,128]{1,0:T(...) custom-call(bf16[2048,1024]{1,0:T(8,128)(2,1)} %get-tuple-element.93, ...), custom_call_target="tpu_custom_call" | custom-call | flops 13958643712 | bytes 33554432 | tf_op jit(solution)/shard_map/pallas_call | solution.py:1111
  537.8 83.7 %shard_map.287 = (f32[256,1024]{1,0:T(8,128)}, bf16[8,128,512]{2,1,0:T(8,128)(2,1)}, bf16[8,128,512]{2,1,0:T(8,128)(2,1)}) custom-call(bf16[2048,384]{1,0:T(8,128)(2,1)} %get-tuple-element.115.refs_0_, bf16[2048,384]{1,0:T(8,128)(2,1)} %get-tuple-element.116.refs_1_, bf16[2048,2048]{1,0:T(8,128)(2,1)} %get-tuple-element.117.refs_2_, ...), custom_call_target="tpu_custom_call" | custom-call | flops 7516192768 | bytes 33554432 | tf_op jit(solution)/shard_map/pallas_call | solution.py:1111
  621.5 2.9 multiply_reduce_fusion
  624.4 2.0 maximum_bitcast_fusion
  626.4 1.6 fusion.5
  628.6 16.3 %shard_map.288 = f32[2,32,128]{2,1,0:T(8,128)} custom-call(f32[32,128]{1,0:T(8,128)} %select_maximum_fusion.src), custom_call_target="tpu_custom_call" | custom-call | tf_op jit(solution)/shard_map/pallas_call | solution.py:1196
  645.7 1.3 slice_bitcast_fusion
  648.1 3.8 all-reduce.2
  651.9 2.6 fusion.2
  655.1 1.4 convert_bitcast_fusion
  657.8 1.0 copy.56
  661.2 1.5 maximum_convert_fusion
  662.7 2.7 copy.53
  665.4 2.6 convert_element_type.71
  668.0 2.6 convert_element_type.70
  (35 shorter events, 12.7 us)
Async XLA Ops:
  138.0 64.1 %copy-start = (bf16[256,1024]{1,0:T(8,128)(2,1)S(1)}, bf16[256,1024]{1,0:T(8,128)(2,1)}, u32[]{:S(2)}) copy-start(bf16[256,1024]{1,0:T(8,128)(2,1)} %refs_0_.2) | copy-start | bytes 1572868
  621.5 6.5 copy-start.5
  621.5 26.5 %copy-start.4 = (bf16[8,128,128]{2,1,0:T(8,128)(2,1)S(1)}, bf16[8,128,128]{2,1,0:T(8,128)(2,1)}, u32[]{:S(2)}) copy-start(bf16[8,128,128]{2,1,0:T(8,128)(2,1)} %get-tuple-element.124) | copy-start | bytes 786436
  656.5 4.6 copy-start.3
  662.7 2.7 copy-start.2
  665.4 2.6 copy-start.1
